TPU v7x, 128 devices: a whole 4x4x4 slice. The times are simulated.
128 devices in a mesh: sph: 16 (over z, y_lo, core), wave: 8 (over y_hi, x).
Axes of the slice: x: 4, y: 4 (y_hi: 2, y_lo: 2; y = y_hi * 2 + y_lo), z: 4, core: 2. Of those that a mesh axis runs over, the one named last changes fastest.
Arguments:
- coefficients: float32 [8, 96, 2048], P(None, None, 'sph'), may hold values from -6 to 6
- incident: float32 [8, 96, 2048], P(None, None, 'sph'), may hold values from -6 to 6
- positions: float32 [3, 2048], P(None, 'sph'), may hold values from 0 to 1
- neighbour_index: int32 [12, 2048], P(None, 'sph'), may hold values from 0 to 2047, as said below
- link_class: int32 [12, 2048], P(None, 'sph'), may hold values from 0 to 25
- link_count: int32 [2048], P('sph'), may hold values from 1 to 12, as said below
- sphere_type: int32 [2048], P('sph'), may hold values from 0 to 3
- translation: float32 [2, 26, 48, 48], replicated, may hold values from -0.1875 to 0.1875
- t_matrix: float32 [2, 4, 48, 48], replicated, may hold values from -0.375 to 0.375
- wave_grid: int32 [2, 4096], P(None, 'wave'), may hold values from -64 to 63
- vertical: float32 [4096], P('wave'), may hold values from 0.5 to 4
- expansion: float32 [2, 2, 48, 4096], P(None, None, None, 'wave'), may hold values from -0.013671875 to 0.013671875
- reflection: float32 [2, 2, 2, 4096], P(None, None, None, 'wave'), may hold values from -3 to 3
- projector: float32 [2, 48, 2, 4096], P(None, None, None, 'wave'), may hold values from -0.03125 to 0.03125
Outputs:
- updated: float32 [8, 96, 2048], P(None, None, 'sph')
Inputs may be any that keep to these rules, and one draw needn't show every extreme that they name: `neighbour_index`: every entry lies within 128 of its own sphere's index; slots at or past link_count hold valid indices that are not used. `link_count`: the spheres of some aligned blocks of 128 have many more live slots than others.
All inputs are finite; a program needn't handle non-finite values.
Results may differ from a plain program's by a relative error of at most 0.0003.
Values sent between devices are 32-bit elements; how exact they have to be, the bound alone decides.
No kernel may reach another device: no remote copies, remote signals or barrier semaphores. Data moves between devices by JAX's collectives and lax.ppermute only.
A program may use at most 64 MiB of HBM per device.

v0:
```python
import jax
import jax.numpy as jnp
from jax import lax
from jax.sharding import PartitionSpec as P

MODES = 48
OFFSETS = 26
TYPES = 4


PRECISE = lax.Precision.HIGHEST
TWO_PI = 6.283185307179586


def with_halo(block, sides, width):
    for axis, dim in sides:
        count = lax.axis_size(axis)
        forward = [(i, i + 1) for i in range(count - 1)]
        backward = [(target, source) for source, target in forward]
        low = lax.ppermute(
            lax.slice_in_dim(block, block.shape[dim] - width, None, axis=dim), axis, forward
        )
        high = lax.ppermute(lax.slice_in_dim(block, 0, width, axis=dim), axis, backward)
        block = jnp.concatenate([low, block, high], axis=dim)
    return block


def realify(complex_pair):
    upper_half = jnp.concatenate([complex_pair[0], -complex_pair[1]], axis=-1)
    lower_half = jnp.concatenate([complex_pair[1], complex_pair[0]], axis=-1)
    return jnp.concatenate([upper_half, lower_half], axis=-2)


def contract(form, left, right):
    return jnp.einsum(form, left, right, precision=PRECISE)


def translate(source, index, link_class, link_count, translation):
    illums = source.shape[0]
    link_slots = index.shape[0]
    spheres = index.shape[1]
    picked = jnp.take(source, index.reshape(-1), axis=2).reshape(
        illums, 2 * MODES, link_slots, spheres
    )
    slot_ids = lax.broadcasted_iota(jnp.int32, index.shape, 0)
    live_links = (slot_ids < link_count[None, :]).astype(jnp.float32)
    class_ids = lax.broadcasted_iota(jnp.int32, (OFFSETS,) + index.shape, 0)
    weights = jnp.where(
        class_ids == link_class[None], live_links[None], jnp.zeros_like(live_links)[None]
    )
    binned = contract("bjks,cks->cjbs", picked, weights)
    operator_rows = jnp.transpose(realify(translation), (1, 0, 2)).reshape(
        2 * MODES, OFFSETS * 2 * MODES
    )
    translated = jnp.dot(
        operator_rows,
        binned.reshape(OFFSETS * 2 * MODES, illums * spheres),
        precision=PRECISE,
        preferred_element_type=jnp.float32,
    )
    return translated.reshape(2 * MODES, illums, spheres)


def angles(positions, wave_ids, vertical):
    across = wave_ids[0].astype(jnp.float32)
    along = wave_ids[1].astype(jnp.float32)
    plane_angle = TWO_PI * (
        positions[0][:, None] * across[None, :] + positions[1][:, None] * along[None, :]
    )
    height_angle = positions[2][:, None] * vertical[None, :]
    return (plane_angle, height_angle)


def expand(coefficients, positions, wave_ids, vertical, expansion):
    illums = coefficients.shape[0]
    waves = wave_ids.shape[1]
    plane_angle, height_angle = angles(positions, wave_ids, vertical)
    down_angle = plane_angle - height_angle
    phase_tiles = jnp.concatenate([jnp.cos(down_angle), jnp.sin(down_angle)], axis=1)
    products = jnp.dot(
        coefficients.reshape(illums * 2 * MODES, -1),
        phase_tiles,
        precision=PRECISE,
        preferred_element_type=jnp.float32,
    )
    products = products.reshape(illums, 2, MODES, 2, waves)
    spec_real = products[:, 0, :, 0] + products[:, 1, :, 1]
    spec_imag = products[:, 1, :, 0] - products[:, 0, :, 1]
    out_real = contract("plw,blw->bpw", expansion[0], spec_real) - contract(
        "plw,blw->bpw", expansion[1], spec_imag
    )
    out_imag = contract("plw,blw->bpw", expansion[0], spec_imag) + contract(
        "plw,blw->bpw", expansion[1], spec_real
    )
    return jnp.stack([out_real, out_imag], axis=1)


def reflect(spectrum, reflection):
    spec_real = spectrum[:, 0]
    spec_imag = spectrum[:, 1]
    out_real = contract("pqw,bqw->bpw", reflection[0], spec_real) - contract(
        "pqw,bqw->bpw", reflection[1], spec_imag
    )
    out_imag = contract("pqw,bqw->bpw", reflection[0], spec_imag) + contract(
        "pqw,bqw->bpw", reflection[1], spec_real
    )
    return jnp.stack([out_real, out_imag], axis=1)


def wave_field(reflected, projector):
    spec_real = reflected[:, 0]
    spec_imag = reflected[:, 1]
    field_real = contract("lpw,bpw->blw", projector[0], spec_real) - contract(
        "lpw,bpw->blw", projector[1], spec_imag
    )
    field_imag = contract("lpw,bpw->blw", projector[0], spec_imag) + contract(
        "lpw,bpw->blw", projector[1], spec_real
    )
    return jnp.stack([field_real, field_imag], axis=1)


def up_tiles(positions, wave_ids, vertical):
    plane_angle, height_angle = angles(positions, wave_ids, vertical)
    up_angle = plane_angle + height_angle
    return jnp.concatenate([jnp.cos(up_angle), jnp.sin(up_angle)], axis=0)


def project(spectral_field, phase_tiles):
    illums = spectral_field.shape[0]
    spheres = phase_tiles.shape[0] // 2
    products = lax.dot_general(
        spectral_field.reshape(illums * 2 * MODES, -1),
        phase_tiles,
        (((1,), (1,)), ((), ())),
        precision=PRECISE,
        preferred_element_type=jnp.float32,
    )
    products = products.reshape(illums, 2, MODES, 2, spheres)
    resp_real = products[:, 0, :, 0] - products[:, 1, :, 1]
    resp_imag = products[:, 0, :, 1] + products[:, 1, :, 0]
    return jnp.stack([resp_real, resp_imag], axis=1).reshape(illums, 2 * MODES, spheres)


def apply_types(exciting, sphere_type, t_matrix):
    operator_rows = realify(t_matrix).reshape(TYPES * 2 * MODES, 2 * MODES)
    all_types = jnp.dot(
        operator_rows,
        exciting.reshape(2 * MODES, -1),
        precision=PRECISE,
        preferred_element_type=jnp.float32,
    )
    all_types = all_types.reshape(TYPES, 2 * MODES, exciting.shape[1], exciting.shape[2])
    type_ids = lax.broadcasted_iota(jnp.int32, (TYPES, exciting.shape[2]), 0)
    type_weights = (type_ids == sphere_type[None, :]).astype(jnp.float32)
    return jnp.sum(all_types * type_weights[:, None, None, :], axis=0)


def per_device(
    coefficients,
    incident,
    positions,
    neighbour_index,
    link_class,
    link_count,
    sphere_type,
    translation,
    t_matrix,
    wave_grid,
    vertical,
    expansion,
    reflection,
    projector,
):
    block_size = coefficients.shape[2]
    illums = coefficients.shape[0]
    local_index = neighbour_index - (lax.axis_index("sph") - 1) * block_size
    partial_value = expand(coefficients, positions, wave_grid, vertical, expansion)
    spectrum = lax.psum(partial_value, "sph")
    reflected = reflect(spectrum, reflection)
    spectral_field = wave_field(reflected, projector)
    phase_tiles = up_tiles(positions, wave_grid, vertical)
    own_count = illums // lax.axis_size("wave")
    first_illum = lax.axis_index("wave") * own_count
    own_coefs = lax.dynamic_slice_in_dim(coefficients, first_illum, own_count, 0)
    own_incident = lax.dynamic_slice_in_dim(incident, first_illum, own_count, 0)
    extended = with_halo(own_coefs, (("sph", 2),), block_size)
    translated = translate(extended, local_index, link_class, link_count, translation)
    response = lax.psum_scatter(
        project(spectral_field, phase_tiles), "wave", scatter_dimension=0, tiled=True
    )
    exciting = jnp.transpose(own_incident + response, (1, 0, 2)) + translated
    own_updated = jnp.transpose(apply_types(exciting, sphere_type, t_matrix), (1, 0, 2))
    updated = lax.all_gather(own_updated, "wave", axis=0, tiled=True)
    return updated


def solution(mesh):
    placed = (
        P(None, None, "sph"),
        P(None, None, "sph"),
        P(None, "sph"),
        P(None, "sph"),
        P(None, "sph"),
        P("sph"),
        P("sph"),
        P(),
        P(),
        P(None, "wave"),
        P("wave"),
        P(None, None, None, "wave"),
        P(None, None, None, "wave"),
        P(None, None, None, "wave"),
    )
    return jax.shard_map(
        per_device, mesh=mesh, in_specs=placed, out_specs=P(None, None, "sph"), check_vma=False
    )
```

profile of v0, /device:TPU:0, one launch (start us, length us, event | category | flops | bytes accessed | tf_op | source)
XLA Modules:
  0.0 346.7 jit_solution(15848195496139171093)
XLA Ops:
  8.3 1.9 collective-permute-start
  13.0 3.7 %fusion.53 = (f32[128,512]{1,0:T(8,128)S(1)}, f32[128,512]{1,0:T(8,128)}, f32[128,512]{1,0:T(8,128)S(1)}, f32[128,512]{1,0:T(8,128)}) fusion(f32[512]{0:T(512)} %param.24, f32[128]{0:T(128)S(1)} %get-tuple-element.24, f32[512]{0:T(512)S(1)} %bitcast.165, f32[128]{0:T(128)S(1)} %get-tuple-element.25, f32[512]{0:T(512)S(1)} %bitcast.164, ...), kind=kLoop, calls=%fused_computation.70 | loop fusion | flops 458752 | bytes 1056256 | tf_op jit(solution)/shard_map/cos | solution.py:79
  16.7 2.7 convolution_bitcast_fusion
  19.4 2.3 copy.78
  21.7 4.2 %reshape.170 = f32[8,2,48,2,512]{4,3,2,1,0:T(2,128)S(1)} reshape(f32[768,1024]{1,0:T(8,128)} %copy.78) | data formatting | bytes 6291456 | tf_op jit(solution)/shard_map/reshape | solution.py:86
  25.9 2.6 slice_add_fusion
  28.5 4.0 %copy.103 = f32[8,1,48,1,512]{2,0,4,3,1:T(8,128)} copy(f32[8,1,48,1,512]{4,3,2,1,0:T(1,128)} %get-tuple-element.6) | data formatting | bytes 1572864 | tf_op jit(solution)/shard_map/sub | solution.py:88
  33.4 2.8 copy.102
  37.5 5.3 %fusion.2 = f32[512,8,2]{1,2,0:T(2,128)S(1)} fusion(f32[8,1,48,1,512]{2,0,4,3,1:T(8,128)} %copy.103, f32[1,2,48,512]{2,1,3,0:T(2,128)S(1)} %copy.105), kind=kOutput, calls=%fused_computation.3 | convolution fusion | flops 4718592 | bytes 1015808 | tf_op jit(solution)/shard_map/plw,blw->bpw/dot_general | solution.py:35
  42.8 3.6 %fusion = f32[512,8,2]{1,2,0:T(2,128)S(1)} fusion(f32[8,1,48,1,512]{2,0,4,3,1:T(8,128)S(1)} %copy-done.1, f32[1,2,48,512]{2,1,3,0:T(2,128)S(1)} %copy.104), kind=kOutput, calls=%fused_computation.1 | convolution fusion | flops 4718592 | bytes 1015808 | tf_op jit(solution)/shard_map/plw,blw->bpw/dot_general | solution.py:35
  46.3 3.6 %fusion.16 = f32[8,1,2,512]{0,2,3,1:T(2,128)S(1)} fusion(f32[512,8,2]{1,2,0:T(2,128)S(1)} %fusion.2, f32[8,1,48,1,512]{2,0,4,3,1:T(8,128)S(1)} %copy.102, f32[1,2,48,512]{2,1,3,0:T(2,128)S(1)} %copy.104), kind=kOutput, calls=%fused_computation.23 | convolution fusion | flops 4726784 | bytes 1048576 | tf_op jit(solution)/shard_map/plw,blw->bpw/dot_general | solution.py:35
  49.9 4.1 %fusion.22 = f32[8,1,2,512]{0,2,3,1:T(2,128)S(1)} fusion(f32[512,8,2]{1,2,0:T(2,128)S(1)} %fusion, f32[8,1,48,1,512]{2,0,4,3,1:T(8,128)S(1)} %copy.102, f32[1,2,48,512]{2,1,3,0:T(2,128)S(1)} %copy.105), kind=kOutput, calls=%fused_computation.25 | convolution fusion | flops 4726784 | bytes 1048576 | tf_op jit(solution)/shard_map/plw,blw->bpw/dot_general | solution.py:35
  54.1 1.5 pad_maximum_fusion
  62.5 1.5 fusion.74
  67.0 115.3 %all-reduce.2.cloned.1.call-done = f32[8,2,2,512]{0,2,3,1:T(2,128)} async-done(((f32[8,2,2,512]{0,2,3,1:T(2,128)}), f32[8,2,2,512]{0,2,3,1:T(2,128)}) %all-reduce.2.cloned.1.call-update) | async-done | bytes 65552 | tf_op jit(solution)/shard_map/psum | solution.py:178
  182.3 4.8 %fusion.41 = f32[512,8,2]{1,2,0:T(2,128)S(1)} fusion(f32[1,2,2,512]{2,1,3,0:T(2,128)} %copy.106, f32[8,2,2,512]{0,2,3,1:T(2,128)} %all-reduce.2.cloned.1.call-done), kind=kOutput, calls=%fused_computation.54 | convolution fusion | flops 196608 | bytes 1081344 | tf_op jit(solution)/shard_map/pqw,bqw->bpw/dot_general | solution.py:35
  187.1 4.6 %fusion.12 = f32[8,2,512]{0,1,2:T(2,128)S(1)} fusion(f32[512,8,2]{1,2,0:T(2,128)S(1)} %fusion.41, f32[1,2,2,512]{2,1,3,0:T(2,128)S(1)} %copy-done.13, f32[8,2,2,512]{0,2,3,1:T(2,128)} %all-reduce.2.cloned.1.call-done), kind=kOutput, calls=%fused_computation.21 | convolution fusion | flops 204800 | bytes 598016 | tf_op jit(solution)/shard_map/pqw,bqw->bpw/dot_general | solution.py:35
  191.8 4.6 %fusion.35 = f32[512,8,48]{2,1,0:T(8,128)S(1)} fusion(f32[8,2,512]{0,1,2:T(2,128)S(1)} %fusion.12, f32[1,48,2,512]{1,2,3,0:T(2,128)S(1)} %copy.108), kind=kOutput, calls=%fused_computation.48 | convolution fusion | flops 4718592 | bytes 1015808 | tf_op jit(solution)/shard_map/lpw,bpw->blw/dot_general | solution.py:35
  196.4 3.6 %fusion.39 = f32[512,8,2]{1,2,0:T(2,128)S(1)} fusion(f32[1,2,2,512]{2,1,3,0:T(2,128)S(1)} %copy-done.12, f32[8,2,2,512]{0,2,3,1:T(2,128)S(1)} %copy-done.24), kind=kOutput, calls=%fused_computation.52 | convolution fusion | flops 196608 | bytes 1081344 | tf_op jit(solution)/shard_map/pqw,bqw->bpw/dot_general | solution.py:35
  200.0 3.6 %fusion.11 = f32[8,2,512]{0,1,2:T(2,128)S(1)} fusion(f32[512,8,2]{1,2,0:T(2,128)S(1)} %fusion.39, f32[1,2,2,512]{2,1,3,0:T(2,128)S(1)} %copy-done.13, f32[8,2,2,512]{0,2,3,1:T(2,128)S(1)} %copy-done.24), kind=kOutput, calls=%fused_computation.19 | convolution fusion | flops 204800 | bytes 1605632 | tf_op jit(solution)/shard_map/pqw,bqw->bpw/dot_general | solution.py:35
  203.7 4.5 %fusion.33 = f32[512,8,48]{2,1,0:T(8,128)S(1)} fusion(f32[8,2,512]{0,1,2:T(2,128)S(1)} %fusion.11, f32[1,48,2,512]{1,2,3,0:T(2,128)S(1)} %copy.108), kind=kOutput, calls=%fused_computation.46 | convolution fusion | flops 4718592 | bytes 1015808 | tf_op jit(solution)/shard_map/lpw,bpw->blw/dot_general | solution.py:35
  208.2 5.6 %subtract_bitcast_fusion = f32[8,1,48,512]{2,0,3,1:T(8,128)} fusion(f32[512,8,48]{2,1,0:T(8,128)S(1)} %fusion.35, f32[8,2,512]{0,1,2:T(2,128)S(1)} %fusion.11, f32[1,48,2,512]{1,2,3,0:T(2,128)S(1)} %copy.109), kind=kOutput, calls=%fused_computation.10 | convolution fusion | flops 4915200 | bytes 1802240 | tf_op jit(solution)/shard_map/lpw,bpw->blw/dot_general | solution.py:35
  213.8 3.1 copy.89
  216.9 5.6 %add_bitcast_fusion = f32[8,1,48,512]{2,0,3,1:T(8,128)} fusion(f32[512,8,48]{2,1,0:T(8,128)S(1)} %fusion.33, f32[8,2,512]{0,1,2:T(2,128)S(1)} %copy-done.8, f32[1,48,2,512]{1,2,3,0:T(2,128)S(1)} %copy.109), kind=kOutput, calls=%fused_computation.9 | convolution fusion | flops 4915200 | bytes 1802240 | tf_op jit(solution)/shard_map/lpw,bpw->blw/dot_general | solution.py:35
  222.5 2.3 copy.90
  224.8 1.7 fusion.8
  230.8 2.6 gather_fusion
  233.4 4.3 %convolution_bitcast_fusion.1 = f32[26,96,1,128]{1,0,3,2:T(8,128)S(1)} fusion(f32[96,12,128]{0,2,1:T(8,128)S(1)} %bitcast.160, f32[12,128]{0,1:T(8,128)S(1)} %copy-done.17, s32[12,128]{0,1:T(8,128)S(1)} %copy.95, pred[12,128]{0,1:T(8,128)(4,1)S(1)} %copy.96), kind=kOutput, calls=%fused_computation.12 | convolution fusion | flops 46233600 | bytes 1881600 | tf_op jit(solution)/shard_map/bjks,cks->cjbs/dot_general | solution.py:35
  237.7 1.8 copy.99
  239.5 60.3 %reduce-scatter.2.cloned.1.call-done = f32[1,96,128]{2,1,0:T(8,128)} async-done(((f32[8,96,128]{2,1,0:T(8,128)}), f32[1,96,128]{2,1,0:T(8,128)}) %reduce-scatter.2.cloned.1.call-update) | async-done | bytes 49168 | tf_op jit(solution)/shard_map/reduce_scatter | solution.py:188
  299.8 3.9 %fusion.26 = f32[96,128,1]{1,0,2:T(8,128)S(1)} fusion(f32[96,2496]{0,1:T(8,128)} %bitcast.159, f32[2496,128]{1,0:T(8,128)} %bitcast.158, f32[1,96,128]{2,1,0:T(8,128)} %reduce-scatter.2.cloned.1.call-done, f32[8,96,128]{2,1,0:T(8,128)} %param.15, s32[]{:T(128)S(6)} %select_n.33), kind=kOutput, calls=%fused_computation.29 | convolution fusion | flops 368074752 | bytes 2383876 | tf_op jit(solution)/shard_map/dot_general | solution.py:55
  304.1 34.6 %all-gather = f32[768,128]{1,0:T(8,128)S(1)} all-gather(f32[96,128]{1,0:T(8,128)S(1)} %fusion.25), channel_id=2, replica_groups=mesh['sph'=16,'wave'=8] {'wave'}, dimensions={0}, use_global_device_ids=true | all-gather | bytes 442368 | tf_op jit(solution)/shard_map/all_gather | solution.py:193
  (91 shorter events, 21.9 us)
Async XLA Ops:
  6.5 1.0 copy-start
  6.5 175.8 %all-reduce.2.cloned.1.call-start = ((), (), s32[]{:S(2)}) async-start(), calls=%async_computation.1 | async-start | bytes 2097152 | tf_op jit(solution)/shard_map/psum | solution.py:178
  8.3 221.6 %collective-permute-start = (f32[1,96,128]{1,2,0:T(8,128)}, f32[1,96,128]{1,2,0:T(8,128)}, u32[]{:S(2)}, u32[]{:S(2)}) collective-permute-start(f32[1,96,128]{1,2,0:T(8,128)} %copy.112), channel_id=1, source_target_pairs={{0,8},{8,16},{16,24},{24,32},{32,40},{40,48},{48,56},{56,64},{64,7... | collective-permute-start | bytes 147464 | tf_op jit(solution)/shard_map/ppermute | solution.py:20
  10.2 219.7 %collective-permute-start.1 = (f32[1,96,128]{1,2,0:T(8,128)}, f32[1,96,128]{1,2,0:T(8,128)}, u32[]{:S(2)}, u32[]{:S(2)}) collective-permute-start(f32[1,96,128]{1,2,0:T(8,128)} %copy.112), channel_id=1, source_target_pairs={{8,0},{16,8},{24,16},{32,24},{40,32},{48,40},{56,48},{64,56},{72,6... | collective-permute-start | bytes 147464 | tf_op jit(solution)/shard_map/ppermute | solution.py:23
  28.5 4.0 %copy-start.15 = (f32[2,2,48,512]{3,2,1,0:T(8,128)S(1)}, f32[2,2,48,512]{3,2,1,0:T(8,128)}, u32[]{:S(2)}) copy-start(f32[2,2,48,512]{3,2,1,0:T(8,128)} %param.25) | copy-start | bytes 1179652
  37.5 5.3 %copy-start.1 = (f32[8,1,48,1,512]{2,0,4,3,1:T(8,128)S(1)}, f32[8,1,48,1,512]{2,0,4,3,1:T(8,128)}, u32[]{:S(2)}) copy-start(f32[8,1,48,1,512]{2,0,4,3,1:T(8,128)} %copy.103) | copy-start | bytes 2359300
  54.0 1.6 copy-start.20
  54.0 1.7 copy-start.4
  55.6 1.9 copy-start.21
  55.6 244.2 %reduce-scatter.2.cloned.1.call-start = ((), (), s32[]{:S(2)}) async-start(), calls=%async_computation.2 | async-start | bytes 442368 | tf_op jit(solution)/shard_map/reduce_scatter | solution.py:188
  55.7 3.9 %copy-start.16 = (f32[2,48,2,512]{3,2,1,0:T(2,128)S(1)}, f32[2,48,2,512]{3,2,1,0:T(2,128)}, u32[]{:S(2)}) copy-start(f32[2,48,2,512]{3,2,1,0:T(2,128)} %param.27) | copy-start | bytes 1179652
  56.6 5.1 %copy-start.23 = (s32[128]{0:T(128)S(1)}, s32[128]{0:T(128)}, u32[]{:S(2)}) copy-start(s32[128]{0:T(128)} %param.19) | copy-start | bytes 1540
  57.5 7.2 %copy-start.5 = (f32[26,48,48]{2,1,0:T(8,128)S(1)}, f32[26,48,48]{2,1,0:T(8,128)}, u32[]{:S(2)}) copy-start(f32[26,48,48]{2,1,0:T(8,128)} %get-tuple-element.8) | copy-start | bytes 718852
  57.5 7.2 %copy-start.6 = (f32[26,48,48]{2,1,0:T(8,128)S(1)}, f32[26,48,48]{2,1,0:T(8,128)}, u32[]{:S(2)}) copy-start(f32[26,48,48]{2,1,0:T(8,128)} %fusion.75) | copy-start | bytes 718852
  61.8 4.4 %copy-start.10 = (f32[128,512]{1,0:T(8,128)S(1)}, f32[128,512]{1,0:T(8,128)}, u32[]{:S(2)}) copy-start(f32[128,512]{1,0:T(8,128)} %get-tuple-element.18) | copy-start | bytes 786436
  61.8 4.4 %copy-start.11 = (f32[128,512]{1,0:T(8,128)S(1)}, f32[128,512]{1,0:T(8,128)}, u32[]{:S(2)}) copy-start(f32[128,512]{1,0:T(8,128)} %get-tuple-element.20) | copy-start | bytes 786436
  66.2 120.9 %copy-start.13 = (f32[1,2,2,512]{2,1,3,0:T(2,128)S(1)}, f32[1,2,2,512]{2,1,3,0:T(2,128)}, u32[]{:S(2)}) copy-start(f32[1,2,2,512]{2,1,3,0:T(2,128)} %copy.107) | copy-start | bytes 24580
  191.8 8.2 %copy-start.7 = (f32[8,2,512]{0,1,2:T(2,128)}, f32[8,2,512]{0,1,2:T(2,128)S(1)}, u32[]{:S(2)}) copy-start(f32[8,2,512]{0,1,2:T(2,128)S(1)} %fusion.12) | copy-start | bytes 98308
  191.8 4.6 %copy-start.12 = (f32[1,2,2,512]{2,1,3,0:T(2,128)S(1)}, f32[1,2,2,512]{2,1,3,0:T(2,128)}, u32[]{:S(2)}) copy-start(f32[1,2,2,512]{2,1,3,0:T(2,128)} %copy.106) | copy-start | bytes 24580
  191.8 4.6 %copy-start.24 = (f32[8,2,2,512]{0,2,3,1:T(2,128)S(1)}, f32[8,2,2,512]{0,2,3,1:T(2,128)}, u32[]{:S(2)}) copy-start(f32[8,2,2,512]{0,2,3,1:T(2,128)} %all-reduce.2.cloned.1.call-done) | copy-start | bytes 196612
  213.8 3.1 copy-start.8
  222.5 2.3 copy-start.3
  222.5 2.3 copy-start.9
  226.6 1.0 copy-start.14
  226.6 1.8 copy-start.22
  226.6 1.9 copy-start.2
  230.8 2.6 copy-start.17
  239.5 64.2 %copy-start.18 = (f32[4,48,48]{2,1,0:T(8,128)S(1)}, f32[4,48,48]{2,1,0:T(8,128)}, u32[]{:S(2)}) copy-start(f32[4,48,48]{2,1,0:T(8,128)} %fusion.74) | copy-start | bytes 110596
  239.5 64.2 %copy-start.19 = (f32[4,48,48]{2,1,0:T(8,128)S(1)}, f32[4,48,48]{2,1,0:T(8,128)}, u32[]{:S(2)}) copy-start(f32[4,48,48]{2,1,0:T(8,128)} %get-tuple-element.14) | copy-start | bytes 110596
Sparse Core Ops, SparseCore 0:
  55.7 126.5 all-reduce.1
  227.6 72.1 reduce-scatter.1
where the time goes:
time: 352 us; the launch traced here: 347 us
  waiting for transfers between devices  176 us (50%)
  matrix products  66.5 us (19%)
  local copies, waits for them, and re-layouts  36.8 us (10%)
  blocking collectives  34.6 us (10%)
  other arithmetic  15.7 us (4%)
  between operations  14.3 us (4%)
    psum x1, waiting for transfers between devices, per_device(): spectrum = lax.psum(partial_value, 'sph')  115 us
    reduce_scatter x1, waiting for transfers between devices, per_device(): lax.psum_scatter(project(spectral_field, phase_tiles), 'wave', scatter_di...  60.3 us
    dot_general x13, matrix products, contract(): return jnp.einsum(form, left, right, precision=PRECISE)  57.8 us
    all_gather x1, blocking collectives, per_device(): updated = lax.all_gather(own_updated, 'wave', axis=0, tiled=True)  34.6 us
    unnamed x59, local copies, waits for them, and re-layouts  7.55 us
  transfers between devices with their start and end apart: 4, of which 2 were waited for; matrix products, arithmetic and copies ran while one was open for 32% of the time, Pallas kernels for 0%

commit v1 on v0

v1 whole, which is shorter than its diff:
```python
import jax
import jax.numpy as jnp
from jax import lax
from jax.experimental import pallas as pl
from jax.experimental.pallas import tpu as pltpu
from jax.sharding import PartitionSpec as P

MODES = 48
OFFSETS = 26
TYPES = 4
LINKS = 12
INV_TWO_PI = 0.15915494309189535

SIN_POLY = (3.14159264, -5.16771008, 2.55007752, -0.59829129, 0.07765766)
COS_POLY = (1.0, -4.93480214, 4.05870916, -1.335212, 0.23493731, -0.02439632)

VMEM = pl.BlockSpec(memory_space=pltpu.VMEM)
SMEM = pl.BlockSpec(memory_space=pltpu.SMEM)
BF16 = jnp.bfloat16
F32 = jnp.float32


def horner(coefs, t):
    acc = coefs[-1] * t + coefs[-2]
    for value in coefs[-3::-1]:
        acc = acc * t + value
    return acc


def cos_sin_turns(turns):
    rest = turns - jnp.round(turns)
    t = rest * rest
    s = rest * horner(SIN_POLY, t)
    c = horner(COS_POLY, t)
    return 1.0 - 2.0 * (s * s), 2.0 * (s * c)


def split(x):
    hi = x.astype(BF16)
    return hi, (x - hi.astype(F32)).astype(BF16)


def dot3(ah, al, bh, bl):
    def dot(a, b):
        return jnp.dot(a, b, preferred_element_type=F32)

    return dot(ah, bh) + (dot(ah, bl) + dot(al, bh))


def columns(rows):
    pad = jnp.zeros((8 - rows.shape[0], rows.shape[1]), F32)
    return jnp.concatenate([rows, pad], axis=0).T


def expand_kernel(flip_ref, coef_ref, pos_ref, grid_ref, vert_ref, exp_ref, out_ref, ah, al, spec):
    illums = coef_ref.shape[0]
    waves = grid_ref.shape[1]
    half = illums * MODES
    for b in range(illums):
        block = coef_ref[jnp.bitwise_xor(flip_ref[0], b)]
        re, im = block[:MODES], block[MODES:]
        for base, left, right in ((0, re, im), (half, im, -re)):
            rows = pl.ds(base + b * MODES, MODES)
            for offset, part in ((0, left), (128, right)):
                hi, lo = split(part)
                ah[rows, offset : offset + 128] = hi
                al[rows, offset : offset + 128] = lo
    pos = columns(pos_ref[...])
    grid = grid_ref[...].astype(F32)
    vert = vert_ref[...].reshape(1, waves) * INV_TWO_PI
    width = 256
    for start in range(0, waves, width):
        lanes = slice(start, start + width)
        turns = pos[:, 0:1] * grid[0:1, lanes] + pos[:, 1:2] * grid[1:2, lanes]
        turns = turns - pos[:, 2:3] * vert[:, lanes]
        cos, sin = cos_sin_turns(turns)
        bh, bl = split(jnp.concatenate([cos, sin], axis=0))
        spec[...] = dot3(ah[...], al[...], bh, bl)
        for p in range(2):
            er, ei = exp_ref[0, p, :, lanes], exp_ref[1, p, :, lanes]
            out_re, out_im = [], []
            for b in range(illums):
                sr = spec[b * MODES : (b + 1) * MODES, :]
                si = spec[half + b * MODES : half + (b + 1) * MODES, :]
                out_re.append(jnp.sum(er * sr - ei * si, axis=0, keepdims=True))
                out_im.append(jnp.sum(er * si + ei * sr, axis=0, keepdims=True))
            out_ref[2 * p, :, lanes] = jnp.concatenate(out_re, axis=0)
            out_ref[2 * p + 1, :, lanes] = jnp.concatenate(out_im, axis=0)


def expand(flip, coefficients, positions, wave_grid, vertical, expansion):
    illums, _, spheres = coefficients.shape
    waves = wave_grid.shape[1]
    rows = illums * 2 * MODES
    return pl.pallas_call(
        expand_kernel,
        name="expand",
        out_shape=jax.ShapeDtypeStruct((4, illums, waves), F32),
        in_specs=[SMEM] + [VMEM] * 5,
        out_specs=VMEM,
        scratch_shapes=[
            pltpu.VMEM((rows, 2 * spheres), BF16),
            pltpu.VMEM((rows, 2 * spheres), BF16),
            pltpu.VMEM((rows, 256), F32),
        ],
        cost_estimate=pl.CostEstimate(
            flops=6 * rows * 2 * spheres * waves, bytes_accessed=4 << 20, transcendentals=0
        ),
    )(flip, coefficients, positions, wave_grid, vertical, expansion)


def prepare_kernel(pos_ref, grid_ref, vert_ref, refl_ref, proj_ref, uh, ul, qr_ref):
    waves = grid_ref.shape[1]
    spheres = pos_ref.shape[1]
    grid = grid_ref[...].astype(F32)
    vert = vert_ref[...].reshape(1, waves) * INV_TWO_PI
    cols = columns(jnp.concatenate([grid, vert], axis=0))
    turns = cols[:, 0:1] * pos_ref[0:1, :] + cols[:, 1:2] * pos_ref[1:2, :]
    turns = turns + cols[:, 2:3] * pos_ref[2:3, :]
    cos, sin = cos_sin_turns(turns)
    ch, cl = split(cos)
    sh, sl = split(sin)
    for ref, c, s in ((uh, ch, sh), (ul, cl, sl)):
        ref[:waves, :spheres] = c
        ref[:waves, spheres:] = s
        ref[waves:, :spheres] = -s
        ref[waves:, spheres:] = c
    for q in range(2):
        acc_re = acc_im = None
        for p in range(2):
            pr, pi = proj_ref[0, :, p, :], proj_ref[1, :, p, :]
            rr = refl_ref[0, p, q : q + 1, :]
            ri = refl_ref[1, p, q : q + 1, :]
            term_re = pr * rr - pi * ri
            term_im = pr * ri + pi * rr
            acc_re = term_re if acc_re is None else acc_re + term_re
            acc_im = term_im if acc_im is None else acc_im + term_im
        qr_ref[2 * q] = acc_re
        qr_ref[2 * q + 1] = acc_im


def prepare(positions, wave_grid, vertical, reflection, projector):
    waves = wave_grid.shape[1]
    spheres = positions.shape[1]
    tiles = jax.ShapeDtypeStruct((2 * waves, 2 * spheres), BF16)
    return pl.pallas_call(
        prepare_kernel,
        name="prepare",
        out_shape=(tiles, tiles, jax.ShapeDtypeStruct((4, MODES, waves), F32)),
        in_specs=[VMEM] * 5,
        out_specs=(VMEM,) * 3,
        cost_estimate=pl.CostEstimate(
            flops=2 << 20, bytes_accessed=2 << 20, transcendentals=0
        ),
    )(positions, wave_grid, vertical, reflection, projector)


def project_kernel(mine_ref, other_ref, qr_ref, uh, ul, *refs):
    outs, (fh, fl) = refs[:-2], refs[-2:]
    illums = mine_ref.shape[1]
    waves = mine_ref.shape[2]
    width = 128
    for start in range(0, waves, width):
        lanes = slice(start, start + width)
        spec = [mine_ref[i, :, lanes] + other_ref[i, :, lanes] for i in range(4)]
        qr = [qr_ref[i, :, lanes] for i in range(4)]
        for b in range(illums):
            rows = slice(b * MODES, (b + 1) * MODES)
            x = [part[b : b + 1, :] for part in spec]
            fr = (qr[0] * x[0] - qr[1] * x[1]) + (qr[2] * x[2] - qr[3] * x[3])
            fi = (qr[0] * x[1] + qr[1] * x[0]) + (qr[2] * x[3] + qr[3] * x[2])
            for base, part in ((0, fr), (waves, fi)):
                hi, lo = split(part)
                fh[rows, base + start : base + start + width] = hi
                fl[rows, base + start : base + start + width] = lo
    out = dot3(fh[...], fl[...], uh[...], ul[...])
    per_piece = illums // len(outs)
    for b in range(illums):
        ref = outs[b // per_piece]
        rows = out[b * MODES : (b + 1) * MODES]
        ref[b % per_piece, :MODES, :] = rows[:, :128]
        ref[b % per_piece, MODES:, :] = rows[:, 128:]


def project(mine, other, qr, uh, ul, pieces):
    illums, waves = mine.shape[1:]
    spheres = uh.shape[1] // 2
    piece = jax.ShapeDtypeStruct((illums // pieces, 2 * MODES, spheres), F32)
    return pl.pallas_call(
        project_kernel,
        name="project",
        out_shape=(piece,) * pieces,
        in_specs=[VMEM] * 5,
        out_specs=(VMEM,) * pieces,
        scratch_shapes=[pltpu.VMEM((illums * MODES, 2 * waves), BF16)] * 2,
        cost_estimate=pl.CostEstimate(
            flops=6 * illums * MODES * 2 * waves * 2 * spheres,
            bytes_accessed=3 << 20,
            transcendentals=0,
        ),
    )(mine, other, qr, uh, ul)


def translate_kernel(
    where_ref, low_ref, own_ref, high_ref, inc_ref, idx_ref, class_ref, count_ref, trans_ref, out_ref, bh, bl, gh, gl
):
    own = where_ref[0]
    slot = where_ref[1]
    base = where_ref[2]
    spheres = own_ref.shape[2]
    local = idx_ref[...] - base
    side = jnp.right_shift(local, 7)
    lane = jnp.bitwise_and(local, 127)
    live = lax.broadcasted_iota(jnp.int32, local.shape, 0) < count_ref[...].reshape(1, spheres)
    kind = jnp.where(live, class_ref[...], OFFSETS)
    source = (low_ref[0], own_ref[own], high_ref[0])
    shape = (2 * MODES, spheres)
    picked = []
    for k in range(LINKS):
        at = jnp.broadcast_to(lane[k : k + 1, :], shape)
        got = [jnp.take_along_axis(x, at, axis=1) for x in source]
        pick = jnp.where(side[k : k + 1, :] == 0, got[0], got[2])
        picked.append(jnp.where(side[k : k + 1, :] == 1, got[1], pick))
    for c in range(OFFSETS):
        total = None
        for k in range(LINKS):
            term = jnp.where(kind[k : k + 1, :] == c, picked[k], 0.0)
            total = term if total is None else total + term
        hi, lo = split(total)
        rows = slice(c * MODES, (c + 1) * MODES)
        for ref, part in ((bh, hi), (bl, lo)):
            ref[rows, :spheres] = part[:MODES]
            ref[rows, spheres:] = part[MODES:]
        hi, lo = split(jnp.concatenate([trans_ref[0, c], trans_ref[1, c]], axis=0))
        gh[:, rows] = hi
        gl[:, rows] = lo
    both = dot3(gh[...], gl[...], bh[...], bl[...])
    upper, lower = both[:MODES], both[MODES:]
    result = jnp.concatenate(
        [upper[:, :spheres] - lower[:, spheres:], upper[:, spheres:] + lower[:, :spheres]], axis=0
    )
    result = result + inc_ref[own]
    out_ref[0] = jnp.where(slot == 0, result, 0.0)
    out_ref[1] = jnp.where(slot == 0, 0.0, result)


def translate(where, low, coefficients, high, incident, index, link_class, link_count, translation):
    spheres = index.shape[1]
    return pl.pallas_call(
        translate_kernel,
        name="translate",
        out_shape=jax.ShapeDtypeStruct((2, 2 * MODES, spheres), F32),
        in_specs=[SMEM] + [VMEM] * 8,
        out_specs=VMEM,
        scratch_shapes=[
            pltpu.VMEM((OFFSETS * MODES, 2 * spheres), BF16),
            pltpu.VMEM((OFFSETS * MODES, 2 * spheres), BF16),
            pltpu.VMEM((2 * MODES, OFFSETS * MODES), BF16),
            pltpu.VMEM((2 * MODES, OFFSETS * MODES), BF16),
        ],
        cost_estimate=pl.CostEstimate(
            flops=6 * 2 * MODES * OFFSETS * MODES * 2 * spheres,
            bytes_accessed=2 << 20,
            transcendentals=0,
        ),
    )(where, low, coefficients, high, incident, index, link_class, link_count, translation)


def types_kernel(mine_ref, other_ref, type_ref, tmat_ref, out_ref, th, tl):
    count = mine_ref.shape[0]
    spheres = mine_ref.shape[2]
    for t in range(TYPES):
        hi, lo = split(jnp.concatenate([tmat_ref[0, t], tmat_ref[1, t]], axis=0))
        th[:, t * MODES : (t + 1) * MODES] = hi
        tl[:, t * MODES : (t + 1) * MODES] = lo
    kind = type_ref[...].reshape(1, spheres)
    for b in range(count):
        x = mine_ref[b] + other_ref[b]
        wide = jnp.concatenate([x[:MODES], x[MODES:]], axis=1)
        kinds = jnp.concatenate([kind, kind], axis=1)
        stacked = jnp.concatenate(
            [jnp.where(kinds == t, wide, 0.0) for t in range(TYPES)], axis=0
        )
        bh, bl = split(stacked)
        both = dot3(th[...], tl[...], bh, bl)
        upper, lower = both[:MODES], both[MODES:]
        out_ref[b, :MODES, :] = upper[:, :spheres] - lower[:, spheres:]
        out_ref[b, MODES:, :] = upper[:, spheres:] + lower[:, :spheres]


def apply_types(mine, other, sphere_type, t_matrix):
    return pl.pallas_call(
        types_kernel,
        name="types",
        out_shape=jax.ShapeDtypeStruct(mine.shape, F32),
        in_specs=[VMEM] * 4,
        out_specs=VMEM,
        scratch_shapes=[pltpu.VMEM((2 * MODES, TYPES * MODES), BF16)] * 2,
        cost_estimate=pl.CostEstimate(
            flops=6 * 2 * MODES * TYPES * MODES * 4 * 128, bytes_accessed=1 << 20, transcendentals=0
        ),
    )(mine, other, sphere_type, t_matrix)


def swap(x, axis, mask):
    return lax.ppermute(x, axis, [(i, i ^ mask) for i in range(lax.axis_size(axis))])


def per_device(
    coefficients,
    incident,
    positions,
    neighbour_index,
    link_class,
    link_count,
    sphere_type,
    translation,
    t_matrix,
    wave_grid,
    vertical,
    expansion,
    reflection,
    projector,
):
    block = coefficients.shape[2]
    sph = lax.axis_index("sph")
    wave = lax.axis_index("wave")
    along_x = jnp.bitwise_and(wave, 3)
    slot = jnp.right_shift(wave, 2)
    own = 2 * along_x + slot
    flip = (2 * along_x)[None]
    where = jnp.stack([own, slot, (sph - 1) * block])

    count = lax.axis_size("sph")
    own_coefs = lax.dynamic_slice_in_dim(coefficients, own, 1, 0)
    up = [(i, i + 1) for i in range(count - 1)]
    down = [(i + 1, i) for i in range(count - 1)]
    low = lax.ppermute(own_coefs, "sph", up)
    high = lax.ppermute(own_coefs, "sph", down)

    part = expand(flip, coefficients, positions, wave_grid, vertical, expansion)
    part = part + swap(part, "sph", 1)
    part = (part + swap(part, "sph", 6)) + (swap(part, "sph", 2) + swap(part, "sph", 4))
    other = swap(part, "sph", 12)

    uh, ul, qr = prepare(positions, wave_grid, vertical, reflection, projector)
    translated = translate(
        where, low, coefficients, high, incident, neighbour_index, link_class, link_count, translation
    )
    keep, to1, to2, to3 = project(part, other, qr, uh, ul, 4)
    got2, got1, got3 = swap(to2, "wave", 2), swap(to1, "wave", 1), swap(to3, "wave", 3)
    summed = ((keep + translated) + got1) + (got2 + got3)
    across = swap(summed, "wave", 4)
    updated = apply_types(summed, across, sphere_type, t_matrix)
    from2, from1, from3 = swap(updated, "wave", 2), swap(updated, "wave", 1), swap(updated, "wave", 3)
    pieces = (updated, from1, from2, from3)

    def pick(group):
        near = jnp.where(along_x == group, pieces[0], pieces[1])
        far = jnp.where(along_x == (group ^ 2), pieces[2], pieces[3])
        is_near = jnp.right_shift(along_x, 1) == (group >> 1)
        return jnp.where(is_near, near, far)

    return jnp.concatenate([pick(group) for group in range(4)], axis=0)


def solution(mesh):
    placed = (
        P(None, None, "sph"),
        P(None, None, "sph"),
        P(None, "sph"),
        P(None, "sph"),
        P(None, "sph"),
        P("sph"),
        P("sph"),
        P(),
        P(),
        P(None, "wave"),
        P("wave"),
        P(None, None, None, "wave"),
        P(None, None, None, "wave"),
        P(None, None, None, "wave"),
    )
    return jax.shard_map(
        per_device, mesh=mesh, in_specs=placed, out_specs=P(None, None, "sph"), check_vma=False
    )
```

time: 352 us -> 63.1 us (0.18)
  the two profiles are of different devices: /device:TPU:0 before, /device:TPU:1 now
where the time goes in v1:
time: 63.1 us; the launch traced here: 62.6 us
  starting transfers between devices  24.9 us (39%)
  Pallas kernels  16.3 us (26%)
  waiting for transfers between devices  14 us (22%)
  other arithmetic  4.1 us (6%)
  local copies, waits for them, and re-layouts  3.28 us (5%)
    ppermute x12, starting transfers between devices, swap(): lax.ppermute(x, axis, [(i, i ^ mask) for i in range(lax.axis_size(axis))])  18.9 us
    ppermute x12, waiting for transfers between devices, swap(): lax.ppermute(x, axis, [(i, i ^ mask) for i in range(lax.axis_size(axis))])  14 us
    pallas_call x1, Pallas kernels, translate(): pl.pallas_call(translate_kernel, name='translate', out_shape=jax.ShapeDty...  4.59 us
    ppermute x1, starting transfers between devices, per_device(): low = lax.ppermute(own_coefs, 'sph', up)  4.13 us
    pallas_call x1, Pallas kernels, expand(): pl.pallas_call(expand_kernel, name='expand', out_shape=jax.ShapeDtypeStru...  3.49 us
    pallas_call x1, Pallas kernels, project(): pl.pallas_call(project_kernel, name='project', out_shape=(piece,) * piece...  3.31 us
    pallas_call x1, Pallas kernels, prepare(): pl.pallas_call(prepare_kernel, name='prepare', out_shape=(tiles, tiles, j...  2.86 us
    unnamed x14, local copies, waits for them, and re-layouts  2.48 us
  transfers between devices with their start and end apart: 14, of which 7 were waited for; matrix products, arithmetic and copies ran while one was open for 2% of the time, Pallas kernels for 17%

profile of v1, /device:TPU:1, one launch (start us, length us, event | category | flops | bytes accessed | tf_op | source)
XLA Modules:
  0.0 62.6 jit_solution(3384476049956072399)
XLA Ops:
  0.0 3.5 %expand.1 = f32[4,8,512]{2,1,0:T(8,128)} custom-call(s32[1]{0:T(128)} %bitcast.flip_ref, f32[8,96,128]{2,1,0:T(8,128)} %own_ref.1, f32[3,128]{1,0:T(4,128)} %pos_ref.3, s32[2,512]{1,0:T(2,128)} %grid_ref.3, f32[512]{0:T(512)} %vert_ref.3, f32[2,2,48,512]{3,2,1,0:T(8,128)} %exp_ref.1), custom_call_target="tpu_custom_call" | custom-call | flops 603979776 | bytes 4194304 | tf_op jit(solution)/shard_map/expand/pallas_call | solution.py:95
  3.5 1.4 %collective-permute-start = (f32[4,8,512]{2,1,0:T(8,128)}, f32[4,8,512]{2,1,0:T(8,128)S(1)}, u32[]{:S(2)}, u32[]{:S(2)}) collective-permute-start(f32[4,8,512]{2,1,0:T(8,128)} %expand.1), channel_id=1, source_target_pairs={{0,8},{8,0},{16,24},{24,16},{32,40},{40,32},{48,56},{56,48},{64,72... | collective-permute-start | bytes 196616 | tf_op jit(solution)/shard_map/ppermute | solution.py:306
  4.9 1.1 %collective-permute-done = f32[4,8,512]{2,1,0:T(8,128)S(1)} collective-permute-done((f32[4,8,512]{2,1,0:T(8,128)}, f32[4,8,512]{2,1,0:T(8,128)S(1)}, u32[]{:S(2)}, u32[]{:S(2)}) %collective-permute-start) | collective-permute-done | bytes 65568 | tf_op jit(solution)/shard_map/ppermute | solution.py:306
  6.0 0.9 %add.31 = f32[4,8,512]{2,1,0:T(8,128)S(1)} add(f32[4,8,512]{2,1,0:T(8,128)} %expand.1, f32[4,8,512]{2,1,0:T(8,128)S(1)} %collective-permute-done) | non-fusion elementwise | flops 16384 | bytes 196608 | tf_op jit(solution)/shard_map/add | solution.py:342
  6.8 2.8 %collective-permute-start.1 = (f32[4,8,512]{2,1,0:T(8,128)S(1)}, f32[4,8,512]{2,1,0:T(8,128)S(1)}, u32[]{:S(2)}, u32[]{:S(2)}) collective-permute-start(f32[4,8,512]{2,1,0:T(8,128)S(1)} %add.31), channel_id=1, source_target_pairs={{0,48},{8,56},{16,32},{24,40},{32,16},{40,24},{48,0},{56,8},{64,11... | collective-permute-start | bytes 196616 | tf_op jit(solution)/shard_map/ppermute | solution.py:306
  10.1 1.7 %collective-permute-done.1 = f32[4,8,512]{2,1,0:T(8,128)S(1)} collective-permute-done((f32[4,8,512]{2,1,0:T(8,128)S(1)}, f32[4,8,512]{2,1,0:T(8,128)S(1)}, u32[]{:S(2)}, u32[]{:S(2)}) %collective-permute-start.1) | collective-permute-done | bytes 65568 | tf_op jit(solution)/shard_map/ppermute | solution.py:306
  11.8 1.2 %collective-permute-done.2 = f32[4,8,512]{2,1,0:T(8,128)S(1)} collective-permute-done((f32[4,8,512]{2,1,0:T(8,128)S(1)}, f32[4,8,512]{2,1,0:T(8,128)S(1)}, u32[]{:S(2)}, u32[]{:S(2)}) %collective-permute-start.2) | collective-permute-done | bytes 65568 | tf_op jit(solution)/shard_map/ppermute | solution.py:306
  13.1 3.9 %collective-permute-start.4 = (f32[4,8,512]{2,1,0:T(8,128)S(1)}, f32[4,8,512]{2,1,0:T(8,128)S(1)}, u32[]{:S(2)}, u32[]{:S(2)}) collective-permute-start(f32[4,8,512]{2,1,0:T(8,128)S(1)} %add_add_fusion.1.mine_ref), channel_id=1, source_target_pairs={{0,96},{8,104},{16,112},{24,120},{32,64},{40,72},{48,80},{56,88},{... | collective-permute-start | bytes 196616 | tf_op jit(solution)/shard_map/ppermute | solution.py:306
  16.9 0.8 %constant_dynamic-slice_fusion = f32[1,96,128]{2,1,0:T(8,128)S(1)} fusion(f32[8,96,128]{2,1,0:T(8,128)} %own_ref.1, s32[]{:T(128)S(6)} %select_n.67), kind=kLoop, calls=%fused_computation.8 | loop fusion | bytes 98308 | tf_op jit(solution)/shard_map/dynamic_slice | solution.py:335
  17.7 4.1 %collective-permute-start.5 = (f32[1,96,128]{2,1,0:T(8,128)S(1)}, f32[1,96,128]{2,1,0:T(8,128)S(1)}, u32[]{:S(2)}, u32[]{:S(2)}) collective-permute-start(f32[1,96,128]{2,1,0:T(8,128)S(1)} %constant_dynamic-slice_fusion), channel_id=1, source_target_pairs={{0,8},{8,16},{16,24},{24,32},{32,40},{40,48},{48,56},{56,64},{64,7... | collective-permute-start | bytes 147464 | tf_op jit(solution)/shard_map/ppermute | solution.py:338
  21.9 1.9 %collective-permute-start.6 = (f32[1,96,128]{2,1,0:T(8,128)S(1)}, f32[1,96,128]{2,1,0:T(8,128)S(1)}, u32[]{:S(2)}, u32[]{:S(2)}) collective-permute-start(f32[1,96,128]{2,1,0:T(8,128)S(1)} %constant_dynamic-slice_fusion), channel_id=1, source_target_pairs={{8,0},{16,8},{24,16},{32,24},{40,32},{48,40},{56,48},{64,56},{72,6... | collective-permute-start | bytes 147464 | tf_op jit(solution)/shard_map/ppermute | solution.py:339
  23.8 2.9 %prepare.1 = (bf16[1024,256]{1,0:T(8,128)(2,1)}, bf16[1024,256]{1,0:T(8,128)(2,1)}, f32[4,48,512]{2,1,0:T(8,128)}) custom-call(f32[3,128]{1,0:T(4,128)} %pos_ref.3, s32[2,512]{1,0:T(2,128)} %grid_ref.3, f32[512]{0:T(512)} %vert_ref.3, f32[2,2,2,512]{3,2,1,0:T(2,128)} %refl_ref.1, f32[2,48,2,512]{3,2,1,0:T(2,128)} %proj_ref.1), custom_call_target="tpu_custom_call" | custom-call | flops 2097152 | bytes 2097152 | tf_op jit(solution)/shard_map/prepare/pallas_call | solution.py:146
  26.7 0.6 copy-done.6
  27.3 3.3 %project.1 = (f32[2,96,128]{2,1,0:T(8,128)}, f32[2,96,128]{2,1,0:T(8,128)}, f32[2,96,128]{2,1,0:T(8,128)}, f32[2,96,128]{2,1,0:T(8,128)}) custom-call(f32[4,8,512]{2,1,0:T(8,128)} %copy-done.3, f32[4,8,512]{2,1,0:T(8,128)} %copy-done.6, f32[4,48,512]{2,1,0:T(8,128)} %get-tuple-element.12.qr_ref, bf16[1024,256]{1,0:T(8,128)(2,1)} %get-tuple-element.13.uh, ...), custom_call_target="tpu_custom_call" | custom-call | flops 603979776 | bytes 3145728 | tf_op jit(solution)/shard_map/project/pallas_call | solution.py:189
  30.6 1.2 %collective-permute-start.7 = (f32[2,96,128]{2,1,0:T(8,128)}, f32[2,96,128]{2,1,0:T(8,128)S(1)}, u32[]{:S(2)}, u32[]{:S(2)}) collective-permute-start(f32[2,96,128]{2,1,0:T(8,128)} %get-tuple-element.16), channel_id=1, source_target_pairs={{0,1},{1,0},{2,3},{3,2},{4,5},{5,4},{6,7},{7,6},{8,9},{9,8},{10,11... | collective-permute-start | bytes 294920 | tf_op jit(solution)/shard_map/ppermute | solution.py:306
  31.8 2.5 %collective-permute-start.8 = (f32[2,96,128]{2,1,0:T(8,128)}, f32[2,96,128]{2,1,0:T(8,128)S(1)}, u32[]{:S(2)}, u32[]{:S(2)}) collective-permute-start(f32[2,96,128]{2,1,0:T(8,128)} %get-tuple-element.17), channel_id=1, source_target_pairs={{0,2},{1,3},{2,0},{3,1},{4,6},{5,7},{6,4},{7,5},{8,10},{9,11},{10,... | collective-permute-start | bytes 294920 | tf_op jit(solution)/shard_map/ppermute | solution.py:306
  34.5 0.6 pad_add_fusion.where_ref
  35.1 0.6 copy-done.4
  35.7 0.6 copy-done.5
  36.3 4.6 %translate.1 = f32[2,96,128]{2,1,0:T(8,128)} custom-call(s32[3]{0:T(128)} %pad_add_fusion.where_ref, f32[1,96,128]{2,1,0:T(8,128)} %copy-done.4, f32[8,96,128]{2,1,0:T(8,128)} %own_ref.1, f32[1,96,128]{2,1,0:T(8,128)} %copy-done.5, f32[8,96,128]{2,1,0:T(8,128)} %inc_ref.1, s32[12,128]{1,0:T(8,128)} %idx_ref.1, s32[12,128]{1,0:T(8,128)} %class_ref.1, ...), custom_call_target="tpu_custom_call" | custom-call | flops 184025088 | bytes 2097152 | tf_op jit(solution)/shard_map/translate/pallas_call | solution.py:249
  40.9 0.9 %add_add_fusion.mine_ref = f32[2,96,128]{2,1,0:T(8,128)S(1)} fusion(f32[2,96,128]{2,1,0:T(8,128)S(1)} %collective-permute-done.8, f32[2,96,128]{2,1,0:T(8,128)S(1)} %collective-permute-done.9, f32[2,96,128]{2,1,0:T(8,128)S(1)} %collective-permute-done.7, f32[2,96,128]{2,1,0:T(8,128)S(1)} %copy-done.1, f32[2,96,128]{2,1,0:T(8,128)} %translate.1), kind=kLoop, calls=%fused_computation.5 | loop fusion | flops 98304 | bytes 589824 | tf_op jit(solution)/shard_map/add | solution.py:352
  41.9 2.7 %collective-permute-start.10 = (f32[2,96,128]{2,1,0:T(8,128)S(1)}, f32[2,96,128]{2,1,0:T(8,128)S(1)}, u32[]{:S(2)}, u32[]{:S(2)}) collective-permute-start(f32[2,96,128]{2,1,0:T(8,128)S(1)} %add_add_fusion.mine_ref), channel_id=1, source_target_pairs={{0,4},{1,5},{2,6},{3,7},{4,0},{5,1},{6,2},{7,3},{8,12},{9,13},{10,... | collective-permute-start | bytes 294920 | tf_op jit(solution)/shard_map/ppermute | solution.py:306
  44.6 3.2 %collective-permute-done.10.other_ref = f32[2,96,128]{2,1,0:T(8,128)S(1)} collective-permute-done((f32[2,96,128]{2,1,0:T(8,128)S(1)}, f32[2,96,128]{2,1,0:T(8,128)S(1)}, u32[]{:S(2)}, u32[]{:S(2)}) %collective-permute-start.10) | collective-permute-done | bytes 98336 | tf_op jit(solution)/shard_map/ppermute | solution.py:306
  47.7 0.6 %copy-done.2 = f32[2,96,128]{2,1,0:T(8,128)} copy-done((f32[2,96,128]{2,1,0:T(8,128)}, f32[2,96,128]{2,1,0:T(8,128)S(1)}, u32[]{:S(2)}) %copy-start.2) | copy-done | bytes 98328
  48.4 2.0 %types.1 = f32[2,96,128]{2,1,0:T(8,128)} custom-call(f32[2,96,128]{2,1,0:T(8,128)} %copy-done, f32[2,96,128]{2,1,0:T(8,128)} %copy-done.2, s32[128]{0:T(128)} %type_ref.1, f32[2,4,48,48]{3,2,1,0:T(8,128)} %tmat_ref.1), custom_call_target="tpu_custom_call" | custom-call | flops 56623104 | bytes 1048576 | tf_op jit(solution)/shard_map/types/pallas_call | solution.py:292
  50.4 2.8 %collective-permute-start.12 = (f32[2,96,128]{2,1,0:T(8,128)}, f32[2,96,128]{2,1,0:T(8,128)S(1)}, u32[]{:S(2)}, u32[]{:S(2)}) collective-permute-start(f32[2,96,128]{2,1,0:T(8,128)} %types.1), channel_id=1, source_target_pairs={{0,2},{1,3},{2,0},{3,1},{4,6},{5,7},{6,4},{7,5},{8,10},{9,11},{10,... | collective-permute-start | bytes 294920 | tf_op jit(solution)/shard_map/ppermute | solution.py:306
  53.2 1.0 %collective-permute-start.13 = (f32[2,96,128]{2,1,0:T(8,128)}, f32[2,96,128]{2,1,0:T(8,128)S(1)}, u32[]{:S(2)}, u32[]{:S(2)}) collective-permute-start(f32[2,96,128]{2,1,0:T(8,128)} %types.1), channel_id=1, source_target_pairs={{0,3},{1,2},{2,1},{3,0},{4,7},{5,6},{6,5},{7,4},{8,11},{9,10},{10,... | collective-permute-start | bytes 294920 | tf_op jit(solution)/shard_map/ppermute | solution.py:306
  54.2 0.3 collective-permute-done.11
  54.5 4.2 %collective-permute-done.12 = f32[2,96,128]{2,1,0:T(8,128)S(1)} collective-permute-done((f32[2,96,128]{2,1,0:T(8,128)}, f32[2,96,128]{2,1,0:T(8,128)S(1)}, u32[]{:S(2)}, u32[]{:S(2)}) %collective-permute-start.12) | collective-permute-done | bytes 98336 | tf_op jit(solution)/shard_map/ppermute | solution.py:306
  58.8 2.1 %collective-permute-done.13 = f32[2,96,128]{2,1,0:T(8,128)S(1)} collective-permute-done((f32[2,96,128]{2,1,0:T(8,128)}, f32[2,96,128]{2,1,0:T(8,128)S(1)}, u32[]{:S(2)}, u32[]{:S(2)}) %collective-permute-start.13) | collective-permute-done | bytes 98336 | tf_op jit(solution)/shard_map/ppermute | solution.py:306
  60.9 0.9 %select_select_fusion.3 = (f32[2,96,128]{2,1,0:T(8,128)S(1)}, f32[2,96,128]{2,1,0:T(8,128)S(1)}, f32[2,96,128]{2,1,0:T(8,128)S(1)}, f32[2,96,128]{2,1,0:T(8,128)S(1)}) fusion(f32[2,96,128]{2,1,0:T(8,128)S(1)} %collective-permute-done.12, f32[2,96,128]{2,1,0:T(8,128)S(1)} %collective-permute-done.13, f32[2,96,128]{2,1,0:T(8,128)} %types.1, ...), kind=kLoop, calls=%fused_computation.4 | loop fusion | flops 294912 | bytes 786438 | tf_op jit(solution)/shard_map/jit(_where)/select_n | solution.py:362
  61.9 0.8 %pad_maximum_fusion = f32[8,96,128]{2,1,0:T(8,128)} fusion(f32[2,96,128]{2,1,0:T(8,128)S(1)} %get-tuple-element.20, f32[2,96,128]{2,1,0:T(8,128)S(1)} %get-tuple-element.21, f32[2,96,128]{2,1,0:T(8,128)S(1)} %get-tuple-element.22, f32[2,96,128]{2,1,0:T(8,128)S(1)} %get-tuple-element.19), kind=kLoop, calls=%fused_computation | loop fusion | flops 294912 | bytes 786432 | tf_op jit(solution)/shard_map/concatenate | solution.py:364
  (22 shorter events, 0.7 us)
Async XLA Ops:
  3.5 2.5 %collective-permute-start = (f32[4,8,512]{2,1,0:T(8,128)}, f32[4,8,512]{2,1,0:T(8,128)S(1)}, u32[]{:S(2)}, u32[]{:S(2)}) collective-permute-start(f32[4,8,512]{2,1,0:T(8,128)} %expand.1), channel_id=1, source_target_pairs={{0,8},{8,0},{16,24},{24,16},{32,40},{40,32},{48,56},{56,48},{64,72... | collective-permute-start | bytes 196616 | tf_op jit(solution)/shard_map/ppermute | solution.py:306
  6.8 5.0 %collective-permute-start.1 = (f32[4,8,512]{2,1,0:T(8,128)S(1)}, f32[4,8,512]{2,1,0:T(8,128)S(1)}, u32[]{:S(2)}, u32[]{:S(2)}) collective-permute-start(f32[4,8,512]{2,1,0:T(8,128)S(1)} %add.31), channel_id=1, source_target_pairs={{0,48},{8,56},{16,32},{24,40},{32,16},{40,24},{48,0},{56,8},{64,11... | collective-permute-start | bytes 196616 | tf_op jit(solution)/shard_map/ppermute | solution.py:306
  9.7 3.3 %collective-permute-start.2 = (f32[4,8,512]{2,1,0:T(8,128)S(1)}, f32[4,8,512]{2,1,0:T(8,128)S(1)}, u32[]{:S(2)}, u32[]{:S(2)}) collective-permute-start(f32[4,8,512]{2,1,0:T(8,128)S(1)} %add.31), channel_id=1, source_target_pairs={{0,16},{8,24},{16,0},{24,8},{32,48},{40,56},{48,32},{56,40},{64,80... | collective-permute-start | bytes 196616 | tf_op jit(solution)/shard_map/ppermute | solution.py:306
  9.9 3.2 %collective-permute-start.3 = (f32[4,8,512]{2,1,0:T(8,128)S(1)}, f32[4,8,512]{2,1,0:T(8,128)S(1)}, u32[]{:S(2)}, u32[]{:S(2)}) collective-permute-start(f32[4,8,512]{2,1,0:T(8,128)S(1)} %add.31), channel_id=1, source_target_pairs={{0,32},{8,40},{16,48},{24,56},{32,0},{40,8},{48,16},{56,24},{64,96... | collective-permute-start | bytes 196616 | tf_op jit(solution)/shard_map/ppermute | solution.py:306
  13.1 13.6 %copy-start.3 = (f32[4,8,512]{2,1,0:T(8,128)}, f32[4,8,512]{2,1,0:T(8,128)S(1)}, u32[]{:S(2)}) copy-start(f32[4,8,512]{2,1,0:T(8,128)S(1)} %add_add_fusion.1.mine_ref) | copy-start | bytes 196612
  13.1 13.6 %collective-permute-start.4 = (f32[4,8,512]{2,1,0:T(8,128)S(1)}, f32[4,8,512]{2,1,0:T(8,128)S(1)}, u32[]{:S(2)}, u32[]{:S(2)}) collective-permute-start(f32[4,8,512]{2,1,0:T(8,128)S(1)} %add_add_fusion.1.mine_ref), channel_id=1, source_target_pairs={{0,96},{8,104},{16,112},{24,120},{32,64},{40,72},{48,80},{56,88},{... | collective-permute-start | bytes 196616 | tf_op jit(solution)/shard_map/ppermute | solution.py:306
  17.7 17.3 %collective-permute-start.5 = (f32[1,96,128]{2,1,0:T(8,128)S(1)}, f32[1,96,128]{2,1,0:T(8,128)S(1)}, u32[]{:S(2)}, u32[]{:S(2)}) collective-permute-start(f32[1,96,128]{2,1,0:T(8,128)S(1)} %constant_dynamic-slice_fusion), channel_id=1, source_target_pairs={{0,8},{8,16},{16,24},{24,32},{32,40},{40,48},{48,56},{56,64},{64,7... | collective-permute-start | bytes 147464 | tf_op jit(solution)/shard_map/ppermute | solution.py:338
  21.9 13.2 %collective-permute-start.6 = (f32[1,96,128]{2,1,0:T(8,128)S(1)}, f32[1,96,128]{2,1,0:T(8,128)S(1)}, u32[]{:S(2)}, u32[]{:S(2)}) collective-permute-start(f32[1,96,128]{2,1,0:T(8,128)S(1)} %constant_dynamic-slice_fusion), channel_id=1, source_target_pairs={{8,0},{16,8},{24,16},{32,24},{40,32},{48,40},{56,48},{64,56},{72,6... | collective-permute-start | bytes 147464 | tf_op jit(solution)/shard_map/ppermute | solution.py:339
  26.7 0.6 copy-start.6
  30.6 10.3 %copy-start.1 = (f32[2,96,128]{2,1,0:T(8,128)S(1)}, f32[2,96,128]{2,1,0:T(8,128)}, u32[]{:S(2)}) copy-start(f32[2,96,128]{2,1,0:T(8,128)} %get-tuple-element.15) | copy-start | bytes 294916
  30.6 10.3 %collective-permute-start.7 = (f32[2,96,128]{2,1,0:T(8,128)}, f32[2,96,128]{2,1,0:T(8,128)S(1)}, u32[]{:S(2)}, u32[]{:S(2)}) collective-permute-start(f32[2,96,128]{2,1,0:T(8,128)} %get-tuple-element.16), channel_id=1, source_target_pairs={{0,1},{1,0},{2,3},{3,2},{4,5},{5,4},{6,7},{7,6},{8,9},{9,8},{10,11... | collective-permute-start | bytes 294920 | tf_op jit(solution)/shard_map/ppermute | solution.py:306
  31.8 9.1 %collective-permute-start.8 = (f32[2,96,128]{2,1,0:T(8,128)}, f32[2,96,128]{2,1,0:T(8,128)S(1)}, u32[]{:S(2)}, u32[]{:S(2)}) collective-permute-start(f32[2,96,128]{2,1,0:T(8,128)} %get-tuple-element.17), channel_id=1, source_target_pairs={{0,2},{1,3},{2,0},{3,1},{4,6},{5,7},{6,4},{7,5},{8,10},{9,11},{10,... | collective-permute-start | bytes 294920 | tf_op jit(solution)/shard_map/ppermute | solution.py:306
  34.3 6.6 %collective-permute-start.9 = (f32[2,96,128]{2,1,0:T(8,128)}, f32[2,96,128]{2,1,0:T(8,128)S(1)}, u32[]{:S(2)}, u32[]{:S(2)}) collective-permute-start(f32[2,96,128]{2,1,0:T(8,128)} %get-tuple-element.18), channel_id=1, source_target_pairs={{0,3},{1,2},{2,1},{3,0},{4,7},{5,6},{6,5},{7,4},{8,11},{9,10},{10,... | collective-permute-start | bytes 294920 | tf_op jit(solution)/shard_map/ppermute | solution.py:306
  35.1 0.6 copy-start.4
  35.7 0.6 copy-start.5
  41.8 5.9 %copy-start = (f32[2,96,128]{2,1,0:T(8,128)}, f32[2,96,128]{2,1,0:T(8,128)S(1)}, u32[]{:S(2)}) copy-start(f32[2,96,128]{2,1,0:T(8,128)S(1)} %add_add_fusion.mine_ref) | copy-start | bytes 294916
  41.9 5.9 %collective-permute-start.10 = (f32[2,96,128]{2,1,0:T(8,128)S(1)}, f32[2,96,128]{2,1,0:T(8,128)S(1)}, u32[]{:S(2)}, u32[]{:S(2)}) collective-permute-start(f32[2,96,128]{2,1,0:T(8,128)S(1)} %add_add_fusion.mine_ref), channel_id=1, source_target_pairs={{0,4},{1,5},{2,6},{3,7},{4,0},{5,1},{6,2},{7,3},{8,12},{9,13},{10,... | collective-permute-start | bytes 294920 | tf_op jit(solution)/shard_map/ppermute | solution.py:306
  47.7 0.6 %copy-start.2 = (f32[2,96,128]{2,1,0:T(8,128)}, f32[2,96,128]{2,1,0:T(8,128)S(1)}, u32[]{:S(2)}) copy-start(f32[2,96,128]{2,1,0:T(8,128)S(1)} %collective-permute-done.10.other_ref) | copy-start | bytes 294916
  50.4 4.2 %collective-permute-start.11 = (f32[2,96,128]{2,1,0:T(8,128)}, f32[2,96,128]{2,1,0:T(8,128)S(1)}, u32[]{:S(2)}, u32[]{:S(2)}) collective-permute-start(f32[2,96,128]{2,1,0:T(8,128)} %types.1), channel_id=1, source_target_pairs={{0,1},{1,0},{2,3},{3,2},{4,5},{5,4},{6,7},{7,6},{8,9},{9,8},{10,11... | collective-permute-start | bytes 294920 | tf_op jit(solution)/shard_map/ppermute | solution.py:306
  50.4 8.4 %collective-permute-start.12 = (f32[2,96,128]{2,1,0:T(8,128)}, f32[2,96,128]{2,1,0:T(8,128)S(1)}, u32[]{:S(2)}, u32[]{:S(2)}) collective-permute-start(f32[2,96,128]{2,1,0:T(8,128)} %types.1), channel_id=1, source_target_pairs={{0,2},{1,3},{2,0},{3,1},{4,6},{5,7},{6,4},{7,5},{8,10},{9,11},{10,... | collective-permute-start | bytes 294920 | tf_op jit(solution)/shard_map/ppermute | solution.py:306
  53.2 7.7 %collective-permute-start.13 = (f32[2,96,128]{2,1,0:T(8,128)}, f32[2,96,128]{2,1,0:T(8,128)S(1)}, u32[]{:S(2)}, u32[]{:S(2)}) collective-permute-start(f32[2,96,128]{2,1,0:T(8,128)} %types.1), channel_id=1, source_target_pairs={{0,3},{1,2},{2,1},{3,0},{4,7},{5,6},{6,5},{7,4},{8,11},{9,10},{10,... | collective-permute-start | bytes 294920 | tf_op jit(solution)/shard_map/ppermute | solution.py:306

commit v2 on v1

--- a/solution.py
+++ b/solution.py
@@ -5,6 +5,7 @@
 from jax.experimental.pallas import tpu as pltpu
 from jax.sharding import PartitionSpec as P
 
+
 MODES = 48
 OFFSETS = 26
 TYPES = 4
@@ -15,9 +16,11 @@
 COS_POLY = (1.0, -4.93480214, 4.05870916, -1.335212, 0.23493731, -0.02439632)
 
 VMEM = pl.BlockSpec(memory_space=pltpu.VMEM)
+HBM = pl.BlockSpec(memory_space=pltpu.HBM)
 SMEM = pl.BlockSpec(memory_space=pltpu.SMEM)
 BF16 = jnp.bfloat16
 F32 = jnp.float32
+PARAMS = pltpu.CompilerParams(vmem_limit_bytes=12 << 20)
 
 
 def horner(coefs, t):
@@ -52,10 +55,53 @@
     return jnp.concatenate([rows, pad], axis=0).T
 
 
-def expand_kernel(flip_ref, coef_ref, pos_ref, grid_ref, vert_ref, exp_ref, out_ref, ah, al, spec):
+def expand_kernel(
+    flip_ref,
+    own_ref,
+    coef_hbm,
+    pos_hbm,
+    grid_hbm,
+    vert_hbm,
+    exp_hbm,
+    out_ref,
+    mine_ref,
+    coef_ref,
+    pos_ref,
+    grid_ref,
+    vert_ref,
+    exp_ref,
+    ah,
+    al,
+    spec,
+    sems,
+):
+    copies = [
+        pltpu.make_async_copy(source, target, sems.at[i])
+        for i, (source, target) in enumerate(
+            (
+                (pos_hbm, pos_ref),
+                (grid_hbm, grid_ref),
+                (vert_hbm, vert_ref),
+                (coef_hbm, coef_ref),
+                (exp_hbm, exp_ref),
+            )
+        )
+    ]
+    for copy in copies:
+        copy.start()
     illums = coef_ref.shape[0]
     waves = grid_ref.shape[1]
     half = illums * MODES
+    for copy in copies[:3]:
+        copy.wait()
+    pos = columns(pos_ref[...])
+    grid = grid_ref[...].astype(F32)
+    vert = vert_ref[...].reshape(1, waves) * INV_TWO_PI
+    turns = pos[:, 0:1] * grid[0:1] + pos[:, 1:2] * grid[1:2] - pos[:, 2:3] * vert
+    cos, sin = cos_sin_turns(turns)
+    bh, bl = split(jnp.concatenate([cos, sin], axis=0))
+    copies[3].wait()
+    mine_ref[0] = coef_ref[own_ref[0]]
     for b in range(illums):
         block = coef_ref[jnp.bitwise_xor(flip_ref[0], b)]
         re, im = block[:MODES], block[MODES:]
@@ -65,17 +111,11 @@
                 hi, lo = split(part)
                 ah[rows, offset : offset + 128] = hi
                 al[rows, offset : offset + 128] = lo
-    pos = columns(pos_ref[...])
-    grid = grid_ref[...].astype(F32)
-    vert = vert_ref[...].reshape(1, waves) * INV_TWO_PI
+    copies[4].wait()
     width = 256
     for start in range(0, waves, width):
         lanes = slice(start, start + width)
-        turns = pos[:, 0:1] * grid[0:1, lanes] + pos[:, 1:2] * grid[1:2, lanes]
-        turns = turns - pos[:, 2:3] * vert[:, lanes]
-        cos, sin = cos_sin_turns(turns)
-        bh, bl = split(jnp.concatenate([cos, sin], axis=0))
-        spec[...] = dot3(ah[...], al[...], bh, bl)
+        spec[...] = dot3(ah[...], al[...], bh[:, lanes], bl[:, lanes])
         for p in range(2):
             er, ei = exp_ref[0, p, :, lanes], exp_ref[1, p, :, lanes]
             out_re, out_im = [], []
@@ -88,28 +128,39 @@
             out_ref[2 * p + 1, :, lanes] = jnp.concatenate(out_im, axis=0)
 
 
-def expand(flip, coefficients, positions, wave_grid, vertical, expansion):
+def expand(flip, own, coefficients, positions, wave_grid, vertical, expansion):
     illums, _, spheres = coefficients.shape
     waves = wave_grid.shape[1]
     rows = illums * 2 * MODES
+    arrays = (coefficients, positions, wave_grid, vertical, expansion)
     return pl.pallas_call(
         expand_kernel,
         name="expand",
-        out_shape=jax.ShapeDtypeStruct((4, illums, waves), F32),
-        in_specs=[SMEM] + [VMEM] * 5,
-        out_specs=VMEM,
-        scratch_shapes=[
+        out_shape=(
+            jax.ShapeDtypeStruct((4, illums, waves), F32),
+            jax.ShapeDtypeStruct((1, 2 * MODES, spheres), F32),
+        ),
+        in_specs=[SMEM] * 2 + [HBM] * 5,
+        out_specs=(VMEM, VMEM),
+        scratch_shapes=[pltpu.VMEM(x.shape, x.dtype) for x in arrays]
+        + [
             pltpu.VMEM((rows, 2 * spheres), BF16),
             pltpu.VMEM((rows, 2 * spheres), BF16),
             pltpu.VMEM((rows, 256), F32),
+            pltpu.SemaphoreType.DMA((5,)),
         ],
+        compiler_params=PARAMS,
         cost_estimate=pl.CostEstimate(
             flops=6 * rows * 2 * spheres * waves, bytes_accessed=4 << 20, transcendentals=0
         ),
-    )(flip, coefficients, positions, wave_grid, vertical, expansion)
-
-
-def prepare_kernel(pos_ref, grid_ref, vert_ref, refl_ref, proj_ref, uh, ul, qr_ref):
+    )(flip, own, *(pltpu.with_memory_space_constraint(x, pltpu.HBM) for x in arrays))
+
+
+def prepare_kernel(pos_ref, grid_ref, vert_ref, refl_ref, proj_ref, tmat_ref, uh, ul, qr_ref, th, tl):
+    for t in range(TYPES):
+        hi, lo = split(jnp.concatenate([tmat_ref[0, t], tmat_ref[1, t]], axis=0))
+        th[:, t * MODES : (t + 1) * MODES] = hi
+        tl[:, t * MODES : (t + 1) * MODES] = lo
     waves = grid_ref.shape[1]
     spheres = pos_ref.shape[1]
     grid = grid_ref[...].astype(F32)
@@ -139,20 +190,22 @@
         qr_ref[2 * q + 1] = acc_im
 
 
-def prepare(positions, wave_grid, vertical, reflection, projector):
+def prepare(positions, wave_grid, vertical, reflection, projector, t_matrix):
     waves = wave_grid.shape[1]
     spheres = positions.shape[1]
     tiles = jax.ShapeDtypeStruct((2 * waves, 2 * spheres), BF16)
+    types = jax.ShapeDtypeStruct((2 * MODES, TYPES * MODES), BF16)
     return pl.pallas_call(
         prepare_kernel,
         name="prepare",
-        out_shape=(tiles, tiles, jax.ShapeDtypeStruct((4, MODES, waves), F32)),
-        in_specs=[VMEM] * 5,
-        out_specs=(VMEM,) * 3,
+        out_shape=(tiles, tiles, jax.ShapeDtypeStruct((4, MODES, waves), F32), types, types),
+        in_specs=[VMEM] * 6,
+        out_specs=(VMEM,) * 5,
+        compiler_params=PARAMS,
         cost_estimate=pl.CostEstimate(
             flops=2 << 20, bytes_accessed=2 << 20, transcendentals=0
         ),
-    )(positions, wave_grid, vertical, reflection, projector)
+    )(positions, wave_grid, vertical, reflection, projector, t_matrix)
 
 
 def project_kernel(mine_ref, other_ref, qr_ref, uh, ul, *refs):
@@ -193,6 +246,7 @@
         in_specs=[VMEM] * 5,
         out_specs=(VMEM,) * pieces,
         scratch_shapes=[pltpu.VMEM((illums * MODES, 2 * waves), BF16)] * 2,
+        compiler_params=PARAMS,
         cost_estimate=pl.CostEstimate(
             flops=6 * illums * MODES * 2 * waves * 2 * spheres,
             bytes_accessed=3 << 20,
@@ -202,18 +256,18 @@
 
 
 def translate_kernel(
-    where_ref, low_ref, own_ref, high_ref, inc_ref, idx_ref, class_ref, count_ref, trans_ref, out_ref, bh, bl, gh, gl
+    pick_ref, slot_ref, base_ref, low_ref, own_ref, high_ref, inc_ref, idx_ref, class_ref, count_ref, trans_ref, out_ref, bh, bl, gh, gl
 ):
-    own = where_ref[0]
-    slot = where_ref[1]
-    base = where_ref[2]
+    own = pick_ref[0]
+    slot = slot_ref[0]
+    base = base_ref[0]
     spheres = own_ref.shape[2]
     local = idx_ref[...] - base
     side = jnp.right_shift(local, 7)
     lane = jnp.bitwise_and(local, 127)
     live = lax.broadcasted_iota(jnp.int32, local.shape, 0) < count_ref[...].reshape(1, spheres)
     kind = jnp.where(live, class_ref[...], OFFSETS)
-    source = (low_ref[0], own_ref[own], high_ref[0])
+    source = (low_ref[0], own_ref[0], high_ref[0])
     shape = (2 * MODES, spheres)
     picked = []
     for k in range(LINKS):
@@ -244,13 +298,13 @@
     out_ref[1] = jnp.where(slot == 0, 0.0, result)
 
 
-def translate(where, low, coefficients, high, incident, index, link_class, link_count, translation):
+def translate(own, slot, base, low, mine, high, incident, index, link_class, link_count, translation):
     spheres = index.shape[1]
     return pl.pallas_call(
         translate_kernel,
         name="translate",
         out_shape=jax.ShapeDtypeStruct((2, 2 * MODES, spheres), F32),
-        in_specs=[SMEM] + [VMEM] * 8,
+        in_specs=[SMEM] * 3 + [VMEM] * 8,
         out_specs=VMEM,
         scratch_shapes=[
             pltpu.VMEM((OFFSETS * MODES, 2 * spheres), BF16),
@@ -258,21 +312,18 @@
             pltpu.VMEM((2 * MODES, OFFSETS * MODES), BF16),
             pltpu.VMEM((2 * MODES, OFFSETS * MODES), BF16),
         ],
+        compiler_params=PARAMS,
         cost_estimate=pl.CostEstimate(
             flops=6 * 2 * MODES * OFFSETS * MODES * 2 * spheres,
             bytes_accessed=2 << 20,
             transcendentals=0,
         ),
-    )(where, low, coefficients, high, incident, index, link_class, link_count, translation)
-
-
-def types_kernel(mine_ref, other_ref, type_ref, tmat_ref, out_ref, th, tl):
+    )(own, slot, base, low, mine, high, incident, index, link_class, link_count, translation)
+
+
+def types_kernel(mine_ref, other_ref, type_ref, th, tl, out_ref):
     count = mine_ref.shape[0]
     spheres = mine_ref.shape[2]
-    for t in range(TYPES):
-        hi, lo = split(jnp.concatenate([tmat_ref[0, t], tmat_ref[1, t]], axis=0))
-        th[:, t * MODES : (t + 1) * MODES] = hi
-        tl[:, t * MODES : (t + 1) * MODES] = lo
     kind = type_ref[...].reshape(1, spheres)
     for b in range(count):
         x = mine_ref[b] + other_ref[b]
@@ -288,18 +339,46 @@
         out_ref[b, MODES:, :] = upper[:, spheres:] + lower[:, :spheres]
 
 
-def apply_types(mine, other, sphere_type, t_matrix):
+def apply_types(mine, other, sphere_type, th, tl):
     return pl.pallas_call(
         types_kernel,
         name="types",
         out_shape=jax.ShapeDtypeStruct(mine.shape, F32),
-        in_specs=[VMEM] * 4,
+        in_specs=[VMEM] * 5,
         out_specs=VMEM,
-        scratch_shapes=[pltpu.VMEM((2 * MODES, TYPES * MODES), BF16)] * 2,
+        compiler_params=PARAMS,
         cost_estimate=pl.CostEstimate(
             flops=6 * 2 * MODES * TYPES * MODES * 4 * 128, bytes_accessed=1 << 20, transcendentals=0
         ),
-    )(mine, other, sphere_type, t_matrix)
+    )(mine, other, sphere_type, th, tl)
+
+
+def place_kernel(flip_ref, *refs):
+    pieces, (out_ref, sems) = refs[:-2], refs[-2:]
+    size = pieces[0].shape[0]
+    copies = []
+    for i, piece in enumerate(pieces):
+        start = jnp.bitwise_xor(flip_ref[0], size * i)
+        copies.append(pltpu.make_async_copy(piece, out_ref.at[pl.ds(start, size)], sems.at[i]))
+    for copy in copies:
+        copy.start()
+    for copy in copies:
+        copy.wait()
+
+
+def place(flip, pieces):
+    count = len(pieces)
+    shape = (count * pieces[0].shape[0],) + pieces[0].shape[1:]
+    return pl.pallas_call(
+        place_kernel,
+        name="place",
+        out_shape=jax.ShapeDtypeStruct(shape, F32),
+        in_specs=[SMEM] + [VMEM] * count,
+        out_specs=HBM,
+        scratch_shapes=[pltpu.SemaphoreType.DMA((count,))],
+        compiler_params=PARAMS,
+        cost_estimate=pl.CostEstimate(flops=0, bytes_accessed=1 << 20, transcendentals=0),
+    )(flip, *pieces)
 
 
 def swap(x, axis, mask):
@@ -328,40 +407,42 @@
     along_x = jnp.bitwise_and(wave, 3)
     slot = jnp.right_shift(wave, 2)
     own = 2 * along_x + slot
-    flip = (2 * along_x)[None]
-    where = jnp.stack([own, slot, (sph - 1) * block])
-
+    flip = 2 * along_x
+
+    part, mine = expand(
+        flip[None], own[None], coefficients, positions, wave_grid, vertical, expansion
+    )
+    part = part + swap(part, "sph", 1)
+    r6, r4, r2 = (swap(part, "sph", mask) for mask in (6, 4, 2))
+    uh, ul, qr, th, tl = prepare(
+        positions, wave_grid, vertical, reflection, projector, t_matrix
+    )
+    part = (part + r6) + (r2 + r4)
+    other = swap(part, "sph", 12)
     count = lax.axis_size("sph")
-    own_coefs = lax.dynamic_slice_in_dim(coefficients, own, 1, 0)
-    up = [(i, i + 1) for i in range(count - 1)]
-    down = [(i + 1, i) for i in range(count - 1)]
-    low = lax.ppermute(own_coefs, "sph", up)
-    high = lax.ppermute(own_coefs, "sph", down)
-
-    part = expand(flip, coefficients, positions, wave_grid, vertical, expansion)
-    part = part + swap(part, "sph", 1)
-    part = (part + swap(part, "sph", 6)) + (swap(part, "sph", 2) + swap(part, "sph", 4))
-    other = swap(part, "sph", 12)
-
-    uh, ul, qr = prepare(positions, wave_grid, vertical, reflection, projector)
+    low = lax.ppermute(mine, "sph", [(i, i + 1) for i in range(count - 1)])
+    high = lax.ppermute(mine, "sph", [(i + 1, i) for i in range(count - 1)])
+
+    keep, to1, to2, to3 = project(part, other, qr, uh, ul, 4)
+    got2, got1, got3 = (swap(x, "wave", mask) for x, mask in ((to2, 2), (to1, 1), (to3, 3)))
     translated = translate(
-        where, low, coefficients, high, incident, neighbour_index, link_class, link_count, translation
-    )
-    keep, to1, to2, to3 = project(part, other, qr, uh, ul, 4)
-    got2, got1, got3 = swap(to2, "wave", 2), swap(to1, "wave", 1), swap(to3, "wave", 3)
+        own[None],
+        slot[None],
+        ((sph - 1) * block)[None],
+        low,
+        mine,
+        high,
+        incident,
+        neighbour_index,
+        link_class,
+        link_count,
+        translation,
+    )
     summed = ((keep + translated) + got1) + (got2 + got3)
     across = swap(summed, "wave", 4)
-    updated = apply_types(summed, across, sphere_type, t_matrix)
-    from2, from1, from3 = swap(updated, "wave", 2), swap(updated, "wave", 1), swap(updated, "wave", 3)
-    pieces = (updated, from1, from2, from3)
-
-    def pick(group):
-        near = jnp.where(along_x == group, pieces[0], pieces[1])
-        far = jnp.where(along_x == (group ^ 2), pieces[2], pieces[3])
-        is_near = jnp.right_shift(along_x, 1) == (group >> 1)
-        return jnp.where(is_near, near, far)
-
-    return jnp.concatenate([pick(group) for group in range(4)], axis=0)
+    updated = apply_types(summed, across, sphere_type, th, tl)
+    from2, from1, from3 = (swap(updated, "wave", mask) for mask in (2, 1, 3))
+    return place(flip[None], (updated, from1, from2, from3))
 
 
 def solution(mesh):
@@ -381,6 +462,7 @@
         P(None, None, None, "wave"),
         P(None, None, None, "wave"),
     )
+
     return jax.shard_map(
         per_device, mesh=mesh, in_specs=placed, out_specs=P(None, None, "sph"), check_vma=False
     )

time: 63.1 us -> 52.7 us (0.84)
  the two profiles are of different devices: /device:TPU:1 before, /device:TPU:25 now
where the time goes in v2:
time: 52.7 us; the launch traced here: 52.5 us
  starting transfers between devices  22.5 us (43%)
  waiting for transfers between devices  21.4 us (41%)
  Pallas kernels  8.26 us (16%)
    ppermute x12, waiting for transfers between devices, swap(): lax.ppermute(x, axis, [(i, i ^ mask) for i in range(lax.axis_size(axis))])  17 us
    ppermute x12, starting transfers between devices, swap(): lax.ppermute(x, axis, [(i, i ^ mask) for i in range(lax.axis_size(axis))])  15.5 us
    ppermute x1, starting transfers between devices, per_device(): low = lax.ppermute(mine, 'sph', [(i, i + 1) for i in range(count - 1)])  5.08 us
    ppermute x1, waiting for transfers between devices, per_device(): high = lax.ppermute(mine, 'sph', [(i + 1, i) for i in range(count - 1)])  4.36 us
    pallas_call x1, Pallas kernels, expand(): pl.pallas_call(expand_kernel, name='expand', out_shape=(jax.ShapeDtypeStr...  2.6 us
    pallas_call x1, Pallas kernels, translate(): pl.pallas_call(translate_kernel, name='translate', out_shape=jax.ShapeDty...  2.31 us
    ppermute x1, starting transfers between devices, per_device(): high = lax.ppermute(mine, 'sph', [(i + 1, i) for i in range(count - 1)])  1.92 us
    pallas_call x1, Pallas kernels, project(): pl.pallas_call(project_kernel, name='project', out_shape=(piece,) * piece...  1.27 us
  transfers between devices with their start and end apart: 14, of which 10 were waited for; matrix products, arithmetic and copies ran while one was open for 0% of the time, Pallas kernels for 6%

profile of v2, /device:TPU:25, one launch (start us, length us, event | category | flops | bytes accessed | tf_op | source)
XLA Modules:
  0.0 52.5 jit_solution(1433904259110487478)
XLA Ops:
  0.0 2.6 %expand.1 = (f32[4,8,512]{2,1,0:T(8,128)S(1)}, f32[1,96,128]{2,1,0:T(8,128)S(1)}) custom-call(s32[1]{0:T(128)} %bitcast.flip_ref, s32[1]{0:T(128)} %bitcast.1.own_ref.pick_ref, f32[8,96,128]{2,1,0:T(8,128)} %coef_hbm.1, f32[3,128]{1,0:T(4,128)} %pos_ref.1, s32[2,512]{1,0:T(2,128)} %grid_ref.1, f32[512]{0:T(512)} %vert_ref.1, f32[2,2,48,512]{3,2,1,0:T(8,128)} %exp_hbm.1), custom_call_target="tpu_custom_call" | custom-call | flops 603979776 | bytes 4194304 | tf_op jit(solution)/shard_map/expand/pallas_call | solution.py:136
  2.6 0.8 %collective-permute-start = (f32[4,8,512]{2,1,0:T(8,128)S(1)}, f32[4,8,512]{2,1,0:T(8,128)S(1)}, u32[]{:S(2)}, u32[]{:S(2)}) collective-permute-start(f32[4,8,512]{2,1,0:T(8,128)S(1)} %get-tuple-element.16), channel_id=1, source_target_pairs={{0,8},{8,0},{16,24},{24,16},{32,40},{40,32},{48,56},{56,48},{64,72... | collective-permute-start | bytes 196616 | tf_op jit(solution)/shard_map/ppermute | solution.py:385
  3.4 0.9 %collective-permute-done = f32[4,8,512]{2,1,0:T(8,128)S(1)} collective-permute-done((f32[4,8,512]{2,1,0:T(8,128)S(1)}, f32[4,8,512]{2,1,0:T(8,128)S(1)}, u32[]{:S(2)}, u32[]{:S(2)}) %collective-permute-start) | collective-permute-done | bytes 65568 | tf_op jit(solution)/shard_map/ppermute | solution.py:385
  4.3 1.9 %collective-permute-start.1 = (f32[4,8,512]{2,1,0:T(8,128)S(1)}, f32[4,8,512]{2,1,0:T(8,128)S(1)}, u32[]{:S(2)}, u32[]{:S(2)}) collective-permute-start(f32[4,8,512]{2,1,0:T(8,128)S(1)} %add.29), channel_id=1, source_target_pairs={{0,48},{8,56},{16,32},{24,40},{32,16},{40,24},{48,0},{56,8},{64,11... | collective-permute-start | bytes 196616 | tf_op jit(solution)/shard_map/ppermute | solution.py:385
  6.2 1.0 %collective-permute-start.2 = (f32[4,8,512]{2,1,0:T(8,128)S(1)}, f32[4,8,512]{2,1,0:T(8,128)S(1)}, u32[]{:S(2)}, u32[]{:S(2)}) collective-permute-start(f32[4,8,512]{2,1,0:T(8,128)S(1)} %add.29), channel_id=1, source_target_pairs={{0,16},{8,24},{16,0},{24,8},{32,48},{40,56},{48,32},{56,40},{64,80... | collective-permute-start | bytes 196616 | tf_op jit(solution)/shard_map/ppermute | solution.py:385
  7.2 1.2 %collective-permute-done.1 = f32[4,8,512]{2,1,0:T(8,128)S(1)} collective-permute-done((f32[4,8,512]{2,1,0:T(8,128)S(1)}, f32[4,8,512]{2,1,0:T(8,128)S(1)}, u32[]{:S(2)}, u32[]{:S(2)}) %collective-permute-start.1) | collective-permute-done | bytes 65568 | tf_op jit(solution)/shard_map/ppermute | solution.py:385
  8.4 1.7 %collective-permute-done.2 = f32[4,8,512]{2,1,0:T(8,128)S(1)} collective-permute-done((f32[4,8,512]{2,1,0:T(8,128)S(1)}, f32[4,8,512]{2,1,0:T(8,128)S(1)}, u32[]{:S(2)}, u32[]{:S(2)}) %collective-permute-start.2) | collective-permute-done | bytes 65568 | tf_op jit(solution)/shard_map/ppermute | solution.py:385
  10.2 0.6 %collective-permute-done.3 = f32[4,8,512]{2,1,0:T(8,128)S(1)} collective-permute-done((f32[4,8,512]{2,1,0:T(8,128)S(1)}, f32[4,8,512]{2,1,0:T(8,128)S(1)}, u32[]{:S(2)}, u32[]{:S(2)}) %collective-permute-start.3) | collective-permute-done | bytes 65568 | tf_op jit(solution)/shard_map/ppermute | solution.py:385
  10.8 3.3 %collective-permute-start.4 = (f32[4,8,512]{2,1,0:T(8,128)S(1)}, f32[4,8,512]{2,1,0:T(8,128)S(1)}, u32[]{:S(2)}, u32[]{:S(2)}) collective-permute-start(f32[4,8,512]{2,1,0:T(8,128)S(1)} %add_add_fusion.1.mine_ref), channel_id=1, source_target_pairs={{0,96},{8,104},{16,112},{24,120},{32,64},{40,72},{48,80},{56,88},{... | collective-permute-start | bytes 196616 | tf_op jit(solution)/shard_map/ppermute | solution.py:385
  14.1 1.1 %prepare.1 = (bf16[1024,256]{1,0:T(8,128)(2,1)S(1)}, bf16[1024,256]{1,0:T(8,128)(2,1)S(1)}, f32[4,48,512]{2,1,0:T(8,128)S(1)}, bf16[96,192]{1,0:T(8,128)(2,1)S(1)}, bf16[96,192]{1,0:T(8,128)(2,1)S(1)}) custom-call(f32[3,128]{1,0:T(4,128)S(1)} %copy-done.8, s32[2,512]{1,0:T(2,128)S(1)} %copy-done.7, f32[512]{0:T(512)S(1)} %copy-done.9, ...), custom_call_target="tpu_custom_call" | custom-call | flops 2097152 | bytes 2097152 | tf_op jit(solution)/shard_map/prepare/pallas_call | solution.py:198
  15.2 0.0 copy-start
  15.2 0.0 copy-start.6
  15.2 0.0 copy-start.10
  15.2 0.5 collective-permute-done.4.other_ref
  15.7 1.3 %project.1 = (f32[2,96,128]{2,1,0:T(8,128)S(1)}, f32[2,96,128]{2,1,0:T(8,128)S(1)}, f32[2,96,128]{2,1,0:T(8,128)S(1)}, f32[2,96,128]{2,1,0:T(8,128)S(1)}) custom-call(f32[4,8,512]{2,1,0:T(8,128)S(1)} %add_add_fusion.1.mine_ref, f32[4,8,512]{2,1,0:T(8,128)S(1)} %collective-permute-done.4.other_ref, f32[4,48,512]{2,1,0:T(8,128)S(1)} %get-tuple-element.17.qr_ref, ...), custom_call_target="tpu_custom_call" | custom-call | flops 603979776 | bytes 3145728 | tf_op jit(solution)/shard_map/project/pallas_call | solution.py:242
  17.0 1.3 %collective-permute-start.7 = (f32[2,96,128]{2,1,0:T(8,128)S(1)}, f32[2,96,128]{2,1,0:T(8,128)S(1)}, u32[]{:S(2)}, u32[]{:S(2)}) collective-permute-start(f32[2,96,128]{2,1,0:T(8,128)S(1)} %get-tuple-element.22), channel_id=1, source_target_pairs={{0,1},{1,0},{2,3},{3,2},{4,5},{5,4},{6,7},{7,6},{8,9},{9,8},{10,11... | collective-permute-start | bytes 294920 | tf_op jit(solution)/shard_map/ppermute | solution.py:385
  18.3 2.5 %collective-permute-start.8 = (f32[2,96,128]{2,1,0:T(8,128)S(1)}, f32[2,96,128]{2,1,0:T(8,128)S(1)}, u32[]{:S(2)}, u32[]{:S(2)}) collective-permute-start(f32[2,96,128]{2,1,0:T(8,128)S(1)} %get-tuple-element.23), channel_id=1, source_target_pairs={{0,2},{1,3},{2,0},{3,1},{4,6},{5,7},{6,4},{7,5},{8,10},{9,11},{10,... | collective-permute-start | bytes 294920 | tf_op jit(solution)/shard_map/ppermute | solution.py:385
  20.8 0.2 collective-permute-start.9
  21.0 5.1 %collective-permute-start.5 = (f32[1,96,128]{2,1,0:T(8,128)S(1)}, f32[1,96,128]{2,1,0:T(8,128)S(1)}, u32[]{:S(2)}, u32[]{:S(2)}) collective-permute-start(f32[1,96,128]{2,1,0:T(8,128)S(1)} %get-tuple-element.21.own_ref), channel_id=1, source_target_pairs={{0,8},{8,16},{16,24},{24,32},{32,40},{40,48},{48,56},{56,64},{64,7... | collective-permute-start | bytes 147464 | tf_op jit(solution)/shard_map/ppermute | solution.py:423
  26.0 1.9 %collective-permute-start.6 = (f32[1,96,128]{2,1,0:T(8,128)S(1)}, f32[1,96,128]{2,1,0:T(8,128)S(1)}, u32[]{:S(2)}, u32[]{:S(2)}) collective-permute-start(f32[1,96,128]{2,1,0:T(8,128)S(1)} %get-tuple-element.21.own_ref), channel_id=1, source_target_pairs={{8,0},{16,8},{24,16},{32,24},{40,32},{48,40},{56,48},{64,56},{72,6... | collective-permute-start | bytes 147464 | tf_op jit(solution)/shard_map/ppermute | solution.py:424
  28.0 4.4 %collective-permute-done.6.high_ref = f32[1,96,128]{2,1,0:T(8,128)S(1)} collective-permute-done((f32[1,96,128]{2,1,0:T(8,128)S(1)}, f32[1,96,128]{2,1,0:T(8,128)S(1)}, u32[]{:S(2)}, u32[]{:S(2)}) %collective-permute-start.6) | collective-permute-done | bytes 49184 | tf_op jit(solution)/shard_map/ppermute | solution.py:424
  32.4 2.3 %translate.1 = f32[2,96,128]{2,1,0:T(8,128)S(1)} custom-call(s32[1]{0:T(128)} %bitcast.1.own_ref.pick_ref, s32[1]{0:T(128)} %bitcast.2.slot_ref, s32[1]{0:T(128)} %bitcast.3.base_ref, f32[1,96,128]{2,1,0:T(8,128)S(1)} %collective-permute-done.5.low_ref, f32[1,96,128]{2,1,0:T(8,128)S(1)} %get-tuple-element.21.own_ref, ...), custom_call_target="tpu_custom_call" | custom-call | flops 184025088 | bytes 2097152 | tf_op jit(solution)/shard_map/translate/pallas_call | solution.py:303
  34.8 0.7 %collective-permute-start.10 = (f32[2,96,128]{2,1,0:T(8,128)S(1)}, f32[2,96,128]{2,1,0:T(8,128)S(1)}, u32[]{:S(2)}, u32[]{:S(2)}) collective-permute-start(f32[2,96,128]{2,1,0:T(8,128)S(1)} %add_add_fusion.mine_ref), channel_id=1, source_target_pairs={{0,4},{1,5},{2,6},{3,7},{4,0},{5,1},{6,2},{7,3},{8,12},{9,13},{10,... | collective-permute-start | bytes 294920 | tf_op jit(solution)/shard_map/ppermute | solution.py:385
  35.5 4.8 %collective-permute-done.10.other_ref = f32[2,96,128]{2,1,0:T(8,128)S(1)} collective-permute-done((f32[2,96,128]{2,1,0:T(8,128)S(1)}, f32[2,96,128]{2,1,0:T(8,128)S(1)}, u32[]{:S(2)}, u32[]{:S(2)}) %collective-permute-start.10) | collective-permute-done | bytes 98336 | tf_op jit(solution)/shard_map/ppermute | solution.py:385
  40.3 0.3 types.1.refs_0_
  40.6 0.1 collective-permute-start.11
  40.7 3.6 %collective-permute-start.12 = (f32[2,96,128]{2,1,0:T(8,128)S(1)}, f32[2,96,128]{2,1,0:T(8,128)S(1)}, u32[]{:S(2)}, u32[]{:S(2)}) collective-permute-start(f32[2,96,128]{2,1,0:T(8,128)S(1)} %types.1.refs_0_), channel_id=1, source_target_pairs={{0,2},{1,3},{2,0},{3,1},{4,6},{5,7},{6,4},{7,5},{8,10},{9,11},{10,... | collective-permute-start | bytes 294920 | tf_op jit(solution)/shard_map/ppermute | solution.py:385
  44.3 0.2 collective-permute-start.13
  44.5 0.4 collective-permute-done.11.refs_1_
  44.9 4.3 %collective-permute-done.12.refs_2_ = f32[2,96,128]{2,1,0:T(8,128)S(1)} collective-permute-done((f32[2,96,128]{2,1,0:T(8,128)S(1)}, f32[2,96,128]{2,1,0:T(8,128)S(1)}, u32[]{:S(2)}, u32[]{:S(2)}) %collective-permute-start.12) | collective-permute-done | bytes 98336 | tf_op jit(solution)/shard_map/ppermute | solution.py:385
  49.2 2.6 %collective-permute-done.13.refs_3_ = f32[2,96,128]{2,1,0:T(8,128)S(1)} collective-permute-done((f32[2,96,128]{2,1,0:T(8,128)S(1)}, f32[2,96,128]{2,1,0:T(8,128)S(1)}, u32[]{:S(2)}, u32[]{:S(2)}) %collective-permute-start.13) | collective-permute-done | bytes 98336 | tf_op jit(solution)/shard_map/ppermute | solution.py:385
  51.8 0.8 %place.1 = f32[8,96,128]{2,1,0:T(8,128)} custom-call(s32[1]{0:T(128)} %bitcast.flip_ref, f32[2,96,128]{2,1,0:T(8,128)S(1)} %types.1.refs_0_, f32[2,96,128]{2,1,0:T(8,128)S(1)} %collective-permute-done.11.refs_1_, f32[2,96,128]{2,1,0:T(8,128)S(1)} %collective-permute-done.12.refs_2_, f32[2,96,128]{2,1,0:T(8,128)S(1)} %collective-permute-done.13.refs_3_), custom_call_target="tpu_custom_call" | custom-call | bytes 1048576 | tf_op jit(solution)/shard_map/place/pallas_call | solution.py:372
  (29 shorter events, 0.1 us)
Async XLA Ops:
  0.0 14.1 %copy-start.1 = (f32[2,48,2,512]{3,2,1,0:T(2,128)S(1)}, f32[2,48,2,512]{3,2,1,0:T(2,128)}, u32[]{:S(2)}) copy-start(f32[2,48,2,512]{3,2,1,0:T(2,128)} %proj_ref.1) | copy-start | bytes 1179652
  0.0 14.1 %copy-start.3 = (f32[2,4,48,48]{3,2,1,0:T(8,128)S(1)}, f32[2,4,48,48]{3,2,1,0:T(8,128)}, u32[]{:S(2)}) copy-start(f32[2,4,48,48]{3,2,1,0:T(8,128)} %tmat_ref.1) | copy-start | bytes 221188
  0.0 14.1 %copy-start.4 = (f32[2,2,2,512]{3,2,1,0:T(2,128)S(1)}, f32[2,2,2,512]{3,2,1,0:T(2,128)}, u32[]{:S(2)}) copy-start(f32[2,2,2,512]{3,2,1,0:T(2,128)} %refl_ref.1) | copy-start | bytes 49156
  0.0 14.1 %copy-start.7 = (s32[2,512]{1,0:T(2,128)S(1)}, s32[2,512]{1,0:T(2,128)}, u32[]{:S(2)}) copy-start(s32[2,512]{1,0:T(2,128)} %grid_ref.1) | copy-start | bytes 12292
  0.0 14.1 %copy-start.8 = (f32[3,128]{1,0:T(4,128)S(1)}, f32[3,128]{1,0:T(4,128)}, u32[]{:S(2)}) copy-start(f32[3,128]{1,0:T(4,128)} %pos_ref.1) | copy-start | bytes 4612
  0.0 14.1 %copy-start.9 = (f32[512]{0:T(512)S(1)}, f32[512]{0:T(512)}, u32[]{:S(2)}) copy-start(f32[512]{0:T(512)} %vert_ref.1) | copy-start | bytes 6148
  2.6 1.7 %collective-permute-start = (f32[4,8,512]{2,1,0:T(8,128)S(1)}, f32[4,8,512]{2,1,0:T(8,128)S(1)}, u32[]{:S(2)}, u32[]{:S(2)}) collective-permute-start(f32[4,8,512]{2,1,0:T(8,128)S(1)} %get-tuple-element.16), channel_id=1, source_target_pairs={{0,8},{8,0},{16,24},{24,16},{32,40},{40,32},{48,56},{56,48},{64,72... | collective-permute-start | bytes 196616 | tf_op jit(solution)/shard_map/ppermute | solution.py:385
  4.3 4.1 %collective-permute-start.1 = (f32[4,8,512]{2,1,0:T(8,128)S(1)}, f32[4,8,512]{2,1,0:T(8,128)S(1)}, u32[]{:S(2)}, u32[]{:S(2)}) collective-permute-start(f32[4,8,512]{2,1,0:T(8,128)S(1)} %add.29), channel_id=1, source_target_pairs={{0,48},{8,56},{16,32},{24,40},{32,16},{40,24},{48,0},{56,8},{64,11... | collective-permute-start | bytes 196616 | tf_op jit(solution)/shard_map/ppermute | solution.py:385
  6.2 3.9 %collective-permute-start.2 = (f32[4,8,512]{2,1,0:T(8,128)S(1)}, f32[4,8,512]{2,1,0:T(8,128)S(1)}, u32[]{:S(2)}, u32[]{:S(2)}) collective-permute-start(f32[4,8,512]{2,1,0:T(8,128)S(1)} %add.29), channel_id=1, source_target_pairs={{0,16},{8,24},{16,0},{24,8},{32,48},{40,56},{48,32},{56,40},{64,80... | collective-permute-start | bytes 196616 | tf_op jit(solution)/shard_map/ppermute | solution.py:385
  7.2 3.6 %collective-permute-start.3 = (f32[4,8,512]{2,1,0:T(8,128)S(1)}, f32[4,8,512]{2,1,0:T(8,128)S(1)}, u32[]{:S(2)}, u32[]{:S(2)}) collective-permute-start(f32[4,8,512]{2,1,0:T(8,128)S(1)} %add.29), channel_id=1, source_target_pairs={{0,32},{8,40},{16,48},{24,56},{32,0},{40,8},{48,16},{56,24},{64,96... | collective-permute-start | bytes 196616 | tf_op jit(solution)/shard_map/ppermute | solution.py:385
  10.8 4.9 %collective-permute-start.4 = (f32[4,8,512]{2,1,0:T(8,128)S(1)}, f32[4,8,512]{2,1,0:T(8,128)S(1)}, u32[]{:S(2)}, u32[]{:S(2)}) collective-permute-start(f32[4,8,512]{2,1,0:T(8,128)S(1)} %add_add_fusion.1.mine_ref), channel_id=1, source_target_pairs={{0,96},{8,104},{16,112},{24,120},{32,64},{40,72},{48,80},{56,88},{... | collective-permute-start | bytes 196616 | tf_op jit(solution)/shard_map/ppermute | solution.py:385
  15.2 17.2 %copy-start = (f32[2,26,48,48]{3,2,1,0:T(8,128)S(1)}, f32[2,26,48,48]{3,2,1,0:T(8,128)}, u32[]{:S(2)}) copy-start(f32[2,26,48,48]{3,2,1,0:T(8,128)} %trans_ref.1) | copy-start | bytes 1437700
  15.2 17.2 %copy-start.2 = (f32[8,96,128]{2,1,0:T(8,128)S(1)}, f32[8,96,128]{2,1,0:T(8,128)}, u32[]{:S(2)}) copy-start(f32[8,96,128]{2,1,0:T(8,128)} %inc_ref.1) | copy-start | bytes 1179652
  15.2 17.2 %copy-start.5 = (s32[12,128]{1,0:T(8,128)S(1)}, s32[12,128]{1,0:T(8,128)}, u32[]{:S(2)}) copy-start(s32[12,128]{1,0:T(8,128)} %idx_ref.1) | copy-start | bytes 18436
  15.2 17.2 %copy-start.6 = (s32[12,128]{1,0:T(8,128)S(1)}, s32[12,128]{1,0:T(8,128)}, u32[]{:S(2)}) copy-start(s32[12,128]{1,0:T(8,128)} %class_ref.1) | copy-start | bytes 18436
  15.2 17.2 %copy-start.10 = (s32[128]{0:T(128)S(1)}, s32[128]{0:T(128)}, u32[]{:S(2)}) copy-start(s32[128]{0:T(128)} %count_ref.1) | copy-start | bytes 1540
  17.0 23.3 %copy-start.11 = (s32[128]{0:T(128)S(1)}, s32[128]{0:T(128)}, u32[]{:S(2)}) copy-start(s32[128]{0:T(128)} %type_ref.1) | copy-start | bytes 1540
  17.0 17.7 %collective-permute-start.7 = (f32[2,96,128]{2,1,0:T(8,128)S(1)}, f32[2,96,128]{2,1,0:T(8,128)S(1)}, u32[]{:S(2)}, u32[]{:S(2)}) collective-permute-start(f32[2,96,128]{2,1,0:T(8,128)S(1)} %get-tuple-element.22), channel_id=1, source_target_pairs={{0,1},{1,0},{2,3},{3,2},{4,5},{5,4},{6,7},{7,6},{8,9},{9,8},{10,11... | collective-permute-start | bytes 294920 | tf_op jit(solution)/shard_map/ppermute | solution.py:385
  18.3 16.4 %collective-permute-start.8 = (f32[2,96,128]{2,1,0:T(8,128)S(1)}, f32[2,96,128]{2,1,0:T(8,128)S(1)}, u32[]{:S(2)}, u32[]{:S(2)}) collective-permute-start(f32[2,96,128]{2,1,0:T(8,128)S(1)} %get-tuple-element.23), channel_id=1, source_target_pairs={{0,2},{1,3},{2,0},{3,1},{4,6},{5,7},{6,4},{7,5},{8,10},{9,11},{10,... | collective-permute-start | bytes 294920 | tf_op jit(solution)/shard_map/ppermute | solution.py:385
  20.8 14.0 %collective-permute-start.9 = (f32[2,96,128]{2,1,0:T(8,128)S(1)}, f32[2,96,128]{2,1,0:T(8,128)S(1)}, u32[]{:S(2)}, u32[]{:S(2)}) collective-permute-start(f32[2,96,128]{2,1,0:T(8,128)S(1)} %get-tuple-element.24), channel_id=1, source_target_pairs={{0,3},{1,2},{2,1},{3,0},{4,7},{5,6},{6,5},{7,4},{8,11},{9,10},{10,... | collective-permute-start | bytes 294920 | tf_op jit(solution)/shard_map/ppermute | solution.py:385
  21.0 7.0 %collective-permute-start.5 = (f32[1,96,128]{2,1,0:T(8,128)S(1)}, f32[1,96,128]{2,1,0:T(8,128)S(1)}, u32[]{:S(2)}, u32[]{:S(2)}) collective-permute-start(f32[1,96,128]{2,1,0:T(8,128)S(1)} %get-tuple-element.21.own_ref), channel_id=1, source_target_pairs={{0,8},{8,16},{16,24},{24,32},{32,40},{40,48},{48,56},{56,64},{64,7... | collective-permute-start | bytes 147464 | tf_op jit(solution)/shard_map/ppermute | solution.py:423
  26.0 6.3 %collective-permute-start.6 = (f32[1,96,128]{2,1,0:T(8,128)S(1)}, f32[1,96,128]{2,1,0:T(8,128)S(1)}, u32[]{:S(2)}, u32[]{:S(2)}) collective-permute-start(f32[1,96,128]{2,1,0:T(8,128)S(1)} %get-tuple-element.21.own_ref), channel_id=1, source_target_pairs={{8,0},{16,8},{24,16},{32,24},{40,32},{48,40},{56,48},{64,56},{72,6... | collective-permute-start | bytes 147464 | tf_op jit(solution)/shard_map/ppermute | solution.py:424
  34.8 5.5 %collective-permute-start.10 = (f32[2,96,128]{2,1,0:T(8,128)S(1)}, f32[2,96,128]{2,1,0:T(8,128)S(1)}, u32[]{:S(2)}, u32[]{:S(2)}) collective-permute-start(f32[2,96,128]{2,1,0:T(8,128)S(1)} %add_add_fusion.mine_ref), channel_id=1, source_target_pairs={{0,4},{1,5},{2,6},{3,7},{4,0},{5,1},{6,2},{7,3},{8,12},{9,13},{10,... | collective-permute-start | bytes 294920 | tf_op jit(solution)/shard_map/ppermute | solution.py:385
  40.6 4.3 %collective-permute-start.11 = (f32[2,96,128]{2,1,0:T(8,128)S(1)}, f32[2,96,128]{2,1,0:T(8,128)S(1)}, u32[]{:S(2)}, u32[]{:S(2)}) collective-permute-start(f32[2,96,128]{2,1,0:T(8,128)S(1)} %types.1.refs_0_), channel_id=1, source_target_pairs={{0,1},{1,0},{2,3},{3,2},{4,5},{5,4},{6,7},{7,6},{8,9},{9,8},{10,11... | collective-permute-start | bytes 294920 | tf_op jit(solution)/shard_map/ppermute | solution.py:385
  40.7 8.5 %collective-permute-start.12 = (f32[2,96,128]{2,1,0:T(8,128)S(1)}, f32[2,96,128]{2,1,0:T(8,128)S(1)}, u32[]{:S(2)}, u32[]{:S(2)}) collective-permute-start(f32[2,96,128]{2,1,0:T(8,128)S(1)} %types.1.refs_0_), channel_id=1, source_target_pairs={{0,2},{1,3},{2,0},{3,1},{4,6},{5,7},{6,4},{7,5},{8,10},{9,11},{10,... | collective-permute-start | bytes 294920 | tf_op jit(solution)/shard_map/ppermute | solution.py:385
  44.3 7.4 %collective-permute-start.13 = (f32[2,96,128]{2,1,0:T(8,128)S(1)}, f32[2,96,128]{2,1,0:T(8,128)S(1)}, u32[]{:S(2)}, u32[]{:S(2)}) collective-permute-start(f32[2,96,128]{2,1,0:T(8,128)S(1)} %types.1.refs_0_), channel_id=1, source_target_pairs={{0,3},{1,2},{2,1},{3,0},{4,7},{5,6},{6,5},{7,4},{8,11},{9,10},{10,... | collective-permute-start | bytes 294920 | tf_op jit(solution)/shard_map/ppermute | solution.py:385

commit v3 on v2

--- a/solution.py
+++ b/solution.py
@@ -75,21 +75,20 @@
     spec,
     sems,
 ):
+    illums = coef_ref.shape[0]
+    flip = flip_ref[0]
+    pairs = [(pos_hbm, pos_ref), (grid_hbm, grid_ref), (vert_hbm, vert_ref)]
+    for b in range(illums):
+        at = jnp.bitwise_xor(flip, b)
+        pairs.append((coef_hbm.at[at], coef_ref.at[b]))
+    for p in range(2):
+        for i in range(2):
+            pairs.append((exp_hbm.at[i, p], exp_ref.at[i, p]))
     copies = [
-        pltpu.make_async_copy(source, target, sems.at[i])
-        for i, (source, target) in enumerate(
-            (
-                (pos_hbm, pos_ref),
-                (grid_hbm, grid_ref),
-                (vert_hbm, vert_ref),
-                (coef_hbm, coef_ref),
-                (exp_hbm, exp_ref),
-            )
-        )
+        pltpu.make_async_copy(source, target, sems.at[i]) for i, (source, target) in enumerate(pairs)
     ]
     for copy in copies:
         copy.start()
-    illums = coef_ref.shape[0]
     waves = grid_ref.shape[1]
     half = illums * MODES
     for copy in copies[:3]:
@@ -100,10 +99,16 @@
     turns = pos[:, 0:1] * grid[0:1] + pos[:, 1:2] * grid[1:2] - pos[:, 2:3] * vert
     cos, sin = cos_sin_turns(turns)
     bh, bl = split(jnp.concatenate([cos, sin], axis=0))
-    copies[3].wait()
-    mine_ref[0] = coef_ref[own_ref[0]]
+    for copy in copies[3 : 3 + illums]:
+        copy.wait()
+    mine = coef_ref[jnp.bitwise_xor(flip, own_ref[0])]
+    mine_ref[0] = mine
+    depth = mine.shape[0] * mine.shape[1] // waves
+    for i in range(waves // mine.shape[1]):
+        lanes = slice(i * mine.shape[1], (i + 1) * mine.shape[1])
+        out_ref[4 * illums :, lanes] = mine[i * depth : (i + 1) * depth]
     for b in range(illums):
-        block = coef_ref[jnp.bitwise_xor(flip_ref[0], b)]
+        block = coef_ref[b]
         re, im = block[:MODES], block[MODES:]
         for base, left, right in ((0, re, im), (half, im, -re)):
             rows = pl.ds(base + b * MODES, MODES)
@@ -111,7 +116,8 @@
                 hi, lo = split(part)
                 ah[rows, offset : offset + 128] = hi
                 al[rows, offset : offset + 128] = lo
-    copies[4].wait()
+    for copy in copies[3 + illums :]:
+        copy.wait()
     width = 256
     for start in range(0, waves, width):
         lanes = slice(start, start + width)
@@ -124,8 +130,9 @@
                 si = spec[half + b * MODES : half + (b + 1) * MODES, :]
                 out_re.append(jnp.sum(er * sr - ei * si, axis=0, keepdims=True))
                 out_im.append(jnp.sum(er * si + ei * sr, axis=0, keepdims=True))
-            out_ref[2 * p, :, lanes] = jnp.concatenate(out_re, axis=0)
-            out_ref[2 * p + 1, :, lanes] = jnp.concatenate(out_im, axis=0)
+            top = 2 * p * illums
+            out_ref[top : top + illums, lanes] = jnp.concatenate(out_re, axis=0)
+            out_ref[top + illums : top + 2 * illums, lanes] = jnp.concatenate(out_im, axis=0)
 
 
 def expand(flip, own, coefficients, positions, wave_grid, vertical, expansion):
@@ -137,7 +144,7 @@
         expand_kernel,
         name="expand",
         out_shape=(
-            jax.ShapeDtypeStruct((4, illums, waves), F32),
+            jax.ShapeDtypeStruct((4 * illums + 2 * MODES * spheres // waves, waves), F32),
             jax.ShapeDtypeStruct((1, 2 * MODES, spheres), F32),
         ),
         in_specs=[SMEM] * 2 + [HBM] * 5,
@@ -147,7 +154,7 @@
             pltpu.VMEM((rows, 2 * spheres), BF16),
             pltpu.VMEM((rows, 2 * spheres), BF16),
             pltpu.VMEM((rows, 256), F32),
-            pltpu.SemaphoreType.DMA((5,)),
+            pltpu.SemaphoreType.DMA((7 + illums,)),
         ],
         compiler_params=PARAMS,
         cost_estimate=pl.CostEstimate(
@@ -256,7 +263,7 @@
 
 
 def translate_kernel(
-    pick_ref, slot_ref, base_ref, low_ref, own_ref, high_ref, inc_ref, idx_ref, class_ref, count_ref, trans_ref, out_ref, bh, bl, gh, gl
+    pick_ref, slot_ref, base_ref, odd_ref, near_ref, own_ref, far_ref, inc_ref, idx_ref, class_ref, count_ref, trans_ref, out_ref, bh, bl, gh, gl
 ):
     own = pick_ref[0]
     slot = slot_ref[0]
@@ -267,8 +274,16 @@
     lane = jnp.bitwise_and(local, 127)
     live = lax.broadcasted_iota(jnp.int32, local.shape, 0) < count_ref[...].reshape(1, spheres)
     kind = jnp.where(live, class_ref[...], OFFSETS)
-    source = (low_ref[0], own_ref[0], high_ref[0])
     shape = (2 * MODES, spheres)
+    blocks = near_ref.shape[1] // spheres
+    depth = shape[0] // blocks
+    rows = slice(near_ref.shape[0] - depth, near_ref.shape[0])
+    near = jnp.concatenate(
+        [near_ref[rows, i * spheres : (i + 1) * spheres] for i in range(blocks)], axis=0
+    )
+    far = far_ref[0]
+    odd = odd_ref[0] == 1
+    source = (jnp.where(odd, near, far), own_ref[0], jnp.where(odd, far, near))
     picked = []
     for k in range(LINKS):
         at = jnp.broadcast_to(lane[k : k + 1, :], shape)
@@ -298,13 +313,13 @@
     out_ref[1] = jnp.where(slot == 0, 0.0, result)
 
 
-def translate(own, slot, base, low, mine, high, incident, index, link_class, link_count, translation):
+def translate(own, slot, base, odd, near, mine, far, incident, index, link_class, link_count, translation):
     spheres = index.shape[1]
     return pl.pallas_call(
         translate_kernel,
         name="translate",
         out_shape=jax.ShapeDtypeStruct((2, 2 * MODES, spheres), F32),
-        in_specs=[SMEM] * 3 + [VMEM] * 8,
+        in_specs=[SMEM] * 4 + [VMEM] * 8,
         out_specs=VMEM,
         scratch_shapes=[
             pltpu.VMEM((OFFSETS * MODES, 2 * spheres), BF16),
@@ -318,7 +333,7 @@
             bytes_accessed=2 << 20,
             transcendentals=0,
         ),
-    )(own, slot, base, low, mine, high, incident, index, link_class, link_count, translation)
+    )(own, slot, base, odd, near, mine, far, incident, index, link_class, link_count, translation)
 
 
 def types_kernel(mine_ref, other_ref, type_ref, th, tl, out_ref):
@@ -409,19 +424,21 @@
     own = 2 * along_x + slot
     flip = 2 * along_x
 
-    part, mine = expand(
+    wide, mine = expand(
         flip[None], own[None], coefficients, positions, wave_grid, vertical, expansion
     )
-    part = part + swap(part, "sph", 1)
+    near = swap(wide, "sph", 1)
+    rows = 4 * coefficients.shape[0]
+    part = (wide[:rows] + near[:rows]).reshape(4, -1, wide.shape[1])
     r6, r4, r2 = (swap(part, "sph", mask) for mask in (6, 4, 2))
     uh, ul, qr, th, tl = prepare(
         positions, wave_grid, vertical, reflection, projector, t_matrix
     )
     part = (part + r6) + (r2 + r4)
     other = swap(part, "sph", 12)
-    count = lax.axis_size("sph")
-    low = lax.ppermute(mine, "sph", [(i, i + 1) for i in range(count - 1)])
-    high = lax.ppermute(mine, "sph", [(i + 1, i) for i in range(count - 1)])
+    size = lax.axis_size("sph")
+    links = [(i, (i + 1) % size) for i in range(1, size, 2)]
+    far = lax.ppermute(mine, "sph", links + [(j, i) for i, j in links])
 
     keep, to1, to2, to3 = project(part, other, qr, uh, ul, 4)
     got2, got1, got3 = (swap(x, "wave", mask) for x, mask in ((to2, 2), (to1, 1), (to3, 3)))
@@ -429,9 +446,10 @@
         own[None],
         slot[None],
         ((sph - 1) * block)[None],
-        low,
+        jnp.bitwise_and(sph, 1)[None],
+        near,
         mine,
-        high,
+        far,
         incident,
         neighbour_index,
         link_class,

time: 52.7 us -> 49 us (0.930)
  the two profiles are of different devices: /device:TPU:25 before, /device:TPU:0 now
where the time goes in v3:
time: 49 us; the launch traced here: 48.9 us
  waiting for transfers between devices  21.9 us (45%)
  starting transfers between devices  18.3 us (37%)
  Pallas kernels  8.36 us (17%)
    ppermute x12, starting transfers between devices, swap(): lax.ppermute(x, axis, [(i, i ^ mask) for i in range(lax.axis_size(axis))])  18.3 us
    ppermute x12, waiting for transfers between devices, swap(): lax.ppermute(x, axis, [(i, i ^ mask) for i in range(lax.axis_size(axis))])  16.3 us
    ppermute x1, waiting for transfers between devices, per_device(): far = lax.ppermute(mine, 'sph', links + [(j, i) for i, j in links])  5.62 us
    pallas_call x1, Pallas kernels, expand(): pl.pallas_call(expand_kernel, name='expand', out_shape=(jax.ShapeDtypeStr...  2.71 us
    pallas_call x1, Pallas kernels, translate(): pl.pallas_call(translate_kernel, name='translate', out_shape=jax.ShapeDty...  2.3 us
    pallas_call x1, Pallas kernels, project(): pl.pallas_call(project_kernel, name='project', out_shape=(piece,) * piece...  1.27 us
    pallas_call x1, Pallas kernels, prepare(): pl.pallas_call(prepare_kernel, name='prepare', out_shape=(tiles, tiles, j...  1.06 us
  transfers between devices with their start and end apart: 13, of which 9 were waited for; matrix products, arithmetic and copies ran while one was open for 0% of the time, Pallas kernels for 7%

profile of v3, /device:TPU:0, one launch (start us, length us, event | category | flops | bytes accessed | tf_op | source)
XLA Modules:
  0.0 48.9 jit_solution(10425528497332897100)
XLA Ops:
  0.0 2.7 %expand.1 = (f32[56,512]{1,0:T(8,128)S(1)}, f32[1,96,128]{2,1,0:T(8,128)S(1)}) custom-call(s32[1]{0:T(128)} %bitcast.flip_ref, s32[1]{0:T(128)} %bitcast.1.own_ref.pick_ref, f32[8,96,128]{2,1,0:T(8,128)} %coef_hbm.1, f32[3,128]{1,0:T(4,128)} %pos_ref.1, s32[2,512]{1,0:T(2,128)} %grid_ref.1, f32[512]{0:T(512)} %vert_ref.1, f32[2,2,48,512]{3,2,1,0:T(8,128)} %exp_hbm.1), custom_call_target="tpu_custom_call" | custom-call | flops 603979776 | bytes 4194304 | tf_op jit(solution)/shard_map/expand/pallas_call | solution.py:143
  2.7 0.1 collective-permute-start
  2.8 1.3 %collective-permute-done.near_ref = f32[56,512]{1,0:T(8,128)S(1)} collective-permute-done((f32[56,512]{1,0:T(8,128)S(1)}, f32[56,512]{1,0:T(8,128)S(1)}, u32[]{:S(2)}, u32[]{:S(2)}) %collective-permute-start) | collective-permute-done | bytes 114720 | tf_op jit(solution)/shard_map/ppermute | solution.py:400
  4.2 1.8 %collective-permute-start.2 = (f32[4,8,512]{2,1,0:T(8,128)S(1)}, f32[4,8,512]{2,1,0:T(8,128)S(1)}, u32[]{:S(2)}, u32[]{:S(2)}) collective-permute-start(f32[4,8,512]{2,1,0:T(8,128)S(1)} %fusion), channel_id=1, source_target_pairs={{0,16},{8,24},{16,0},{24,8},{32,48},{40,56},{48,32},{56,40},{64,80... | collective-permute-start | bytes 196616 | tf_op jit(solution)/shard_map/ppermute | solution.py:400
  5.9 1.9 %collective-permute-start.3 = (f32[4,8,512]{2,1,0:T(8,128)S(1)}, f32[4,8,512]{2,1,0:T(8,128)S(1)}, u32[]{:S(2)}, u32[]{:S(2)}) collective-permute-start(f32[4,8,512]{2,1,0:T(8,128)S(1)} %fusion), channel_id=1, source_target_pairs={{0,32},{8,40},{16,48},{24,56},{32,0},{40,8},{48,16},{56,24},{64,96... | collective-permute-start | bytes 196616 | tf_op jit(solution)/shard_map/ppermute | solution.py:400
  7.9 0.6 %collective-permute-done.2 = f32[4,8,512]{2,1,0:T(8,128)S(1)} collective-permute-done((f32[4,8,512]{2,1,0:T(8,128)S(1)}, f32[4,8,512]{2,1,0:T(8,128)S(1)}, u32[]{:S(2)}, u32[]{:S(2)}) %collective-permute-start.2) | collective-permute-done | bytes 65568 | tf_op jit(solution)/shard_map/ppermute | solution.py:400
  8.5 1.7 %collective-permute-done.3 = f32[4,8,512]{2,1,0:T(8,128)S(1)} collective-permute-done((f32[4,8,512]{2,1,0:T(8,128)S(1)}, f32[4,8,512]{2,1,0:T(8,128)S(1)}, u32[]{:S(2)}, u32[]{:S(2)}) %collective-permute-start.3) | collective-permute-done | bytes 65568 | tf_op jit(solution)/shard_map/ppermute | solution.py:400
  10.2 2.8 %collective-permute-done.1 = f32[4,8,512]{2,1,0:T(8,128)S(1)} collective-permute-done((f32[4,8,512]{2,1,0:T(8,128)S(1)}, f32[4,8,512]{2,1,0:T(8,128)S(1)}, u32[]{:S(2)}, u32[]{:S(2)}) %collective-permute-start.1) | collective-permute-done | bytes 65568 | tf_op jit(solution)/shard_map/ppermute | solution.py:400
  13.1 2.6 %collective-permute-start.4 = (f32[4,8,512]{2,1,0:T(8,128)S(1)}, f32[4,8,512]{2,1,0:T(8,128)S(1)}, u32[]{:S(2)}, u32[]{:S(2)}) collective-permute-start(f32[4,8,512]{2,1,0:T(8,128)S(1)} %add_add_fusion.1.mine_ref), channel_id=1, source_target_pairs={{0,96},{8,104},{16,112},{24,120},{32,64},{40,72},{48,80},{56,88},{... | collective-permute-start | bytes 196616 | tf_op jit(solution)/shard_map/ppermute | solution.py:400
  15.7 1.1 %prepare.1 = (bf16[1024,256]{1,0:T(8,128)(2,1)S(1)}, bf16[1024,256]{1,0:T(8,128)(2,1)S(1)}, f32[4,48,512]{2,1,0:T(8,128)S(1)}, bf16[96,192]{1,0:T(8,128)(2,1)S(1)}, bf16[96,192]{1,0:T(8,128)(2,1)S(1)}) custom-call(f32[3,128]{1,0:T(4,128)S(1)} %copy-done.8, s32[2,512]{1,0:T(2,128)S(1)} %copy-done.7, f32[512]{0:T(512)S(1)} %copy-done.9, ...), custom_call_target="tpu_custom_call" | custom-call | flops 2097152 | bytes 2097152 | tf_op jit(solution)/shard_map/prepare/pallas_call | solution.py:205
  16.8 0.0 copy-start
  16.8 0.0 copy-start.2
  16.8 0.0 copy-start.5
  16.8 0.0 copy-start.6
  16.8 0.0 copy-start.11
  16.8 1.8 %collective-permute-done.4.other_ref = f32[4,8,512]{2,1,0:T(8,128)S(1)} collective-permute-done((f32[4,8,512]{2,1,0:T(8,128)S(1)}, f32[4,8,512]{2,1,0:T(8,128)S(1)}, u32[]{:S(2)}, u32[]{:S(2)}) %collective-permute-start.4) | collective-permute-done | bytes 65568 | tf_op jit(solution)/shard_map/ppermute | solution.py:400
  18.6 1.3 %project.1 = (f32[2,96,128]{2,1,0:T(8,128)S(1)}, f32[2,96,128]{2,1,0:T(8,128)S(1)}, f32[2,96,128]{2,1,0:T(8,128)S(1)}, f32[2,96,128]{2,1,0:T(8,128)S(1)}) custom-call(f32[4,8,512]{2,1,0:T(8,128)S(1)} %add_add_fusion.1.mine_ref, f32[4,8,512]{2,1,0:T(8,128)S(1)} %collective-permute-done.4.other_ref, f32[4,48,512]{2,1,0:T(8,128)S(1)} %get-tuple-element.17.qr_ref, ...), custom_call_target="tpu_custom_call" | custom-call | flops 603979776 | bytes 3145728 | tf_op jit(solution)/shard_map/project/pallas_call | solution.py:249
  19.9 1.6 %collective-permute-start.6 = (f32[2,96,128]{2,1,0:T(8,128)S(1)}, f32[2,96,128]{2,1,0:T(8,128)S(1)}, u32[]{:S(2)}, u32[]{:S(2)}) collective-permute-start(f32[2,96,128]{2,1,0:T(8,128)S(1)} %get-tuple-element.22), channel_id=1, source_target_pairs={{0,1},{1,0},{2,3},{3,2},{4,5},{5,4},{6,7},{7,6},{8,9},{9,8},{10,11... | collective-permute-start | bytes 294920 | tf_op jit(solution)/shard_map/ppermute | solution.py:400
  21.5 2.7 %collective-permute-start.7 = (f32[2,96,128]{2,1,0:T(8,128)S(1)}, f32[2,96,128]{2,1,0:T(8,128)S(1)}, u32[]{:S(2)}, u32[]{:S(2)}) collective-permute-start(f32[2,96,128]{2,1,0:T(8,128)S(1)} %get-tuple-element.23), channel_id=1, source_target_pairs={{0,2},{1,3},{2,0},{3,1},{4,6},{5,7},{6,4},{7,5},{8,10},{9,11},{10,... | collective-permute-start | bytes 294920 | tf_op jit(solution)/shard_map/ppermute | solution.py:400
  24.2 0.5 collective-permute-start.8
  24.7 0.0 collective-permute-start.5
  24.7 5.6 %collective-permute-done.5.far_ref = f32[1,96,128]{2,1,0:T(8,128)S(1)} collective-permute-done((f32[1,96,128]{2,1,0:T(8,128)S(1)}, f32[1,96,128]{2,1,0:T(8,128)S(1)}, u32[]{:S(2)}, u32[]{:S(2)}) %collective-permute-start.5) | collective-permute-done | bytes 49184 | tf_op jit(solution)/shard_map/ppermute | solution.py:441
  30.3 0.0 copy-start.10
  30.3 2.3 %translate.1 = f32[2,96,128]{2,1,0:T(8,128)S(1)} custom-call(s32[1]{0:T(128)} %bitcast.1.own_ref.pick_ref, s32[1]{0:T(128)} %bitcast.3.slot_ref, s32[1]{0:T(128)} %bitcast.4.base_ref, s32[1]{0:T(128)} %bitcast.5.odd_ref, f32[56,512]{1,0:T(8,128)S(1)} %collective-permute-done.near_ref, f32[1,96,128]{2,1,0:T(8,128)S(1)} %get-tuple-element.21.own_ref, ...), custom_call_target="tpu_custom_call" | custom-call | flops 184025088 | bytes 2097152 | tf_op jit(solution)/shard_map/translate/pallas_call | solution.py:318
  32.7 3.0 %collective-permute-start.9 = (f32[2,96,128]{2,1,0:T(8,128)S(1)}, f32[2,96,128]{2,1,0:T(8,128)S(1)}, u32[]{:S(2)}, u32[]{:S(2)}) collective-permute-start(f32[2,96,128]{2,1,0:T(8,128)S(1)} %add_add_fusion.mine_ref), channel_id=1, source_target_pairs={{0,4},{1,5},{2,6},{3,7},{4,0},{5,1},{6,2},{7,3},{8,12},{9,13},{10,... | collective-permute-start | bytes 294920 | tf_op jit(solution)/shard_map/ppermute | solution.py:400
  35.7 3.2 %collective-permute-done.9.other_ref = f32[2,96,128]{2,1,0:T(8,128)S(1)} collective-permute-done((f32[2,96,128]{2,1,0:T(8,128)S(1)}, f32[2,96,128]{2,1,0:T(8,128)S(1)}, u32[]{:S(2)}, u32[]{:S(2)}) %collective-permute-start.9) | collective-permute-done | bytes 98336 | tf_op jit(solution)/shard_map/ppermute | solution.py:400
  38.9 0.3 types.1.refs_0_
  39.2 2.8 %collective-permute-start.12 = (f32[2,96,128]{2,1,0:T(8,128)S(1)}, f32[2,96,128]{2,1,0:T(8,128)S(1)}, u32[]{:S(2)}, u32[]{:S(2)}) collective-permute-start(f32[2,96,128]{2,1,0:T(8,128)S(1)} %types.1.refs_0_), channel_id=1, source_target_pairs={{0,3},{1,2},{2,1},{3,0},{4,7},{5,6},{6,5},{7,4},{8,11},{9,10},{10,... | collective-permute-start | bytes 294920 | tf_op jit(solution)/shard_map/ppermute | solution.py:400
  42.0 1.3 %collective-permute-start.10 = (f32[2,96,128]{2,1,0:T(8,128)S(1)}, f32[2,96,128]{2,1,0:T(8,128)S(1)}, u32[]{:S(2)}, u32[]{:S(2)}) collective-permute-start(f32[2,96,128]{2,1,0:T(8,128)S(1)} %types.1.refs_0_), channel_id=1, source_target_pairs={{0,1},{1,0},{2,3},{3,2},{4,5},{5,4},{6,7},{7,6},{8,9},{9,8},{10,11... | collective-permute-start | bytes 294920 | tf_op jit(solution)/shard_map/ppermute | solution.py:400
  43.3 1.9 %collective-permute-done.12.refs_3_ = f32[2,96,128]{2,1,0:T(8,128)S(1)} collective-permute-done((f32[2,96,128]{2,1,0:T(8,128)S(1)}, f32[2,96,128]{2,1,0:T(8,128)S(1)}, u32[]{:S(2)}, u32[]{:S(2)}) %collective-permute-start.12) | collective-permute-done | bytes 98336 | tf_op jit(solution)/shard_map/ppermute | solution.py:400
  45.2 2.9 %collective-permute-done.11.refs_2_ = f32[2,96,128]{2,1,0:T(8,128)S(1)} collective-permute-done((f32[2,96,128]{2,1,0:T(8,128)S(1)}, f32[2,96,128]{2,1,0:T(8,128)S(1)}, u32[]{:S(2)}, u32[]{:S(2)}) %collective-permute-start.11) | collective-permute-done | bytes 98336 | tf_op jit(solution)/shard_map/ppermute | solution.py:400
  48.1 0.8 %place.1 = f32[8,96,128]{2,1,0:T(8,128)} custom-call(s32[1]{0:T(128)} %bitcast.flip_ref, f32[2,96,128]{2,1,0:T(8,128)S(1)} %types.1.refs_0_, f32[2,96,128]{2,1,0:T(8,128)S(1)} %collective-permute-done.10.refs_1_, f32[2,96,128]{2,1,0:T(8,128)S(1)} %collective-permute-done.11.refs_2_, f32[2,96,128]{2,1,0:T(8,128)S(1)} %collective-permute-done.12.refs_3_), custom_call_target="tpu_custom_call" | custom-call | bytes 1048576 | tf_op jit(solution)/shard_map/place/pallas_call | solution.py:387
  (27 shorter events, 0.1 us)
Async XLA Ops:
  0.0 15.7 %copy-start.1 = (f32[2,48,2,512]{3,2,1,0:T(2,128)S(1)}, f32[2,48,2,512]{3,2,1,0:T(2,128)}, u32[]{:S(2)}) copy-start(f32[2,48,2,512]{3,2,1,0:T(2,128)} %proj_ref.1) | copy-start | bytes 1179652
  0.0 15.7 %copy-start.3 = (f32[2,4,48,48]{3,2,1,0:T(8,128)S(1)}, f32[2,4,48,48]{3,2,1,0:T(8,128)}, u32[]{:S(2)}) copy-start(f32[2,4,48,48]{3,2,1,0:T(8,128)} %tmat_ref.1) | copy-start | bytes 221188
  0.0 15.7 %copy-start.4 = (f32[2,2,2,512]{3,2,1,0:T(2,128)S(1)}, f32[2,2,2,512]{3,2,1,0:T(2,128)}, u32[]{:S(2)}) copy-start(f32[2,2,2,512]{3,2,1,0:T(2,128)} %refl_ref.1) | copy-start | bytes 49156
  0.0 15.7 %copy-start.7 = (s32[2,512]{1,0:T(2,128)S(1)}, s32[2,512]{1,0:T(2,128)}, u32[]{:S(2)}) copy-start(s32[2,512]{1,0:T(2,128)} %grid_ref.1) | copy-start | bytes 12292
  0.0 15.7 %copy-start.8 = (f32[3,128]{1,0:T(4,128)S(1)}, f32[3,128]{1,0:T(4,128)}, u32[]{:S(2)}) copy-start(f32[3,128]{1,0:T(4,128)} %pos_ref.1) | copy-start | bytes 4612
  0.0 15.7 %copy-start.9 = (f32[512]{0:T(512)S(1)}, f32[512]{0:T(512)}, u32[]{:S(2)}) copy-start(f32[512]{0:T(512)} %vert_ref.1) | copy-start | bytes 6148
  2.7 1.4 %collective-permute-start = (f32[56,512]{1,0:T(8,128)S(1)}, f32[56,512]{1,0:T(8,128)S(1)}, u32[]{:S(2)}, u32[]{:S(2)}) collective-permute-start(f32[56,512]{1,0:T(8,128)S(1)} %get-tuple-element.16), channel_id=1, source_target_pairs={{0,8},{8,0},{16,24},{24,16},{32,40},{40,32},{48,56},{56,48},{64,72... | collective-permute-start | bytes 344072 | tf_op jit(solution)/shard_map/ppermute | solution.py:400
  4.2 4.3 %collective-permute-start.2 = (f32[4,8,512]{2,1,0:T(8,128)S(1)}, f32[4,8,512]{2,1,0:T(8,128)S(1)}, u32[]{:S(2)}, u32[]{:S(2)}) collective-permute-start(f32[4,8,512]{2,1,0:T(8,128)S(1)} %fusion), channel_id=1, source_target_pairs={{0,16},{8,24},{16,0},{24,8},{32,48},{40,56},{48,32},{56,40},{64,80... | collective-permute-start | bytes 196616 | tf_op jit(solution)/shard_map/ppermute | solution.py:400
  5.9 4.3 %collective-permute-start.3 = (f32[4,8,512]{2,1,0:T(8,128)S(1)}, f32[4,8,512]{2,1,0:T(8,128)S(1)}, u32[]{:S(2)}, u32[]{:S(2)}) collective-permute-start(f32[4,8,512]{2,1,0:T(8,128)S(1)} %fusion), channel_id=1, source_target_pairs={{0,32},{8,40},{16,48},{24,56},{32,0},{40,8},{48,16},{56,24},{64,96... | collective-permute-start | bytes 196616 | tf_op jit(solution)/shard_map/ppermute | solution.py:400
  7.9 5.2 %collective-permute-start.1 = (f32[4,8,512]{2,1,0:T(8,128)S(1)}, f32[4,8,512]{2,1,0:T(8,128)S(1)}, u32[]{:S(2)}, u32[]{:S(2)}) collective-permute-start(f32[4,8,512]{2,1,0:T(8,128)S(1)} %fusion), channel_id=1, source_target_pairs={{0,48},{8,56},{16,32},{24,40},{32,16},{40,24},{48,0},{56,8},{64,11... | collective-permute-start | bytes 196616 | tf_op jit(solution)/shard_map/ppermute | solution.py:400
  13.1 5.6 %collective-permute-start.4 = (f32[4,8,512]{2,1,0:T(8,128)S(1)}, f32[4,8,512]{2,1,0:T(8,128)S(1)}, u32[]{:S(2)}, u32[]{:S(2)}) collective-permute-start(f32[4,8,512]{2,1,0:T(8,128)S(1)} %add_add_fusion.1.mine_ref), channel_id=1, source_target_pairs={{0,96},{8,104},{16,112},{24,120},{32,64},{40,72},{48,80},{56,88},{... | collective-permute-start | bytes 196616 | tf_op jit(solution)/shard_map/ppermute | solution.py:400
  16.8 13.5 %copy-start = (f32[2,26,48,48]{3,2,1,0:T(8,128)S(1)}, f32[2,26,48,48]{3,2,1,0:T(8,128)}, u32[]{:S(2)}) copy-start(f32[2,26,48,48]{3,2,1,0:T(8,128)} %trans_ref.1) | copy-start | bytes 1437700
  16.8 13.5 %copy-start.2 = (f32[8,96,128]{2,1,0:T(8,128)S(1)}, f32[8,96,128]{2,1,0:T(8,128)}, u32[]{:S(2)}) copy-start(f32[8,96,128]{2,1,0:T(8,128)} %inc_ref.1) | copy-start | bytes 1179652
  16.8 13.5 %copy-start.5 = (s32[12,128]{1,0:T(8,128)S(1)}, s32[12,128]{1,0:T(8,128)}, u32[]{:S(2)}) copy-start(s32[12,128]{1,0:T(8,128)} %idx_ref.1) | copy-start | bytes 18436
  16.8 13.5 %copy-start.6 = (s32[12,128]{1,0:T(8,128)S(1)}, s32[12,128]{1,0:T(8,128)}, u32[]{:S(2)}) copy-start(s32[12,128]{1,0:T(8,128)} %class_ref.1) | copy-start | bytes 18436
  16.8 13.5 %copy-start.11 = (s32[128]{0:T(128)S(1)}, s32[128]{0:T(128)}, u32[]{:S(2)}) copy-start(s32[128]{0:T(128)} %count_ref.1) | copy-start | bytes 1540
  19.9 12.8 %collective-permute-start.6 = (f32[2,96,128]{2,1,0:T(8,128)S(1)}, f32[2,96,128]{2,1,0:T(8,128)S(1)}, u32[]{:S(2)}, u32[]{:S(2)}) collective-permute-start(f32[2,96,128]{2,1,0:T(8,128)S(1)} %get-tuple-element.22), channel_id=1, source_target_pairs={{0,1},{1,0},{2,3},{3,2},{4,5},{5,4},{6,7},{7,6},{8,9},{9,8},{10,11... | collective-permute-start | bytes 294920 | tf_op jit(solution)/shard_map/ppermute | solution.py:400
  21.5 11.2 %collective-permute-start.7 = (f32[2,96,128]{2,1,0:T(8,128)S(1)}, f32[2,96,128]{2,1,0:T(8,128)S(1)}, u32[]{:S(2)}, u32[]{:S(2)}) collective-permute-start(f32[2,96,128]{2,1,0:T(8,128)S(1)} %get-tuple-element.23), channel_id=1, source_target_pairs={{0,2},{1,3},{2,0},{3,1},{4,6},{5,7},{6,4},{7,5},{8,10},{9,11},{10,... | collective-permute-start | bytes 294920 | tf_op jit(solution)/shard_map/ppermute | solution.py:400
  24.2 8.5 %collective-permute-start.8 = (f32[2,96,128]{2,1,0:T(8,128)S(1)}, f32[2,96,128]{2,1,0:T(8,128)S(1)}, u32[]{:S(2)}, u32[]{:S(2)}) collective-permute-start(f32[2,96,128]{2,1,0:T(8,128)S(1)} %get-tuple-element.24), channel_id=1, source_target_pairs={{0,3},{1,2},{2,1},{3,0},{4,7},{5,6},{6,5},{7,4},{8,11},{9,10},{10,... | collective-permute-start | bytes 294920 | tf_op jit(solution)/shard_map/ppermute | solution.py:400
  24.7 5.6 %collective-permute-start.5 = (f32[1,96,128]{2,1,0:T(8,128)S(1)}, f32[1,96,128]{2,1,0:T(8,128)S(1)}, u32[]{:S(2)}, u32[]{:S(2)}) collective-permute-start(f32[1,96,128]{2,1,0:T(8,128)S(1)} %get-tuple-element.21.own_ref), channel_id=1, source_target_pairs={{8,16},{24,32},{40,48},{56,64},{72,80},{88,96},{104,112},{120,0},{... | collective-permute-start | bytes 147464 | tf_op jit(solution)/shard_map/ppermute | solution.py:441
  30.3 8.6 %copy-start.10 = (s32[128]{0:T(128)S(1)}, s32[128]{0:T(128)}, u32[]{:S(2)}) copy-start(s32[128]{0:T(128)} %type_ref.1) | copy-start | bytes 1540
  32.7 6.2 %collective-permute-start.9 = (f32[2,96,128]{2,1,0:T(8,128)S(1)}, f32[2,96,128]{2,1,0:T(8,128)S(1)}, u32[]{:S(2)}, u32[]{:S(2)}) collective-permute-start(f32[2,96,128]{2,1,0:T(8,128)S(1)} %add_add_fusion.mine_ref), channel_id=1, source_target_pairs={{0,4},{1,5},{2,6},{3,7},{4,0},{5,1},{6,2},{7,3},{8,12},{9,13},{10,... | collective-permute-start | bytes 294920 | tf_op jit(solution)/shard_map/ppermute | solution.py:400
  39.2 6.1 %collective-permute-start.12 = (f32[2,96,128]{2,1,0:T(8,128)S(1)}, f32[2,96,128]{2,1,0:T(8,128)S(1)}, u32[]{:S(2)}, u32[]{:S(2)}) collective-permute-start(f32[2,96,128]{2,1,0:T(8,128)S(1)} %types.1.refs_0_), channel_id=1, source_target_pairs={{0,3},{1,2},{2,1},{3,0},{4,7},{5,6},{6,5},{7,4},{8,11},{9,10},{10,... | collective-permute-start | bytes 294920 | tf_op jit(solution)/shard_map/ppermute | solution.py:400
  42.0 6.1 %collective-permute-start.11 = (f32[2,96,128]{2,1,0:T(8,128)S(1)}, f32[2,96,128]{2,1,0:T(8,128)S(1)}, u32[]{:S(2)}, u32[]{:S(2)}) collective-permute-start(f32[2,96,128]{2,1,0:T(8,128)S(1)} %types.1.refs_0_), channel_id=1, source_target_pairs={{0,2},{1,3},{2,0},{3,1},{4,6},{5,7},{6,4},{7,5},{8,10},{9,11},{10,... | collective-permute-start | bytes 294920 | tf_op jit(solution)/shard_map/ppermute | solution.py:400
  42.0 6.1 %collective-permute-start.10 = (f32[2,96,128]{2,1,0:T(8,128)S(1)}, f32[2,96,128]{2,1,0:T(8,128)S(1)}, u32[]{:S(2)}, u32[]{:S(2)}) collective-permute-start(f32[2,96,128]{2,1,0:T(8,128)S(1)} %types.1.refs_0_), channel_id=1, source_target_pairs={{0,1},{1,0},{2,3},{3,2},{4,5},{5,4},{6,7},{7,6},{8,9},{9,8},{10,11... | collective-permute-start | bytes 294920 | tf_op jit(solution)/shard_map/ppermute | solution.py:400

commit v4 on v3

--- a/solution.py
+++ b/solution.py
@@ -400,6 +400,11 @@
     return lax.ppermute(x, axis, [(i, i ^ mask) for i in range(lax.axis_size(axis))])
 
 
+def peers(x, axis, masks):
+    pairs = [(i, i ^ masks[i & 1]) for i in range(lax.axis_size(axis))]
+    return lax.ppermute(x, axis, pairs)
+
+
 def per_device(
     coefficients,
     incident,
@@ -430,12 +435,16 @@
     near = swap(wide, "sph", 1)
     rows = 4 * coefficients.shape[0]
     part = (wide[:rows] + near[:rows]).reshape(4, -1, wide.shape[1])
-    r6, r4, r2 = (swap(part, "sph", mask) for mask in (6, 4, 2))
+    even = jnp.bitwise_and(sph, 1) == 0
+    r6, r4, r2, r1 = (
+        peers(part, "sph", masks)
+        for masks in ((10, 14), (12, 8), (4, 6), (4, 2))
+    )
     uh, ul, qr, th, tl = prepare(
         positions, wave_grid, vertical, reflection, projector, t_matrix
     )
-    part = (part + r6) + (r2 + r4)
-    other = swap(part, "sph", 12)
+    part = (jnp.where(even, part, r1) + r6) + (r2 + r4)
+    other = swap(part, "sph", 1)
     size = lax.axis_size("sph")
     links = [(i, (i + 1) % size) for i in range(1, size, 2)]
     far = lax.ppermute(mine, "sph", links + [(j, i) for i, j in links])

time: 49 us -> 48.1 us (0.982)
  waiting for transfers between devices: 21.9 us -> 19.4 us
  starting transfers between devices: 18.3 us -> 19.9 us
    ppermute x12 -> x9, waiting for transfers between devices: 16.3 us -> 9.39 us  [swap(): lax.ppermute(x, axis, [(i, i ^ mask) for i in range(lax.axis_size(axis))])]
    ppermute x0 -> x4, starting transfers between devices: none -> 6.72 us  [peers(): return lax.ppermute(x, axis, pairs)]
    ppermute x12 -> x9, starting transfers between devices: 18.3 us -> 12.1 us  [swap(): lax.ppermute(x, axis, [(i, i ^ mask) for i in range(lax.axis_size(axis))])]
    ppermute x0 -> x4, waiting for transfers between devices: none -> 5.47 us  [peers(): return lax.ppermute(x, axis, pairs)]
    ppermute x1, starting transfers between devices: 0.01 us -> 1.09 us  [per_device(): far = lax.ppermute(mine, 'sph', links + [(j, i) for i, j in links])]
    ppermute x1, waiting for transfers between devices: 5.62 us -> 4.53 us  [per_device(): far = lax.ppermute(mine, 'sph', links + [(j, i) for i, j in links])]
  transfers between devices with their start and end apart: 13 -> 14, of which waited for: 9 -> 8; matrix products, arithmetic and copies ran while one was open for 0% -> 0% of each run, Pallas kernels for 7% -> 7%
where the time goes in v4:
time: 48.1 us; the launch traced here: 48 us
  starting transfers between devices  19.9 us (41%)
  waiting for transfers between devices  19.4 us (40%)
  Pallas kernels  8.32 us (17%)
    ppermute x9, starting transfers between devices, swap(): lax.ppermute(x, axis, [(i, i ^ mask) for i in range(lax.axis_size(axis))])  12.1 us
    ppermute x9, waiting for transfers between devices, swap(): lax.ppermute(x, axis, [(i, i ^ mask) for i in range(lax.axis_size(axis))])  9.39 us
    ppermute x4, starting transfers between devices, peers(): return lax.ppermute(x, axis, pairs)  6.72 us
    ppermute x4, waiting for transfers between devices, peers(): return lax.ppermute(x, axis, pairs)  5.47 us
    ppermute x1, waiting for transfers between devices, per_device(): far = lax.ppermute(mine, 'sph', links + [(j, i) for i, j in links])  4.53 us
    pallas_call x1, Pallas kernels, expand(): pl.pallas_call(expand_kernel, name='expand', out_shape=(jax.ShapeDtypeStr...  2.71 us
    pallas_call x1, Pallas kernels, translate(): pl.pallas_call(translate_kernel, name='translate', out_shape=jax.ShapeDty...  2.3 us
    pallas_call x1, Pallas kernels, project(): pl.pallas_call(project_kernel, name='project', out_shape=(piece,) * piece...  1.24 us
  transfers between devices with their start and end apart: 14, of which 8 were waited for; matrix products, arithmetic and copies ran while one was open for 0% of the time, Pallas kernels for 7%

profile of v4, /device:TPU:0, one launch (start us, length us, event | category | flops | bytes accessed | tf_op | source)
XLA Modules:
  0.0 48.0 jit_solution(7631545718251031622)
XLA Ops:
  0.0 2.7 %expand.1 = (f32[56,512]{1,0:T(8,128)S(1)}, f32[1,96,128]{2,1,0:T(8,128)S(1)}) custom-call(s32[1]{0:T(128)} %bitcast.flip_ref, s32[1]{0:T(128)} %bitcast.1.own_ref.pick_ref, f32[8,96,128]{2,1,0:T(8,128)} %coef_hbm.1, f32[3,128]{1,0:T(4,128)} %pos_ref.1, s32[2,512]{1,0:T(2,128)} %grid_ref.1, f32[512]{0:T(512)} %vert_ref.1, f32[2,2,48,512]{3,2,1,0:T(8,128)} %exp_hbm.1), custom_call_target="tpu_custom_call" | custom-call | flops 603979776 | bytes 4194304 | tf_op jit(solution)/shard_map/expand/pallas_call | solution.py:143
  2.7 0.1 collective-permute-start
  2.8 1.3 %collective-permute-done.near_ref = f32[56,512]{1,0:T(8,128)S(1)} collective-permute-done((f32[56,512]{1,0:T(8,128)S(1)}, f32[56,512]{1,0:T(8,128)S(1)}, u32[]{:S(2)}, u32[]{:S(2)}) %collective-permute-start) | collective-permute-done | bytes 114720 | tf_op jit(solution)/shard_map/ppermute | solution.py:400
  4.2 2.1 %collective-permute-start.3 = (f32[4,8,512]{2,1,0:T(8,128)S(1)}, f32[4,8,512]{2,1,0:T(8,128)S(1)}, u32[]{:S(2)}, u32[]{:S(2)}) collective-permute-start(f32[4,8,512]{2,1,0:T(8,128)S(1)} %fusion), channel_id=1, source_target_pairs={{0,32},{8,56},{16,48},{24,40},{32,0},{40,24},{48,16},{56,8},{64,96... | collective-permute-start | bytes 196616 | tf_op jit(solution)/shard_map/ppermute | solution.py:405
  6.3 4.6 %collective-permute-start.2 = (f32[4,8,512]{2,1,0:T(8,128)S(1)}, f32[4,8,512]{2,1,0:T(8,128)S(1)}, u32[]{:S(2)}, u32[]{:S(2)}) collective-permute-start(f32[4,8,512]{2,1,0:T(8,128)S(1)} %fusion), channel_id=1, source_target_pairs={{0,80},{8,120},{16,64},{24,104},{32,112},{40,88},{48,96},{56,72},{... | collective-permute-start | bytes 196616 | tf_op jit(solution)/shard_map/ppermute | solution.py:405
  10.9 0.0 collective-permute-start.4
  10.9 2.7 %collective-permute-done.2 = f32[4,8,512]{2,1,0:T(8,128)S(1)} collective-permute-done((f32[4,8,512]{2,1,0:T(8,128)S(1)}, f32[4,8,512]{2,1,0:T(8,128)S(1)}, u32[]{:S(2)}, u32[]{:S(2)}) %collective-permute-start.2) | collective-permute-done | bytes 65568 | tf_op jit(solution)/shard_map/ppermute | solution.py:405
  13.6 2.8 %collective-permute-done.4 = f32[4,8,512]{2,1,0:T(8,128)S(1)} collective-permute-done((f32[4,8,512]{2,1,0:T(8,128)S(1)}, f32[4,8,512]{2,1,0:T(8,128)S(1)}, u32[]{:S(2)}, u32[]{:S(2)}) %collective-permute-start.4) | collective-permute-done | bytes 65568 | tf_op jit(solution)/shard_map/ppermute | solution.py:405
  16.4 0.1 collective-permute-start.5
  16.5 1.0 %prepare.1 = (bf16[1024,256]{1,0:T(8,128)(2,1)S(1)}, bf16[1024,256]{1,0:T(8,128)(2,1)S(1)}, f32[4,48,512]{2,1,0:T(8,128)S(1)}, bf16[96,192]{1,0:T(8,128)(2,1)S(1)}, bf16[96,192]{1,0:T(8,128)(2,1)S(1)}) custom-call(f32[3,128]{1,0:T(4,128)S(1)} %copy-done.8, s32[2,512]{1,0:T(2,128)S(1)} %copy-done.7, f32[512]{0:T(512)S(1)} %copy-done.9, ...), custom_call_target="tpu_custom_call" | custom-call | flops 2097152 | bytes 2097152 | tf_op jit(solution)/shard_map/prepare/pallas_call | solution.py:205
  17.6 0.0 copy-start
  17.6 0.0 copy-start.2
  17.6 0.0 copy-start.5
  17.6 0.0 copy-start.6
  17.6 0.0 copy-start.11
  17.7 0.1 collective-permute-done.5.other_ref
  17.7 1.2 %project.1 = (f32[2,96,128]{2,1,0:T(8,128)S(1)}, f32[2,96,128]{2,1,0:T(8,128)S(1)}, f32[2,96,128]{2,1,0:T(8,128)S(1)}, f32[2,96,128]{2,1,0:T(8,128)S(1)}) custom-call(f32[4,8,512]{2,1,0:T(8,128)S(1)} %add_add_fusion.1.mine_ref, f32[4,8,512]{2,1,0:T(8,128)S(1)} %collective-permute-done.5.other_ref, f32[4,48,512]{2,1,0:T(8,128)S(1)} %get-tuple-element.17.qr_ref, ...), custom_call_target="tpu_custom_call" | custom-call | flops 603979776 | bytes 3145728 | tf_op jit(solution)/shard_map/project/pallas_call | solution.py:249
  19.0 1.6 %collective-permute-start.7 = (f32[2,96,128]{2,1,0:T(8,128)S(1)}, f32[2,96,128]{2,1,0:T(8,128)S(1)}, u32[]{:S(2)}, u32[]{:S(2)}) collective-permute-start(f32[2,96,128]{2,1,0:T(8,128)S(1)} %get-tuple-element.22), channel_id=1, source_target_pairs={{0,1},{1,0},{2,3},{3,2},{4,5},{5,4},{6,7},{7,6},{8,9},{9,8},{10,11... | collective-permute-start | bytes 294920 | tf_op jit(solution)/shard_map/ppermute | solution.py:400
  20.5 2.7 %collective-permute-start.8 = (f32[2,96,128]{2,1,0:T(8,128)S(1)}, f32[2,96,128]{2,1,0:T(8,128)S(1)}, u32[]{:S(2)}, u32[]{:S(2)}) collective-permute-start(f32[2,96,128]{2,1,0:T(8,128)S(1)} %get-tuple-element.23), channel_id=1, source_target_pairs={{0,2},{1,3},{2,0},{3,1},{4,6},{5,7},{6,4},{7,5},{8,10},{9,11},{10,... | collective-permute-start | bytes 294920 | tf_op jit(solution)/shard_map/ppermute | solution.py:400
  23.3 0.5 collective-permute-start.9
  23.8 1.1 %collective-permute-start.6 = (f32[1,96,128]{2,1,0:T(8,128)S(1)}, f32[1,96,128]{2,1,0:T(8,128)S(1)}, u32[]{:S(2)}, u32[]{:S(2)}) collective-permute-start(f32[1,96,128]{2,1,0:T(8,128)S(1)} %get-tuple-element.21.own_ref), channel_id=1, source_target_pairs={{8,16},{24,32},{40,48},{56,64},{72,80},{88,96},{104,112},{120,0},{... | collective-permute-start | bytes 147464 | tf_op jit(solution)/shard_map/ppermute | solution.py:450
  24.8 4.5 %collective-permute-done.6.far_ref = f32[1,96,128]{2,1,0:T(8,128)S(1)} collective-permute-done((f32[1,96,128]{2,1,0:T(8,128)S(1)}, f32[1,96,128]{2,1,0:T(8,128)S(1)}, u32[]{:S(2)}, u32[]{:S(2)}) %collective-permute-start.6) | collective-permute-done | bytes 49184 | tf_op jit(solution)/shard_map/ppermute | solution.py:450
  29.4 0.0 copy-start.10
  29.4 2.3 %translate.1 = f32[2,96,128]{2,1,0:T(8,128)S(1)} custom-call(s32[1]{0:T(128)} %bitcast.1.own_ref.pick_ref, s32[1]{0:T(128)} %bitcast.3.slot_ref, s32[1]{0:T(128)} %bitcast.4.base_ref, s32[1]{0:T(128)} %bitcast.5.odd_ref, f32[56,512]{1,0:T(8,128)S(1)} %collective-permute-done.near_ref, f32[1,96,128]{2,1,0:T(8,128)S(1)} %get-tuple-element.21.own_ref, ...), custom_call_target="tpu_custom_call" | custom-call | flops 184025088 | bytes 2097152 | tf_op jit(solution)/shard_map/translate/pallas_call | solution.py:318
  31.8 3.0 %collective-permute-start.10 = (f32[2,96,128]{2,1,0:T(8,128)S(1)}, f32[2,96,128]{2,1,0:T(8,128)S(1)}, u32[]{:S(2)}, u32[]{:S(2)}) collective-permute-start(f32[2,96,128]{2,1,0:T(8,128)S(1)} %add_add_fusion.mine_ref), channel_id=1, source_target_pairs={{0,4},{1,5},{2,6},{3,7},{4,0},{5,1},{6,2},{7,3},{8,12},{9,13},{10,... | collective-permute-start | bytes 294920 | tf_op jit(solution)/shard_map/ppermute | solution.py:400
  34.8 3.2 %collective-permute-done.10.other_ref = f32[2,96,128]{2,1,0:T(8,128)S(1)} collective-permute-done((f32[2,96,128]{2,1,0:T(8,128)S(1)}, f32[2,96,128]{2,1,0:T(8,128)S(1)}, u32[]{:S(2)}, u32[]{:S(2)}) %collective-permute-start.10) | collective-permute-done | bytes 98336 | tf_op jit(solution)/shard_map/ppermute | solution.py:400
  38.0 0.3 types.1.refs_0_
  38.3 2.8 %collective-permute-start.13 = (f32[2,96,128]{2,1,0:T(8,128)S(1)}, f32[2,96,128]{2,1,0:T(8,128)S(1)}, u32[]{:S(2)}, u32[]{:S(2)}) collective-permute-start(f32[2,96,128]{2,1,0:T(8,128)S(1)} %types.1.refs_0_), channel_id=1, source_target_pairs={{0,3},{1,2},{2,1},{3,0},{4,7},{5,6},{6,5},{7,4},{8,11},{9,10},{10,... | collective-permute-start | bytes 294920 | tf_op jit(solution)/shard_map/ppermute | solution.py:400
  41.1 1.3 %collective-permute-start.11 = (f32[2,96,128]{2,1,0:T(8,128)S(1)}, f32[2,96,128]{2,1,0:T(8,128)S(1)}, u32[]{:S(2)}, u32[]{:S(2)}) collective-permute-start(f32[2,96,128]{2,1,0:T(8,128)S(1)} %types.1.refs_0_), channel_id=1, source_target_pairs={{0,1},{1,0},{2,3},{3,2},{4,5},{5,4},{6,7},{7,6},{8,9},{9,8},{10,11... | collective-permute-start | bytes 294920 | tf_op jit(solution)/shard_map/ppermute | solution.py:400
  42.4 1.9 %collective-permute-done.13.refs_3_ = f32[2,96,128]{2,1,0:T(8,128)S(1)} collective-permute-done((f32[2,96,128]{2,1,0:T(8,128)S(1)}, f32[2,96,128]{2,1,0:T(8,128)S(1)}, u32[]{:S(2)}, u32[]{:S(2)}) %collective-permute-start.13) | collective-permute-done | bytes 98336 | tf_op jit(solution)/shard_map/ppermute | solution.py:400
  44.3 2.9 %collective-permute-done.12.refs_2_ = f32[2,96,128]{2,1,0:T(8,128)S(1)} collective-permute-done((f32[2,96,128]{2,1,0:T(8,128)S(1)}, f32[2,96,128]{2,1,0:T(8,128)S(1)}, u32[]{:S(2)}, u32[]{:S(2)}) %collective-permute-start.12) | collective-permute-done | bytes 98336 | tf_op jit(solution)/shard_map/ppermute | solution.py:400
  47.2 0.8 %place.1 = f32[8,96,128]{2,1,0:T(8,128)} custom-call(s32[1]{0:T(128)} %bitcast.flip_ref, f32[2,96,128]{2,1,0:T(8,128)S(1)} %types.1.refs_0_, f32[2,96,128]{2,1,0:T(8,128)S(1)} %collective-permute-done.11.refs_1_, f32[2,96,128]{2,1,0:T(8,128)S(1)} %collective-permute-done.12.refs_2_, f32[2,96,128]{2,1,0:T(8,128)S(1)} %collective-permute-done.13.refs_3_), custom_call_target="tpu_custom_call" | custom-call | bytes 1048576 | tf_op jit(solution)/shard_map/place/pallas_call | solution.py:387
  (29 shorter events, 0.1 us)
Async XLA Ops:
  0.0 16.5 %copy-start.1 = (f32[2,48,2,512]{3,2,1,0:T(2,128)S(1)}, f32[2,48,2,512]{3,2,1,0:T(2,128)}, u32[]{:S(2)}) copy-start(f32[2,48,2,512]{3,2,1,0:T(2,128)} %proj_ref.1) | copy-start | bytes 1179652
  0.0 16.5 %copy-start.3 = (f32[2,4,48,48]{3,2,1,0:T(8,128)S(1)}, f32[2,4,48,48]{3,2,1,0:T(8,128)}, u32[]{:S(2)}) copy-start(f32[2,4,48,48]{3,2,1,0:T(8,128)} %tmat_ref.1) | copy-start | bytes 221188
  0.0 16.5 %copy-start.4 = (f32[2,2,2,512]{3,2,1,0:T(2,128)S(1)}, f32[2,2,2,512]{3,2,1,0:T(2,128)}, u32[]{:S(2)}) copy-start(f32[2,2,2,512]{3,2,1,0:T(2,128)} %refl_ref.1) | copy-start | bytes 49156
  0.0 16.5 %copy-start.7 = (s32[2,512]{1,0:T(2,128)S(1)}, s32[2,512]{1,0:T(2,128)}, u32[]{:S(2)}) copy-start(s32[2,512]{1,0:T(2,128)} %grid_ref.1) | copy-start | bytes 12292
  0.0 16.5 %copy-start.8 = (f32[3,128]{1,0:T(4,128)S(1)}, f32[3,128]{1,0:T(4,128)}, u32[]{:S(2)}) copy-start(f32[3,128]{1,0:T(4,128)} %pos_ref.1) | copy-start | bytes 4612
  0.0 16.5 %copy-start.9 = (f32[512]{0:T(512)S(1)}, f32[512]{0:T(512)}, u32[]{:S(2)}) copy-start(f32[512]{0:T(512)} %vert_ref.1) | copy-start | bytes 6148
  2.7 1.4 %collective-permute-start = (f32[56,512]{1,0:T(8,128)S(1)}, f32[56,512]{1,0:T(8,128)S(1)}, u32[]{:S(2)}, u32[]{:S(2)}) collective-permute-start(f32[56,512]{1,0:T(8,128)S(1)} %get-tuple-element.16), channel_id=1, source_target_pairs={{0,8},{8,0},{16,24},{24,16},{32,40},{40,32},{48,56},{56,48},{64,72... | collective-permute-start | bytes 344072 | tf_op jit(solution)/shard_map/ppermute | solution.py:400
  4.2 6.7 %collective-permute-start.3 = (f32[4,8,512]{2,1,0:T(8,128)S(1)}, f32[4,8,512]{2,1,0:T(8,128)S(1)}, u32[]{:S(2)}, u32[]{:S(2)}) collective-permute-start(f32[4,8,512]{2,1,0:T(8,128)S(1)} %fusion), channel_id=1, source_target_pairs={{0,32},{8,56},{16,48},{24,40},{32,0},{40,24},{48,16},{56,8},{64,96... | collective-permute-start | bytes 196616 | tf_op jit(solution)/shard_map/ppermute | solution.py:405
  6.3 7.3 %collective-permute-start.2 = (f32[4,8,512]{2,1,0:T(8,128)S(1)}, f32[4,8,512]{2,1,0:T(8,128)S(1)}, u32[]{:S(2)}, u32[]{:S(2)}) collective-permute-start(f32[4,8,512]{2,1,0:T(8,128)S(1)} %fusion), channel_id=1, source_target_pairs={{0,80},{8,120},{16,64},{24,104},{32,112},{40,88},{48,96},{56,72},{... | collective-permute-start | bytes 196616 | tf_op jit(solution)/shard_map/ppermute | solution.py:405
  10.9 5.5 %collective-permute-start.4 = (f32[4,8,512]{2,1,0:T(8,128)S(1)}, f32[4,8,512]{2,1,0:T(8,128)S(1)}, u32[]{:S(2)}, u32[]{:S(2)}) collective-permute-start(f32[4,8,512]{2,1,0:T(8,128)S(1)} %fusion), channel_id=1, source_target_pairs={{0,96},{8,72},{16,112},{24,88},{32,64},{40,104},{48,80},{56,120},{... | collective-permute-start | bytes 196616 | tf_op jit(solution)/shard_map/ppermute | solution.py:405
  10.9 5.5 %collective-permute-start.1 = (f32[4,8,512]{2,1,0:T(8,128)S(1)}, f32[4,8,512]{2,1,0:T(8,128)S(1)}, u32[]{:S(2)}, u32[]{:S(2)}) collective-permute-start(f32[4,8,512]{2,1,0:T(8,128)S(1)} %fusion), channel_id=1, source_target_pairs={{0,32},{8,24},{16,48},{24,8},{32,0},{40,56},{48,16},{56,40},{64,96... | collective-permute-start | bytes 196616 | tf_op jit(solution)/shard_map/ppermute | solution.py:405
  16.4 1.3 %collective-permute-start.5 = (f32[4,8,512]{2,1,0:T(8,128)S(1)}, f32[4,8,512]{2,1,0:T(8,128)S(1)}, u32[]{:S(2)}, u32[]{:S(2)}) collective-permute-start(f32[4,8,512]{2,1,0:T(8,128)S(1)} %add_add_fusion.1.mine_ref), channel_id=1, source_target_pairs={{0,8},{8,0},{16,24},{24,16},{32,40},{40,32},{48,56},{56,48},{64,72... | collective-permute-start | bytes 196616 | tf_op jit(solution)/shard_map/ppermute | solution.py:400
  17.6 11.8 %copy-start = (f32[2,26,48,48]{3,2,1,0:T(8,128)S(1)}, f32[2,26,48,48]{3,2,1,0:T(8,128)}, u32[]{:S(2)}) copy-start(f32[2,26,48,48]{3,2,1,0:T(8,128)} %trans_ref.1) | copy-start | bytes 1437700
  17.6 11.8 %copy-start.2 = (f32[8,96,128]{2,1,0:T(8,128)S(1)}, f32[8,96,128]{2,1,0:T(8,128)}, u32[]{:S(2)}) copy-start(f32[8,96,128]{2,1,0:T(8,128)} %inc_ref.1) | copy-start | bytes 1179652
  17.6 11.8 %copy-start.5 = (s32[12,128]{1,0:T(8,128)S(1)}, s32[12,128]{1,0:T(8,128)}, u32[]{:S(2)}) copy-start(s32[12,128]{1,0:T(8,128)} %idx_ref.1) | copy-start | bytes 18436
  17.6 11.8 %copy-start.6 = (s32[12,128]{1,0:T(8,128)S(1)}, s32[12,128]{1,0:T(8,128)}, u32[]{:S(2)}) copy-start(s32[12,128]{1,0:T(8,128)} %class_ref.1) | copy-start | bytes 18436
  17.6 11.8 %copy-start.11 = (s32[128]{0:T(128)S(1)}, s32[128]{0:T(128)}, u32[]{:S(2)}) copy-start(s32[128]{0:T(128)} %count_ref.1) | copy-start | bytes 1540
  19.0 12.8 %collective-permute-start.7 = (f32[2,96,128]{2,1,0:T(8,128)S(1)}, f32[2,96,128]{2,1,0:T(8,128)S(1)}, u32[]{:S(2)}, u32[]{:S(2)}) collective-permute-start(f32[2,96,128]{2,1,0:T(8,128)S(1)} %get-tuple-element.22), channel_id=1, source_target_pairs={{0,1},{1,0},{2,3},{3,2},{4,5},{5,4},{6,7},{7,6},{8,9},{9,8},{10,11... | collective-permute-start | bytes 294920 | tf_op jit(solution)/shard_map/ppermute | solution.py:400
  20.5 11.2 %collective-permute-start.8 = (f32[2,96,128]{2,1,0:T(8,128)S(1)}, f32[2,96,128]{2,1,0:T(8,128)S(1)}, u32[]{:S(2)}, u32[]{:S(2)}) collective-permute-start(f32[2,96,128]{2,1,0:T(8,128)S(1)} %get-tuple-element.23), channel_id=1, source_target_pairs={{0,2},{1,3},{2,0},{3,1},{4,6},{5,7},{6,4},{7,5},{8,10},{9,11},{10,... | collective-permute-start | bytes 294920 | tf_op jit(solution)/shard_map/ppermute | solution.py:400
  23.3 8.5 %collective-permute-start.9 = (f32[2,96,128]{2,1,0:T(8,128)S(1)}, f32[2,96,128]{2,1,0:T(8,128)S(1)}, u32[]{:S(2)}, u32[]{:S(2)}) collective-permute-start(f32[2,96,128]{2,1,0:T(8,128)S(1)} %get-tuple-element.24), channel_id=1, source_target_pairs={{0,3},{1,2},{2,1},{3,0},{4,7},{5,6},{6,5},{7,4},{8,11},{9,10},{10,... | collective-permute-start | bytes 294920 | tf_op jit(solution)/shard_map/ppermute | solution.py:400
  23.8 5.6 %collective-permute-start.6 = (f32[1,96,128]{2,1,0:T(8,128)S(1)}, f32[1,96,128]{2,1,0:T(8,128)S(1)}, u32[]{:S(2)}, u32[]{:S(2)}) collective-permute-start(f32[1,96,128]{2,1,0:T(8,128)S(1)} %get-tuple-element.21.own_ref), channel_id=1, source_target_pairs={{8,16},{24,32},{40,48},{56,64},{72,80},{88,96},{104,112},{120,0},{... | collective-permute-start | bytes 147464 | tf_op jit(solution)/shard_map/ppermute | solution.py:450
  29.4 8.6 %copy-start.10 = (s32[128]{0:T(128)S(1)}, s32[128]{0:T(128)}, u32[]{:S(2)}) copy-start(s32[128]{0:T(128)} %type_ref.1) | copy-start | bytes 1540
  31.8 6.2 %collective-permute-start.10 = (f32[2,96,128]{2,1,0:T(8,128)S(1)}, f32[2,96,128]{2,1,0:T(8,128)S(1)}, u32[]{:S(2)}, u32[]{:S(2)}) collective-permute-start(f32[2,96,128]{2,1,0:T(8,128)S(1)} %add_add_fusion.mine_ref), channel_id=1, source_target_pairs={{0,4},{1,5},{2,6},{3,7},{4,0},{5,1},{6,2},{7,3},{8,12},{9,13},{10,... | collective-permute-start | bytes 294920 | tf_op jit(solution)/shard_map/ppermute | solution.py:400
  38.3 6.1 %collective-permute-start.13 = (f32[2,96,128]{2,1,0:T(8,128)S(1)}, f32[2,96,128]{2,1,0:T(8,128)S(1)}, u32[]{:S(2)}, u32[]{:S(2)}) collective-permute-start(f32[2,96,128]{2,1,0:T(8,128)S(1)} %types.1.refs_0_), channel_id=1, source_target_pairs={{0,3},{1,2},{2,1},{3,0},{4,7},{5,6},{6,5},{7,4},{8,11},{9,10},{10,... | collective-permute-start | bytes 294920 | tf_op jit(solution)/shard_map/ppermute | solution.py:400
  41.1 6.1 %collective-permute-start.12 = (f32[2,96,128]{2,1,0:T(8,128)S(1)}, f32[2,96,128]{2,1,0:T(8,128)S(1)}, u32[]{:S(2)}, u32[]{:S(2)}) collective-permute-start(f32[2,96,128]{2,1,0:T(8,128)S(1)} %types.1.refs_0_), channel_id=1, source_target_pairs={{0,2},{1,3},{2,0},{3,1},{4,6},{5,7},{6,4},{7,5},{8,10},{9,11},{10,... | collective-permute-start | bytes 294920 | tf_op jit(solution)/shard_map/ppermute | solution.py:400
  41.1 6.1 %collective-permute-start.11 = (f32[2,96,128]{2,1,0:T(8,128)S(1)}, f32[2,96,128]{2,1,0:T(8,128)S(1)}, u32[]{:S(2)}, u32[]{:S(2)}) collective-permute-start(f32[2,96,128]{2,1,0:T(8,128)S(1)} %types.1.refs_0_), channel_id=1, source_target_pairs={{0,1},{1,0},{2,3},{3,2},{4,5},{5,4},{6,7},{7,6},{8,9},{9,8},{10,11... | collective-permute-start | bytes 294920 | tf_op jit(solution)/shard_map/ppermute | solution.py:400

commit v5 on v4

--- a/solution.py
+++ b/solution.py
@@ -47,7 +47,7 @@
     def dot(a, b):
         return jnp.dot(a, b, preferred_element_type=F32)
 
-    return dot(ah, bh) + (dot(ah, bl) + dot(al, bh))
+    return dot(jnp.concatenate([ah, ah, al], axis=1), jnp.concatenate([bh, bl, bh], axis=0))
 
 
 def columns(rows):
@@ -118,7 +118,7 @@
                 al[rows, offset : offset + 128] = lo
     for copy in copies[3 + illums :]:
         copy.wait()
-    width = 256
+    width = 512
     for start in range(0, waves, width):
         lanes = slice(start, start + width)
         spec[...] = dot3(ah[...], al[...], bh[:, lanes], bl[:, lanes])
@@ -153,7 +153,7 @@
         + [
             pltpu.VMEM((rows, 2 * spheres), BF16),
             pltpu.VMEM((rows, 2 * spheres), BF16),
-            pltpu.VMEM((rows, 256), F32),
+            pltpu.VMEM((rows, 512), F32),
             pltpu.SemaphoreType.DMA((7 + illums,)),
         ],
         compiler_params=PARAMS,

time: 48.1 us -> 48.2 us (level)
  no operation moved by 1% of the time
where the time goes in v5:
time: 48.2 us; the launch traced here: 48.1 us
  starting transfers between devices  19.9 us (41%)
  waiting for transfers between devices  19.4 us (40%)
  Pallas kernels  8.38 us (17%)
    ppermute x9, starting transfers between devices, swap(): lax.ppermute(x, axis, [(i, i ^ mask) for i in range(lax.axis_size(axis))])  12.1 us
    ppermute x9, waiting for transfers between devices, swap(): lax.ppermute(x, axis, [(i, i ^ mask) for i in range(lax.axis_size(axis))])  9.4 us
    ppermute x4, starting transfers between devices, peers(): return lax.ppermute(x, axis, pairs)  6.72 us
    ppermute x4, waiting for transfers between devices, peers(): return lax.ppermute(x, axis, pairs)  5.47 us
    ppermute x1, waiting for transfers between devices, per_device(): far = lax.ppermute(mine, 'sph', links + [(j, i) for i, j in links])  4.54 us
    pallas_call x1, Pallas kernels, expand(): pl.pallas_call(expand_kernel, name='expand', out_shape=(jax.ShapeDtypeStr...  2.71 us
    pallas_call x1, Pallas kernels, translate(): pl.pallas_call(translate_kernel, name='translate', out_shape=jax.ShapeDty...  2.36 us
    pallas_call x1, Pallas kernels, project(): pl.pallas_call(project_kernel, name='project', out_shape=(piece,) * piece...  1.21 us
  transfers between devices with their start and end apart: 14, of which 8 were waited for; matrix products, arithmetic and copies ran while one was open for 0% of the time, Pallas kernels for 7%

profile of v5, /device:TPU:0, one launch (start us, length us, event | category | flops | bytes accessed | tf_op | source)
XLA Modules:
  0.0 48.1 jit_solution(9920778856878634669)
XLA Ops:
  0.0 2.7 %expand.1 = (f32[56,512]{1,0:T(8,128)S(1)}, f32[1,96,128]{2,1,0:T(8,128)S(1)}) custom-call(s32[1]{0:T(128)} %bitcast.flip_ref, s32[1]{0:T(128)} %bitcast.1.own_ref.pick_ref, f32[8,96,128]{2,1,0:T(8,128)} %coef_hbm.1, f32[3,128]{1,0:T(4,128)} %pos_ref.1, s32[2,512]{1,0:T(2,128)} %grid_ref.1, f32[512]{0:T(512)} %vert_ref.1, f32[2,2,48,512]{3,2,1,0:T(8,128)} %exp_hbm.1), custom_call_target="tpu_custom_call" | custom-call | flops 603979776 | bytes 4194304 | tf_op jit(solution)/shard_map/expand/pallas_call | solution.py:143
  2.7 0.1 collective-permute-start
  2.8 1.3 %collective-permute-done.near_ref = f32[56,512]{1,0:T(8,128)S(1)} collective-permute-done((f32[56,512]{1,0:T(8,128)S(1)}, f32[56,512]{1,0:T(8,128)S(1)}, u32[]{:S(2)}, u32[]{:S(2)}) %collective-permute-start) | collective-permute-done | bytes 114720 | tf_op jit(solution)/shard_map/ppermute | solution.py:400
  4.2 2.1 %collective-permute-start.3 = (f32[4,8,512]{2,1,0:T(8,128)S(1)}, f32[4,8,512]{2,1,0:T(8,128)S(1)}, u32[]{:S(2)}, u32[]{:S(2)}) collective-permute-start(f32[4,8,512]{2,1,0:T(8,128)S(1)} %fusion), channel_id=1, source_target_pairs={{0,32},{8,56},{16,48},{24,40},{32,0},{40,24},{48,16},{56,8},{64,96... | collective-permute-start | bytes 196616 | tf_op jit(solution)/shard_map/ppermute | solution.py:405
  6.3 4.6 %collective-permute-start.2 = (f32[4,8,512]{2,1,0:T(8,128)S(1)}, f32[4,8,512]{2,1,0:T(8,128)S(1)}, u32[]{:S(2)}, u32[]{:S(2)}) collective-permute-start(f32[4,8,512]{2,1,0:T(8,128)S(1)} %fusion), channel_id=1, source_target_pairs={{0,80},{8,120},{16,64},{24,104},{32,112},{40,88},{48,96},{56,72},{... | collective-permute-start | bytes 196616 | tf_op jit(solution)/shard_map/ppermute | solution.py:405
  10.9 2.7 %collective-permute-done.2 = f32[4,8,512]{2,1,0:T(8,128)S(1)} collective-permute-done((f32[4,8,512]{2,1,0:T(8,128)S(1)}, f32[4,8,512]{2,1,0:T(8,128)S(1)}, u32[]{:S(2)}, u32[]{:S(2)}) %collective-permute-start.2) | collective-permute-done | bytes 65568 | tf_op jit(solution)/shard_map/ppermute | solution.py:405
  13.6 2.8 %collective-permute-done.4 = f32[4,8,512]{2,1,0:T(8,128)S(1)} collective-permute-done((f32[4,8,512]{2,1,0:T(8,128)S(1)}, f32[4,8,512]{2,1,0:T(8,128)S(1)}, u32[]{:S(2)}, u32[]{:S(2)}) %collective-permute-start.4) | collective-permute-done | bytes 65568 | tf_op jit(solution)/shard_map/ppermute | solution.py:405
  16.4 0.1 collective-permute-start.5
  16.5 1.0 %prepare.1 = (bf16[1024,256]{1,0:T(8,128)(2,1)S(1)}, bf16[1024,256]{1,0:T(8,128)(2,1)S(1)}, f32[4,48,512]{2,1,0:T(8,128)S(1)}, bf16[96,192]{1,0:T(8,128)(2,1)S(1)}, bf16[96,192]{1,0:T(8,128)(2,1)S(1)}) custom-call(f32[3,128]{1,0:T(4,128)S(1)} %copy-done.8, s32[2,512]{1,0:T(2,128)S(1)} %copy-done.7, f32[512]{0:T(512)S(1)} %copy-done.9, ...), custom_call_target="tpu_custom_call" | custom-call | flops 2097152 | bytes 2097152 | tf_op jit(solution)/shard_map/prepare/pallas_call | solution.py:205
  17.6 0.0 copy-start
  17.6 0.0 copy-start.2
  17.6 0.0 copy-start.5
  17.6 0.0 copy-start.6
  17.6 0.0 copy-start.11
  17.7 0.1 collective-permute-done.5.other_ref
  17.7 1.2 %project.1 = (f32[2,96,128]{2,1,0:T(8,128)S(1)}, f32[2,96,128]{2,1,0:T(8,128)S(1)}, f32[2,96,128]{2,1,0:T(8,128)S(1)}, f32[2,96,128]{2,1,0:T(8,128)S(1)}) custom-call(f32[4,8,512]{2,1,0:T(8,128)S(1)} %add_add_fusion.1.mine_ref, f32[4,8,512]{2,1,0:T(8,128)S(1)} %collective-permute-done.5.other_ref, f32[4,48,512]{2,1,0:T(8,128)S(1)} %get-tuple-element.17.qr_ref, ...), custom_call_target="tpu_custom_call" | custom-call | flops 603979776 | bytes 3145728 | tf_op jit(solution)/shard_map/project/pallas_call | solution.py:249
  18.9 1.6 %collective-permute-start.7 = (f32[2,96,128]{2,1,0:T(8,128)S(1)}, f32[2,96,128]{2,1,0:T(8,128)S(1)}, u32[]{:S(2)}, u32[]{:S(2)}) collective-permute-start(f32[2,96,128]{2,1,0:T(8,128)S(1)} %get-tuple-element.22), channel_id=1, source_target_pairs={{0,1},{1,0},{2,3},{3,2},{4,5},{5,4},{6,7},{7,6},{8,9},{9,8},{10,11... | collective-permute-start | bytes 294920 | tf_op jit(solution)/shard_map/ppermute | solution.py:400
  20.5 2.7 %collective-permute-start.8 = (f32[2,96,128]{2,1,0:T(8,128)S(1)}, f32[2,96,128]{2,1,0:T(8,128)S(1)}, u32[]{:S(2)}, u32[]{:S(2)}) collective-permute-start(f32[2,96,128]{2,1,0:T(8,128)S(1)} %get-tuple-element.23), channel_id=1, source_target_pairs={{0,2},{1,3},{2,0},{3,1},{4,6},{5,7},{6,4},{7,5},{8,10},{9,11},{10,... | collective-permute-start | bytes 294920 | tf_op jit(solution)/shard_map/ppermute | solution.py:400
  23.2 0.5 collective-permute-start.9
  23.7 1.1 %collective-permute-start.6 = (f32[1,96,128]{2,1,0:T(8,128)S(1)}, f32[1,96,128]{2,1,0:T(8,128)S(1)}, u32[]{:S(2)}, u32[]{:S(2)}) collective-permute-start(f32[1,96,128]{2,1,0:T(8,128)S(1)} %get-tuple-element.21.own_ref), channel_id=1, source_target_pairs={{8,16},{24,32},{40,48},{56,64},{72,80},{88,96},{104,112},{120,0},{... | collective-permute-start | bytes 147464 | tf_op jit(solution)/shard_map/ppermute | solution.py:450
  24.8 4.5 %collective-permute-done.6.far_ref = f32[1,96,128]{2,1,0:T(8,128)S(1)} collective-permute-done((f32[1,96,128]{2,1,0:T(8,128)S(1)}, f32[1,96,128]{2,1,0:T(8,128)S(1)}, u32[]{:S(2)}, u32[]{:S(2)}) %collective-permute-start.6) | collective-permute-done | bytes 49184 | tf_op jit(solution)/shard_map/ppermute | solution.py:450
  29.4 0.0 copy-start.10
  29.4 2.4 %translate.1 = f32[2,96,128]{2,1,0:T(8,128)S(1)} custom-call(s32[1]{0:T(128)} %bitcast.1.own_ref.pick_ref, s32[1]{0:T(128)} %bitcast.3.slot_ref, s32[1]{0:T(128)} %bitcast.4.base_ref, s32[1]{0:T(128)} %bitcast.5.odd_ref, f32[56,512]{1,0:T(8,128)S(1)} %collective-permute-done.near_ref, f32[1,96,128]{2,1,0:T(8,128)S(1)} %get-tuple-element.21.own_ref, ...), custom_call_target="tpu_custom_call" | custom-call | flops 184025088 | bytes 2097152 | tf_op jit(solution)/shard_map/translate/pallas_call | solution.py:318
  31.8 0.0 collective-permute-done.8
  31.8 3.0 %collective-permute-start.10 = (f32[2,96,128]{2,1,0:T(8,128)S(1)}, f32[2,96,128]{2,1,0:T(8,128)S(1)}, u32[]{:S(2)}, u32[]{:S(2)}) collective-permute-start(f32[2,96,128]{2,1,0:T(8,128)S(1)} %add_add_fusion.mine_ref), channel_id=1, source_target_pairs={{0,4},{1,5},{2,6},{3,7},{4,0},{5,1},{6,2},{7,3},{8,12},{9,13},{10,... | collective-permute-start | bytes 294920 | tf_op jit(solution)/shard_map/ppermute | solution.py:400
  34.8 3.2 %collective-permute-done.10.other_ref = f32[2,96,128]{2,1,0:T(8,128)S(1)} collective-permute-done((f32[2,96,128]{2,1,0:T(8,128)S(1)}, f32[2,96,128]{2,1,0:T(8,128)S(1)}, u32[]{:S(2)}, u32[]{:S(2)}) %collective-permute-start.10) | collective-permute-done | bytes 98336 | tf_op jit(solution)/shard_map/ppermute | solution.py:400
  38.0 0.3 types.1.refs_0_
  38.3 2.8 %collective-permute-start.13 = (f32[2,96,128]{2,1,0:T(8,128)S(1)}, f32[2,96,128]{2,1,0:T(8,128)S(1)}, u32[]{:S(2)}, u32[]{:S(2)}) collective-permute-start(f32[2,96,128]{2,1,0:T(8,128)S(1)} %types.1.refs_0_), channel_id=1, source_target_pairs={{0,3},{1,2},{2,1},{3,0},{4,7},{5,6},{6,5},{7,4},{8,11},{9,10},{10,... | collective-permute-start | bytes 294920 | tf_op jit(solution)/shard_map/ppermute | solution.py:400
  41.2 1.3 %collective-permute-start.11 = (f32[2,96,128]{2,1,0:T(8,128)S(1)}, f32[2,96,128]{2,1,0:T(8,128)S(1)}, u32[]{:S(2)}, u32[]{:S(2)}) collective-permute-start(f32[2,96,128]{2,1,0:T(8,128)S(1)} %types.1.refs_0_), channel_id=1, source_target_pairs={{0,1},{1,0},{2,3},{3,2},{4,5},{5,4},{6,7},{7,6},{8,9},{9,8},{10,11... | collective-permute-start | bytes 294920 | tf_op jit(solution)/shard_map/ppermute | solution.py:400
  42.5 1.9 %collective-permute-done.13.refs_3_ = f32[2,96,128]{2,1,0:T(8,128)S(1)} collective-permute-done((f32[2,96,128]{2,1,0:T(8,128)S(1)}, f32[2,96,128]{2,1,0:T(8,128)S(1)}, u32[]{:S(2)}, u32[]{:S(2)}) %collective-permute-start.13) | collective-permute-done | bytes 98336 | tf_op jit(solution)/shard_map/ppermute | solution.py:400
  44.4 2.9 %collective-permute-done.12.refs_2_ = f32[2,96,128]{2,1,0:T(8,128)S(1)} collective-permute-done((f32[2,96,128]{2,1,0:T(8,128)S(1)}, f32[2,96,128]{2,1,0:T(8,128)S(1)}, u32[]{:S(2)}, u32[]{:S(2)}) %collective-permute-start.12) | collective-permute-done | bytes 98336 | tf_op jit(solution)/shard_map/ppermute | solution.py:400
  47.3 0.8 %place.1 = f32[8,96,128]{2,1,0:T(8,128)} custom-call(s32[1]{0:T(128)} %bitcast.flip_ref, f32[2,96,128]{2,1,0:T(8,128)S(1)} %types.1.refs_0_, f32[2,96,128]{2,1,0:T(8,128)S(1)} %collective-permute-done.11.refs_1_, f32[2,96,128]{2,1,0:T(8,128)S(1)} %collective-permute-done.12.refs_2_, f32[2,96,128]{2,1,0:T(8,128)S(1)} %collective-permute-done.13.refs_3_), custom_call_target="tpu_custom_call" | custom-call | bytes 1048576 | tf_op jit(solution)/shard_map/place/pallas_call | solution.py:387
  (29 shorter events, 0.1 us)
Async XLA Ops:
  0.0 16.5 %copy-start.1 = (f32[2,48,2,512]{3,2,1,0:T(2,128)S(1)}, f32[2,48,2,512]{3,2,1,0:T(2,128)}, u32[]{:S(2)}) copy-start(f32[2,48,2,512]{3,2,1,0:T(2,128)} %proj_ref.1) | copy-start | bytes 1179652
  0.0 16.5 %copy-start.3 = (f32[2,4,48,48]{3,2,1,0:T(8,128)S(1)}, f32[2,4,48,48]{3,2,1,0:T(8,128)}, u32[]{:S(2)}) copy-start(f32[2,4,48,48]{3,2,1,0:T(8,128)} %tmat_ref.1) | copy-start | bytes 221188
  0.0 16.5 %copy-start.4 = (f32[2,2,2,512]{3,2,1,0:T(2,128)S(1)}, f32[2,2,2,512]{3,2,1,0:T(2,128)}, u32[]{:S(2)}) copy-start(f32[2,2,2,512]{3,2,1,0:T(2,128)} %refl_ref.1) | copy-start | bytes 49156
  0.0 16.5 %copy-start.7 = (s32[2,512]{1,0:T(2,128)S(1)}, s32[2,512]{1,0:T(2,128)}, u32[]{:S(2)}) copy-start(s32[2,512]{1,0:T(2,128)} %grid_ref.1) | copy-start | bytes 12292
  0.0 16.5 %copy-start.8 = (f32[3,128]{1,0:T(4,128)S(1)}, f32[3,128]{1,0:T(4,128)}, u32[]{:S(2)}) copy-start(f32[3,128]{1,0:T(4,128)} %pos_ref.1) | copy-start | bytes 4612
  0.0 16.5 %copy-start.9 = (f32[512]{0:T(512)S(1)}, f32[512]{0:T(512)}, u32[]{:S(2)}) copy-start(f32[512]{0:T(512)} %vert_ref.1) | copy-start | bytes 6148
  2.7 1.4 %collective-permute-start = (f32[56,512]{1,0:T(8,128)S(1)}, f32[56,512]{1,0:T(8,128)S(1)}, u32[]{:S(2)}, u32[]{:S(2)}) collective-permute-start(f32[56,512]{1,0:T(8,128)S(1)} %get-tuple-element.16), channel_id=1, source_target_pairs={{0,8},{8,0},{16,24},{24,16},{32,40},{40,32},{48,56},{56,48},{64,72... | collective-permute-start | bytes 344072 | tf_op jit(solution)/shard_map/ppermute | solution.py:400
  4.2 6.7 %collective-permute-start.3 = (f32[4,8,512]{2,1,0:T(8,128)S(1)}, f32[4,8,512]{2,1,0:T(8,128)S(1)}, u32[]{:S(2)}, u32[]{:S(2)}) collective-permute-start(f32[4,8,512]{2,1,0:T(8,128)S(1)} %fusion), channel_id=1, source_target_pairs={{0,32},{8,56},{16,48},{24,40},{32,0},{40,24},{48,16},{56,8},{64,96... | collective-permute-start | bytes 196616 | tf_op jit(solution)/shard_map/ppermute | solution.py:405
  6.3 7.3 %collective-permute-start.2 = (f32[4,8,512]{2,1,0:T(8,128)S(1)}, f32[4,8,512]{2,1,0:T(8,128)S(1)}, u32[]{:S(2)}, u32[]{:S(2)}) collective-permute-start(f32[4,8,512]{2,1,0:T(8,128)S(1)} %fusion), channel_id=1, source_target_pairs={{0,80},{8,120},{16,64},{24,104},{32,112},{40,88},{48,96},{56,72},{... | collective-permute-start | bytes 196616 | tf_op jit(solution)/shard_map/ppermute | solution.py:405
  10.9 5.5 %collective-permute-start.4 = (f32[4,8,512]{2,1,0:T(8,128)S(1)}, f32[4,8,512]{2,1,0:T(8,128)S(1)}, u32[]{:S(2)}, u32[]{:S(2)}) collective-permute-start(f32[4,8,512]{2,1,0:T(8,128)S(1)} %fusion), channel_id=1, source_target_pairs={{0,96},{8,72},{16,112},{24,88},{32,64},{40,104},{48,80},{56,120},{... | collective-permute-start | bytes 196616 | tf_op jit(solution)/shard_map/ppermute | solution.py:405
  10.9 5.5 %collective-permute-start.1 = (f32[4,8,512]{2,1,0:T(8,128)S(1)}, f32[4,8,512]{2,1,0:T(8,128)S(1)}, u32[]{:S(2)}, u32[]{:S(2)}) collective-permute-start(f32[4,8,512]{2,1,0:T(8,128)S(1)} %fusion), channel_id=1, source_target_pairs={{0,32},{8,24},{16,48},{24,8},{32,0},{40,56},{48,16},{56,40},{64,96... | collective-permute-start | bytes 196616 | tf_op jit(solution)/shard_map/ppermute | solution.py:405
  16.4 1.3 %collective-permute-start.5 = (f32[4,8,512]{2,1,0:T(8,128)S(1)}, f32[4,8,512]{2,1,0:T(8,128)S(1)}, u32[]{:S(2)}, u32[]{:S(2)}) collective-permute-start(f32[4,8,512]{2,1,0:T(8,128)S(1)} %add_add_fusion.1.mine_ref), channel_id=1, source_target_pairs={{0,8},{8,0},{16,24},{24,16},{32,40},{40,32},{48,56},{56,48},{64,72... | collective-permute-start | bytes 196616 | tf_op jit(solution)/shard_map/ppermute | solution.py:400
  17.6 11.8 %copy-start = (f32[2,26,48,48]{3,2,1,0:T(8,128)S(1)}, f32[2,26,48,48]{3,2,1,0:T(8,128)}, u32[]{:S(2)}) copy-start(f32[2,26,48,48]{3,2,1,0:T(8,128)} %trans_ref.1) | copy-start | bytes 1437700
  17.6 11.7 %copy-start.2 = (f32[8,96,128]{2,1,0:T(8,128)S(1)}, f32[8,96,128]{2,1,0:T(8,128)}, u32[]{:S(2)}) copy-start(f32[8,96,128]{2,1,0:T(8,128)} %inc_ref.1) | copy-start | bytes 1179652
  17.6 11.7 %copy-start.5 = (s32[12,128]{1,0:T(8,128)S(1)}, s32[12,128]{1,0:T(8,128)}, u32[]{:S(2)}) copy-start(s32[12,128]{1,0:T(8,128)} %idx_ref.1) | copy-start | bytes 18436
  17.6 11.7 %copy-start.6 = (s32[12,128]{1,0:T(8,128)S(1)}, s32[12,128]{1,0:T(8,128)}, u32[]{:S(2)}) copy-start(s32[12,128]{1,0:T(8,128)} %class_ref.1) | copy-start | bytes 18436
  17.6 11.7 %copy-start.11 = (s32[128]{0:T(128)S(1)}, s32[128]{0:T(128)}, u32[]{:S(2)}) copy-start(s32[128]{0:T(128)} %count_ref.1) | copy-start | bytes 1540
  18.9 12.8 %collective-permute-start.7 = (f32[2,96,128]{2,1,0:T(8,128)S(1)}, f32[2,96,128]{2,1,0:T(8,128)S(1)}, u32[]{:S(2)}, u32[]{:S(2)}) collective-permute-start(f32[2,96,128]{2,1,0:T(8,128)S(1)} %get-tuple-element.22), channel_id=1, source_target_pairs={{0,1},{1,0},{2,3},{3,2},{4,5},{5,4},{6,7},{7,6},{8,9},{9,8},{10,11... | collective-permute-start | bytes 294920 | tf_op jit(solution)/shard_map/ppermute | solution.py:400
  20.5 11.3 %collective-permute-start.8 = (f32[2,96,128]{2,1,0:T(8,128)S(1)}, f32[2,96,128]{2,1,0:T(8,128)S(1)}, u32[]{:S(2)}, u32[]{:S(2)}) collective-permute-start(f32[2,96,128]{2,1,0:T(8,128)S(1)} %get-tuple-element.23), channel_id=1, source_target_pairs={{0,2},{1,3},{2,0},{3,1},{4,6},{5,7},{6,4},{7,5},{8,10},{9,11},{10,... | collective-permute-start | bytes 294920 | tf_op jit(solution)/shard_map/ppermute | solution.py:400
  23.2 8.5 %collective-permute-start.9 = (f32[2,96,128]{2,1,0:T(8,128)S(1)}, f32[2,96,128]{2,1,0:T(8,128)S(1)}, u32[]{:S(2)}, u32[]{:S(2)}) collective-permute-start(f32[2,96,128]{2,1,0:T(8,128)S(1)} %get-tuple-element.24), channel_id=1, source_target_pairs={{0,3},{1,2},{2,1},{3,0},{4,7},{5,6},{6,5},{7,4},{8,11},{9,10},{10,... | collective-permute-start | bytes 294920 | tf_op jit(solution)/shard_map/ppermute | solution.py:400
  23.7 5.6 %collective-permute-start.6 = (f32[1,96,128]{2,1,0:T(8,128)S(1)}, f32[1,96,128]{2,1,0:T(8,128)S(1)}, u32[]{:S(2)}, u32[]{:S(2)}) collective-permute-start(f32[1,96,128]{2,1,0:T(8,128)S(1)} %get-tuple-element.21.own_ref), channel_id=1, source_target_pairs={{8,16},{24,32},{40,48},{56,64},{72,80},{88,96},{104,112},{120,0},{... | collective-permute-start | bytes 147464 | tf_op jit(solution)/shard_map/ppermute | solution.py:450
  29.4 8.7 %copy-start.10 = (s32[128]{0:T(128)S(1)}, s32[128]{0:T(128)}, u32[]{:S(2)}) copy-start(s32[128]{0:T(128)} %type_ref.1) | copy-start | bytes 1540
  31.8 6.2 %collective-permute-start.10 = (f32[2,96,128]{2,1,0:T(8,128)S(1)}, f32[2,96,128]{2,1,0:T(8,128)S(1)}, u32[]{:S(2)}, u32[]{:S(2)}) collective-permute-start(f32[2,96,128]{2,1,0:T(8,128)S(1)} %add_add_fusion.mine_ref), channel_id=1, source_target_pairs={{0,4},{1,5},{2,6},{3,7},{4,0},{5,1},{6,2},{7,3},{8,12},{9,13},{10,... | collective-permute-start | bytes 294920 | tf_op jit(solution)/shard_map/ppermute | solution.py:400
  38.3 6.1 %collective-permute-start.13 = (f32[2,96,128]{2,1,0:T(8,128)S(1)}, f32[2,96,128]{2,1,0:T(8,128)S(1)}, u32[]{:S(2)}, u32[]{:S(2)}) collective-permute-start(f32[2,96,128]{2,1,0:T(8,128)S(1)} %types.1.refs_0_), channel_id=1, source_target_pairs={{0,3},{1,2},{2,1},{3,0},{4,7},{5,6},{6,5},{7,4},{8,11},{9,10},{10,... | collective-permute-start | bytes 294920 | tf_op jit(solution)/shard_map/ppermute | solution.py:400
  41.2 6.1 %collective-permute-start.12 = (f32[2,96,128]{2,1,0:T(8,128)S(1)}, f32[2,96,128]{2,1,0:T(8,128)S(1)}, u32[]{:S(2)}, u32[]{:S(2)}) collective-permute-start(f32[2,96,128]{2,1,0:T(8,128)S(1)} %types.1.refs_0_), channel_id=1, source_target_pairs={{0,2},{1,3},{2,0},{3,1},{4,6},{5,7},{6,4},{7,5},{8,10},{9,11},{10,... | collective-permute-start | bytes 294920 | tf_op jit(solution)/shard_map/ppermute | solution.py:400
  41.2 6.1 %collective-permute-start.11 = (f32[2,96,128]{2,1,0:T(8,128)S(1)}, f32[2,96,128]{2,1,0:T(8,128)S(1)}, u32[]{:S(2)}, u32[]{:S(2)}) collective-permute-start(f32[2,96,128]{2,1,0:T(8,128)S(1)} %types.1.refs_0_), channel_id=1, source_target_pairs={{0,1},{1,0},{2,3},{3,2},{4,5},{5,4},{6,7},{7,6},{8,9},{9,8},{10,11... | collective-permute-start | bytes 294920 | tf_op jit(solution)/shard_map/ppermute | solution.py:400
